TPU v7x, 512 devices: a whole 4x4x16 slice. The times are simulated.
512 devices in a mesh: pipe: 8 (over x, core), dp: 64 (over y, z).
Axes of the slice: x: 4, y: 4, z: 16, core: 2. Of those that a mesh axis runs over, the one named last changes fastest.
Arguments:
- saved_inputs: bfloat16 [8, 8192, 8192], P('pipe', 'dp'), may hold values from -1000 to 1000
- cotangent: bfloat16 [8192, 8192], P('dp', 'pipe'), may hold values from -500 to 500
- weights_bf16: bfloat16 [8, 2, 64, 8192], P('pipe', None, None, 'dp'), may hold values from -6 to 6
- master: float32 [8, 2, 64, 8192], P('pipe', None, None, 'dp'), may hold values from -6 to 6
- moment1: float32 [8, 2, 64, 8192], P('pipe', None, None, 'dp'), may hold values from -6 to 6
- moment2: float32 [8, 2, 64, 8192], P('pipe', None, None, 'dp'), may hold values from 0.5 to 8
- valid_rows: int32 [64], P('dp'), may hold values from 1 to 128, 6144 in all
Outputs:
- new_master: float32 [8, 2, 64, 8192], P('pipe', None, None, 'dp')
- new_moment1: float32 [8, 2, 64, 8192], P('pipe', None, None, 'dp')
- new_moment2: float32 [8, 2, 64, 8192], P('pipe', None, None, 'dp')
- new_weights: bfloat16 [8, 2, 64, 8192], P('pipe', None, None, 'dp')
Inputs may be any that keep to these rules, and one draw needn't show every extreme that they name: `valid_rows`: the counts sum to 6144.
All inputs are finite; a program needn't handle non-finite values. No bound on the sum of `valid_rows` on one device may be relied on, other than what follows from the above.
Results may differ from a plain program's by a relative error of at most 0.02.
Values may be sent and summed in bfloat16 or wider, within the bound.
No kernel may reach another device: no remote copies, remote signals or barrier semaphores. Data moves between devices by JAX's collectives and lax.ppermute only.
A program may use at most 64 MiB of HBM per device.

v0:
```python
import math

import jax
import jax.numpy as jnp
from jax import lax
from jax.sharding import PartitionSpec as P

BETA_ONE = 0.9
BETA_TWO = 0.95
LEARN_RATE = 0.05
DECAY_RATE = 0.1
ADAM_EPS = 1e-08
CLIP_RMS = 2.0
NORM_EPS = 1e-12


def shifted(x, axis, by):
    length = lax.axis_size(axis)
    pairs = [(i, i + by) for i in range(length) if 0 <= i + by < length]
    return lax.ppermute(x, axis, pairs)


def section_backward(inputs_block, incoming, weights):
    down_proj = weights[0]
    up_proj = weights[1]
    model_width = inputs_block.shape[1]
    adapter_rank = weights.shape[1]
    pre_act = lax.dot_general(
        inputs_block, down_proj, (((1,), (1,)), ((), ())), preferred_element_type=jnp.float32
    ) * (1.0 / math.sqrt(model_width))
    activated = jax.nn.silu(pre_act).astype(jnp.bfloat16)
    logistic = jax.nn.sigmoid(pre_act)
    derivative = logistic * (1.0 + pre_act * (1.0 - logistic))
    along_rank = lax.dot_general(
        incoming, up_proj, (((1,), (1,)), ((), ())), preferred_element_type=jnp.float32
    ) * (1.0 / math.sqrt(adapter_rank))
    back_grad = (along_rank * derivative).astype(jnp.bfloat16)
    grad_up = lax.dot_general(
        activated, incoming, (((0,), (0,)), ((), ())), preferred_element_type=jnp.float32
    ) * (1.0 / math.sqrt(adapter_rank))
    grad_down = lax.dot_general(
        back_grad, inputs_block, (((0,), (0,)), ((), ())), preferred_element_type=jnp.float32
    ) * (1.0 / math.sqrt(model_width))
    outgoing = (
        incoming.astype(jnp.float32)
        + jnp.dot(back_grad, down_proj, preferred_element_type=jnp.float32)
        * (1.0 / math.sqrt(model_width))
    ).astype(jnp.bfloat16)
    return (outgoing, jnp.stack([grad_down, grad_up]))


def body(saved_inputs, cotangent, weights_bf16, master, moment1, moment2, valid_rows):
    sections = lax.axis_size("pipe")
    section_index = lax.axis_index("pipe")
    weights = lax.all_gather(weights_bf16[0], "dp", axis=2, tiled=True)
    loss_grad = lax.all_gather(cotangent, "pipe", axis=1, tiled=True)
    inputs = saved_inputs[0]
    row_count = inputs.shape[0]
    model_width = inputs.shape[1]
    adapter_rank = weights.shape[1]
    live_rows = jnp.arange(row_count, dtype=jnp.int32) < valid_rows[0]
    loss_grad = jnp.where(live_rows[:, None], loss_grad, jnp.zeros_like(loss_grad))
    blocks = 1
    block_rows = row_count // blocks
    grad_shape = (2, adapter_rank, model_width)

    def chain_turn(step_index, state_pair):
        gradients, received = state_pair
        position = step_index - (sections - 1 - section_index)
        active = (position >= 0) & (position < blocks)
        incoming = jnp.where(section_index == sections - 1, loss_grad, received)

        def compute():
            return section_backward(inputs, incoming, weights)

        def skipped():
            return (
                jnp.zeros((block_rows, model_width), jnp.bfloat16),
                jnp.zeros(grad_shape, jnp.float32),
            )

        outgoing, grad_part = lax.cond(active, compute, skipped)
        received = shifted(outgoing, "pipe", -1)
        return (gradients + grad_part, received)

    start_pair = (
        jnp.zeros(grad_shape, jnp.float32),
        jnp.zeros((block_rows, model_width), jnp.bfloat16),
    )
    gradients, unused = lax.fori_loop(0, sections + blocks - 1, chain_turn, start_pair)
    grad_shard = lax.psum_scatter(gradients, "dp", scatter_dimension=2, tiled=True)
    square_sum = lax.psum(jnp.sum(grad_shard * grad_shard), ("pipe", "dp"))
    norm_limit = CLIP_RMS * math.sqrt(2.0 * sections * adapter_rank * model_width)
    clip_factor = jnp.minimum(1.0, norm_limit / jnp.sqrt(square_sum + NORM_EPS))
    scaled = grad_shard * clip_factor
    new_moment1 = BETA_ONE * moment1[0] + (1.0 - BETA_ONE) * scaled
    new_moment2 = BETA_TWO * moment2[0] + (1.0 - BETA_TWO) * scaled * scaled
    new_master = master[0] - LEARN_RATE * (
        new_moment1 / (jnp.sqrt(new_moment2) + ADAM_EPS) + DECAY_RATE * master[0]
    )
    return (
        new_master[None],
        new_moment1[None],
        new_moment2[None],
        new_master.astype(jnp.bfloat16)[None],
    )


def solution(mesh):
    in_specs = (
        P("pipe", "dp", None),
        P("dp", "pipe"),
        P("pipe", None, None, "dp"),
        P("pipe", None, None, "dp"),
        P("pipe", None, None, "dp"),
        P("pipe", None, None, "dp"),
        P("dp"),
    )
    out_specs = (
        P("pipe", None, None, "dp"),
        P("pipe", None, None, "dp"),
        P("pipe", None, None, "dp"),
        P("pipe", None, None, "dp"),
    )
    return jax.shard_map(body, mesh=mesh, in_specs=in_specs, out_specs=out_specs, check_vma=False)
```

profile of v0, /device:TPU:1, one launch (start us, length us, event | category | flops | bytes accessed | tf_op | source)
XLA Modules:
  0.0 1259.6 jit_solution(12248657878223781486)
XLA Ops:
  7.2 0.7 all-gather.4.cloned.1.call-update
  7.9 0.7 all-gather.6.cloned.1.call-update
  9.4 39.3 %all-gather.4.cloned.1.call-done = bf16[128,8192]{1,0:T(8,128)(2,1)} async-done(((bf16[128,1024]{1,0:T(8,128)(2,1)}), bf16[128,8192]{1,0:T(8,128)(2,1)}) %all-gather.4.cloned.1.call-update) | async-done | bytes 2097168 | tf_op jit(solution)/shard_map/all_gather | solution.py:56
  48.7 3.1 broadcast_select_fusion.1
  51.8 126.0 %all-gather.6.cloned.1.call-done = bf16[1,2,64,8192]{3,2,1,0:T(8,128)(2,1)} async-done(((bf16[1,2,64,128]{3,2,1,0:T(8,128)(2,1)}), bf16[1,2,64,8192]{3,2,1,0:T(8,128)(2,1)}) %all-gather.6.cloned.1.call-update) | async-done | bytes 2097168 | tf_op jit(solution)/shard_map/all_gather | solution.py:55
  177.8 1.5 broadcast.47
  179.3 272.9 %while.18 = (s32[]{:T(128)}, f32[2,64,8192]{2,1,0:T(8,128)}, bf16[128,8192]{1,0:T(8,128)(2,1)}, s32[]{:T(128)}, pred[]{:T(512)}, /*index=5*/bf16[128,8192]{1,0:T...) while((s32[]{:T(128)}, f32[2,64,8192]{2,1,0:T(8,128)}, ...), condition=%wide.region_3.4_spmd.clone, body=%wide.region_0.3_spmd.clone.sunk | while | flops 680656896 | bytes 72499496 | solution.py:90
  179.3 3.9 conditional.3
  179.3 2.4 broadcast.35
  181.7 1.5 broadcast.34
  183.3 11.6 collective-permute-start
  194.9 4.7 select_add_fusion.2
  199.5 20.4 %collective-permute-done = bf16[128,8192]{1,0:T(8,128)(2,1)} collective-permute-done((bf16[128,8192]{1,0:T(8,128)(2,1)}, bf16[128,8192]{1,0:T(8,128)(2,1)}, u32[]{:S(2)}, u32[]{:S(2)}) %collective-permute-start) | collective-permute-done | bytes 2097184 | tf_op jit(solution)/shard_map/while/body/eval_jaxpr/ppermute | solution.py:20
  220.0 3.9 conditional.3
  220.0 2.4 broadcast.35
  222.4 1.5 broadcast.34
  223.9 1.9 collective-permute-start
  225.8 5.9 select_add_fusion.2
  231.7 19.8 %collective-permute-done = bf16[128,8192]{1,0:T(8,128)(2,1)} collective-permute-done((bf16[128,8192]{1,0:T(8,128)(2,1)}, bf16[128,8192]{1,0:T(8,128)(2,1)}, u32[]{:S(2)}, u32[]{:S(2)}) %collective-permute-start) | collective-permute-done | bytes 2097184 | tf_op jit(solution)/shard_map/while/body/eval_jaxpr/ppermute | solution.py:20
  251.5 3.9 conditional.3
  251.5 2.4 broadcast.35
  253.9 1.5 broadcast.34
  255.4 1.9 collective-permute-start
  257.3 5.9 select_add_fusion.2
  263.3 19.8 %collective-permute-done = bf16[128,8192]{1,0:T(8,128)(2,1)} collective-permute-done((bf16[128,8192]{1,0:T(8,128)(2,1)}, bf16[128,8192]{1,0:T(8,128)(2,1)}, u32[]{:S(2)}, u32[]{:S(2)}) %collective-permute-start) | collective-permute-done | bytes 2097184 | tf_op jit(solution)/shard_map/while/body/eval_jaxpr/ppermute | solution.py:20
  283.1 3.9 conditional.3
  283.1 2.4 broadcast.35
  285.5 1.5 broadcast.34
  287.0 1.9 collective-permute-start
  288.9 5.9 select_add_fusion.2
  294.9 19.8 %collective-permute-done = bf16[128,8192]{1,0:T(8,128)(2,1)} collective-permute-done((bf16[128,8192]{1,0:T(8,128)(2,1)}, bf16[128,8192]{1,0:T(8,128)(2,1)}, u32[]{:S(2)}, u32[]{:S(2)}) %collective-permute-start) | collective-permute-done | bytes 2097184 | tf_op jit(solution)/shard_map/while/body/eval_jaxpr/ppermute | solution.py:20
  314.7 3.9 conditional.3
  314.7 2.4 broadcast.35
  317.1 1.5 broadcast.34
  318.6 1.9 collective-permute-start
  320.5 5.9 select_add_fusion.2
  326.4 19.8 %collective-permute-done = bf16[128,8192]{1,0:T(8,128)(2,1)} collective-permute-done((bf16[128,8192]{1,0:T(8,128)(2,1)}, bf16[128,8192]{1,0:T(8,128)(2,1)}, u32[]{:S(2)}, u32[]{:S(2)}) %collective-permute-start) | collective-permute-done | bytes 2097184 | tf_op jit(solution)/shard_map/while/body/eval_jaxpr/ppermute | solution.py:20
  346.2 3.9 conditional.3
  346.2 2.4 broadcast.35
  348.6 1.5 broadcast.34
  350.1 1.9 collective-permute-start
  352.1 5.9 select_add_fusion.2
  358.0 24.5 %collective-permute-done = bf16[128,8192]{1,0:T(8,128)(2,1)} collective-permute-done((bf16[128,8192]{1,0:T(8,128)(2,1)}, bf16[128,8192]{1,0:T(8,128)(2,1)}, u32[]{:S(2)}, u32[]{:S(2)}) %collective-permute-start) | collective-permute-done | bytes 2097184 | tf_op jit(solution)/shard_map/while/body/eval_jaxpr/ppermute | solution.py:20
  382.5 10.5 conditional.3
  382.5 2.2 convolution_multiply_fusion.3
  384.8 2.0 broadcast_select_fusion
  387.0 0.8 fusion.5
  387.8 0.5 fusion.3
  388.3 0.5 fusion.2
  388.8 2.3 pad_maximum_fusion
  391.0 2.0 fusion.1
  393.0 1.9 collective-permute-start
  395.0 5.9 select_add_fusion.2
  400.9 19.8 %collective-permute-done = bf16[128,8192]{1,0:T(8,128)(2,1)} collective-permute-done((bf16[128,8192]{1,0:T(8,128)(2,1)}, bf16[128,8192]{1,0:T(8,128)(2,1)}, u32[]{:S(2)}, u32[]{:S(2)}) %collective-permute-start) | collective-permute-done | bytes 2097184 | tf_op jit(solution)/shard_map/while/body/eval_jaxpr/ppermute | solution.py:20
  420.7 3.9 conditional.3
  420.7 2.4 broadcast.35
  423.1 1.5 broadcast.34
  424.6 1.9 collective-permute-start
  426.5 5.9 select_add_fusion.2
  432.5 19.8 %collective-permute-done = bf16[128,8192]{1,0:T(8,128)(2,1)} collective-permute-done((bf16[128,8192]{1,0:T(8,128)(2,1)}, bf16[128,8192]{1,0:T(8,128)(2,1)}, u32[]{:S(2)}, u32[]{:S(2)}) %collective-permute-start) | collective-permute-done | bytes 2097184 | tf_op jit(solution)/shard_map/while/body/eval_jaxpr/ppermute | solution.py:20
  452.3 684.5 %reduce-scatter.2.cloned.1.call-done = f32[2,64,128]{2,1,0:T(8,128)} async-done(((f32[2,64,8192]{2,1,0:T(8,128)}), f32[2,64,128]{2,1,0:T(8,128)}) %reduce-scatter.2.cloned.1.call-update) | async-done | bytes 65552 | tf_op jit(solution)/shard_map/reduce_scatter | solution.py:91
  1136.8 1.5 multiply_reduce_fusion
  1138.2 112.5 %psum.7 = f32[]{:T(128)} all-reduce(f32[]{:T(128)} %multiply_reduce_fusion), channel_id=1, replica_groups=mesh['pipe'=8,'dp'=64] {'pipe','dp'}, use_global_device_ids=true, to_apply=%region_6.7 | all-reduce | flops 1 | bytes 8 | tf_op jit(solution)/shard_map/psum | solution.py:92
  1251.5 1.6 convert_bitcast_fusion
  (18 shorter events, 0.4 us)
Async XLA Ops:
  7.2 41.5 %all-gather.4.cloned.1.call-start = ((), (), s32[]{:S(2)}) async-start(), calls=%async_computation.1 | async-start | bytes 2359296 | tf_op jit(solution)/shard_map/all_gather | solution.py:56
  7.9 169.9 %all-gather.6.cloned.1.call-start = ((), (), s32[]{:S(2)}) async-start(), calls=%async_computation.3 | async-start | bytes 2129920 | tf_op jit(solution)/shard_map/all_gather | solution.py:55
  8.6 1128.1 %reduce-scatter.2.cloned.1.call-start = ((), (), s32[]{:S(2)}) async-start(), calls=%async_computation.2 | async-start | bytes 4259840 | tf_op jit(solution)/shard_map/reduce_scatter | solution.py:91
  51.8 127.5 %copy-start = (bf16[1,128,8192]{2,1,0:T(8,128)(2,1)S(1)}, bf16[1,128,8192]{2,1,0:T(8,128)(2,1)}, u32[]{:S(2)}) copy-start(bf16[1,128,8192]{2,1,0:T(8,128)(2,1)} %param.11) | copy-start | bytes 6291460
  183.3 36.7 %collective-permute-start = (bf16[128,8192]{1,0:T(8,128)(2,1)}, bf16[128,8192]{1,0:T(8,128)(2,1)}, u32[]{:S(2)}, u32[]{:S(2)}) collective-permute-start(bf16[128,8192]{1,0:T(8,128)(2,1)} %get-tuple-element.300), channel_id=1, source_target_pairs={{64,0},{128,64},{192,128},{256,192},{320,256},{384,320},{448,384},... | collective-permute-start | bytes 6291464 | tf_op jit(solution)/shard_map/while/body/eval_jaxpr/ppermute | solution.py:20
  223.9 27.7 %collective-permute-start = (bf16[128,8192]{1,0:T(8,128)(2,1)}, bf16[128,8192]{1,0:T(8,128)(2,1)}, u32[]{:S(2)}, u32[]{:S(2)}) collective-permute-start(bf16[128,8192]{1,0:T(8,128)(2,1)} %get-tuple-element.300), channel_id=1, source_target_pairs={{64,0},{128,64},{192,128},{256,192},{320,256},{384,320},{448,384},... | collective-permute-start | bytes 6291464 | tf_op jit(solution)/shard_map/while/body/eval_jaxpr/ppermute | solution.py:20
  255.4 27.7 %collective-permute-start = (bf16[128,8192]{1,0:T(8,128)(2,1)}, bf16[128,8192]{1,0:T(8,128)(2,1)}, u32[]{:S(2)}, u32[]{:S(2)}) collective-permute-start(bf16[128,8192]{1,0:T(8,128)(2,1)} %get-tuple-element.300), channel_id=1, source_target_pairs={{64,0},{128,64},{192,128},{256,192},{320,256},{384,320},{448,384},... | collective-permute-start | bytes 6291464 | tf_op jit(solution)/shard_map/while/body/eval_jaxpr/ppermute | solution.py:20
  287.0 27.7 %collective-permute-start = (bf16[128,8192]{1,0:T(8,128)(2,1)}, bf16[128,8192]{1,0:T(8,128)(2,1)}, u32[]{:S(2)}, u32[]{:S(2)}) collective-permute-start(bf16[128,8192]{1,0:T(8,128)(2,1)} %get-tuple-element.300), channel_id=1, source_target_pairs={{64,0},{128,64},{192,128},{256,192},{320,256},{384,320},{448,384},... | collective-permute-start | bytes 6291464 | tf_op jit(solution)/shard_map/while/body/eval_jaxpr/ppermute | solution.py:20
  318.6 27.7 %collective-permute-start = (bf16[128,8192]{1,0:T(8,128)(2,1)}, bf16[128,8192]{1,0:T(8,128)(2,1)}, u32[]{:S(2)}, u32[]{:S(2)}) collective-permute-start(bf16[128,8192]{1,0:T(8,128)(2,1)} %get-tuple-element.300), channel_id=1, source_target_pairs={{64,0},{128,64},{192,128},{256,192},{320,256},{384,320},{448,384},... | collective-permute-start | bytes 6291464 | tf_op jit(solution)/shard_map/while/body/eval_jaxpr/ppermute | solution.py:20
  350.1 32.4 %collective-permute-start = (bf16[128,8192]{1,0:T(8,128)(2,1)}, bf16[128,8192]{1,0:T(8,128)(2,1)}, u32[]{:S(2)}, u32[]{:S(2)}) collective-permute-start(bf16[128,8192]{1,0:T(8,128)(2,1)} %get-tuple-element.300), channel_id=1, source_target_pairs={{64,0},{128,64},{192,128},{256,192},{320,256},{384,320},{448,384},... | collective-permute-start | bytes 6291464 | tf_op jit(solution)/shard_map/while/body/eval_jaxpr/ppermute | solution.py:20
  382.5 2.2 copy-start.2
  384.7 2.2 copy-start.1
  393.0 27.7 %collective-permute-start = (bf16[128,8192]{1,0:T(8,128)(2,1)}, bf16[128,8192]{1,0:T(8,128)(2,1)}, u32[]{:S(2)}, u32[]{:S(2)}) collective-permute-start(bf16[128,8192]{1,0:T(8,128)(2,1)} %get-tuple-element.300), channel_id=1, source_target_pairs={{64,0},{128,64},{192,128},{256,192},{320,256},{384,320},{448,384},... | collective-permute-start | bytes 6291464 | tf_op jit(solution)/shard_map/while/body/eval_jaxpr/ppermute | solution.py:20
  424.6 27.7 %collective-permute-start = (bf16[128,8192]{1,0:T(8,128)(2,1)}, bf16[128,8192]{1,0:T(8,128)(2,1)}, u32[]{:S(2)}, u32[]{:S(2)}) collective-permute-start(bf16[128,8192]{1,0:T(8,128)(2,1)} %get-tuple-element.300), channel_id=1, source_target_pairs={{64,0},{128,64},{192,128},{256,192},{320,256},{384,320},{448,384},... | collective-permute-start | bytes 6291464 | tf_op jit(solution)/shard_map/while/body/eval_jaxpr/ppermute | solution.py:20
  452.3 799.2 %copy-start.3 = (f32[1,2,64,128]{3,2,1,0:T(8,128)S(1)}, f32[1,2,64,128]{3,2,1,0:T(8,128)}, u32[]{:S(2)}) copy-start(f32[1,2,64,128]{3,2,1,0:T(8,128)} %param.16) | copy-start | bytes 196612
  452.3 799.2 %copy-start.4 = (f32[1,2,64,128]{3,2,1,0:T(8,128)S(1)}, f32[1,2,64,128]{3,2,1,0:T(8,128)}, u32[]{:S(2)}) copy-start(f32[1,2,64,128]{3,2,1,0:T(8,128)} %param.15) | copy-start | bytes 196612
  452.3 799.2 %copy-start.5 = (f32[1,2,64,128]{3,2,1,0:T(8,128)S(1)}, f32[1,2,64,128]{3,2,1,0:T(8,128)}, u32[]{:S(2)}) copy-start(f32[1,2,64,128]{3,2,1,0:T(8,128)} %param.14) | copy-start | bytes 196612
Sparse Core Ops, SparseCore 0:
  10.1 38.5 all-gather.3
  51.6 126.1 all-gather.5
  452.4 684.2 reduce-scatter.1
where the time goes:
time: 1260 us
  waiting for transfers between devices  1010 us (80%)
  blocking collectives  113 us (9%)
  other arithmetic  56.6 us (4%)
  local copies, waits for them, and re-layouts  29.1 us (2%)
  starting transfers between devices  25.1 us (2%)
  between operations  15.1 us (1%)
    reduce_scatter x1, waiting for transfers between devices, body(): lax.psum_scatter(gradients, 'dp', scatter_dimension=2, tiled=True)  684 us
    ppermute x8, waiting for transfers between devices, shifted(): return lax.ppermute(x, axis, pairs)  164 us
    all_gather x1, waiting for transfers between devices, body(): weights = lax.all_gather(weights_bf16[0], 'dp', axis=2, tiled=True)  126 us
    psum x1, blocking collectives, body(): square_sum = lax.psum(jnp.sum(grad_shard * grad_shard), ('pipe', 'dp'))  113 us
    add x8, other arithmetic, chain_turn(): return (gradients + grad_part, received)  46.2 us
    all_gather x1, waiting for transfers between devices, body(): loss_grad = lax.all_gather(cotangent, 'pipe', axis=1, tiled=True)  39.3 us
    another operation x15, local copies, waits for them, and re-layouts  28.9 us
  transfers between devices with their start and end apart: 11, of which 11 were waited for; matrix products, arithmetic and copies ran while one was open for 4% of the time, Pallas kernels for 0%

commit v1 on v0

v1 whole, which is shorter than its diff:
```python
import functools
import math

import jax
import jax.numpy as jnp
import numpy as np
from jax import lax
from jax.experimental import pallas as pl
from jax.experimental.pallas import tpu as pltpu
from jax.sharding import PartitionSpec as P

BETA_ONE = 0.9
BETA_TWO = 0.95
LEARN_RATE = 0.05
DECAY_RATE = 0.1
ADAM_EPS = 1e-08
CLIP_RMS = 2.0
NORM_EPS = 1e-12

LANES = 128
Y_SIZE = 4
VMEM_LIMIT = 48 * 1024 * 1024
INTERPRET = False
BF16 = jnp.bfloat16
F32 = jnp.float32


def contract_last(a, b):
    return lax.dot_general(a, b, (((1,), (1,)), ((), ())), preferred_element_type=F32)


def contract_first(a, b):
    return lax.dot_general(a, b, (((0,), (0,)), ((), ())), preferred_element_type=F32)


def vmem_specs(count):
    return [pl.BlockSpec(memory_space=pltpu.VMEM)] * count


def call(kernel, out_shape, operands, scratch=(), flops=0):
    size = sum(math.prod(a.shape) * a.dtype.itemsize for a in (*operands, out_shape))
    return pl.pallas_call(
        kernel,
        out_shape=out_shape,
        in_specs=[pl.BlockSpec(memory_space=pltpu.SMEM)] + vmem_specs(len(operands) - 1),
        out_specs=pl.BlockSpec(memory_space=pltpu.VMEM),
        scratch_shapes=list(scratch),
        compiler_params=pltpu.CompilerParams(vmem_limit_bytes=VMEM_LIMIT),
        cost_estimate=pl.CostEstimate(flops=flops, bytes_accessed=size, transcendentals=0),
        interpret=INTERPRET,
    )(*operands)


class Layout:
    def __init__(self, pipe, dp, rows, width, rank):
        self.pipe, self.dp, self.rows, self.width, self.rank = pipe, dp, rows, width, rank
        self.y = Y_SIZE if dp >= 64 else 2
        self.z = dp // self.y
        self.group = pipe * self.y
        self.span = width // self.y
        self.share = width // self.group
        self.per = self.z // pipe
        self.half = pipe // self.y
        self.piece = rows // pipe
        self.tiles = pipe * rank // LANES
        self.ranks = pipe * rank
        self.gram = max(self.tiles - 1, 2) * LANES
        y, z = self.y, self.z
        self.along_z = [[a * z + b for b in range(z)] for a in range(y)]
        self.along_y = [[a * z + b for a in range(y)] for b in range(z)]
        self.plane = [
            [p * dp + a * z + b for p in range(pipe) for a in range(y)] for b in range(z)
        ]

    def device(self, p, y, z):
        return p * self.dp + y * self.z + z

    def everywhere(self):
        return [(p, a, b) for p in range(self.pipe) for a in range(self.y) for b in range(self.z)]

    def turn_y(self, by):
        return [
            (a * self.z + b, (a + by) % self.y * self.z + b)
            for a in range(self.y)
            for b in range(self.z)
        ]

    def cotangent_turn(self, i):
        return [
            (
                self.device(p, a, b),
                self.device(self.y * (p % self.half) + (i + a) % self.y, p // self.half, b),
            )
            for p, a, b in self.everywhere()
        ]

    def gradient_home(self):
        return [
            (
                self.device(p, a, b),
                self.device(b // self.per, a, p * self.per + b % self.per),
            )
            for p, a, b in self.everywhere()
        ]

    def table(self):
        rows = []
        for p, a, b in self.everywhere():
            row = [(a - k) % self.y for k in range(self.y)]
            row += [(p % self.y - i) % self.y for i in range(self.y)]
            row += [p // 2, p % 2, 1 - p % 2]
            rows.append(row + [0] * (16 - len(row)))
        return np.asarray(rows, np.int32)


def pre_kernel(lay, table, w_ref, *refs):
    x_refs, out_ref = refs[: lay.y], refs[lay.y]
    lower, upper = table[0, 2 * lay.y + 1], table[0, 2 * lay.y + 2]
    maps = jnp.concatenate(
        [jnp.concatenate([w_ref[b, lower], w_ref[b, upper]], axis=0) for b in range(lay.z)],
        axis=1,
    )
    for k in range(lay.y):
        out_ref[table[0, k]] = contract_last(x_refs[k][...], maps).astype(BF16)


def section_maps(lay, w_ref, which):
    return jnp.concatenate(
        [
            jnp.concatenate([w_ref[s, j, which] for j in range(lay.per)], axis=1)
            for s in range(lay.pipe)
        ],
        axis=0,
    )


def pack_kernel(lay, table, w_ref, pre_ref, *refs):
    c_refs, out_ref = refs[: lay.y], refs[lay.y]
    down, up = section_maps(lay, w_ref, 0), section_maps(lay, w_ref, 1)
    gram_at, pre_at = lay.ranks, lay.ranks + lay.gram
    for i in range(lay.y):
        block = table[0, lay.y + i]
        part = contract_last(c_refs[i][...], up).astype(BF16)
        for p in range(lay.pipe):
            rows = slice(p * lay.piece, (p + 1) * lay.piece)
            out_ref[p * lay.y + block, :, 0:gram_at] = part[rows]
    for a in range(lay.y):
        for p in range(lay.pipe):
            rows = slice(p * lay.piece, (p + 1) * lay.piece)
            out_ref[p * lay.y + a, :, pre_at:] = pre_ref[a, rows, :]
    last = lay.tiles - 1
    each = lay.ranks // lay.group
    for t in range(lay.tiles):
        rows = down[t * LANES : (t + 1) * LANES]
        wide = min(t + 1, last if last >= 2 else t + 1) if t < last else last
        cols = [contract_last(rows, up[: wide * LANES]).astype(BF16)]
        if t == 0:
            corner = slice(last * LANES, (last + 1) * LANES)
            cols.append(contract_last(down[corner], up[corner]).astype(BF16))
            wide += 1
        if wide * LANES < lay.gram:
            cols.append(jnp.zeros((LANES, lay.gram - wide * LANES), BF16))
        full = jnp.concatenate(cols, axis=1) if len(cols) > 1 else cols[0]
        for q in range(LANES // each):
            out_ref[t * (LANES // each) + q, :, gram_at:pre_at] = full[q * each : (q + 1) * each]


def sum_kernel(lay, table, r_ref, out_ref):
    gram_end = lay.ranks + lay.gram
    total = r_ref[0, :, 0:gram_end].astype(F32)
    for q in range(1, lay.group):
        total += r_ref[q, :, 0:gram_end].astype(F32)
    lower = lax.broadcasted_iota(jnp.int32, (lay.piece, LANES), 1) < lay.rank
    pres = []
    for s in range(lay.pipe):
        one = r_ref[s * lay.y, :, gram_end:].astype(F32)
        for a in range(1, lay.y):
            one += r_ref[s * lay.y + a, :, gram_end:].astype(F32)
        pres.append(one)
    cols = [total] + [jnp.where(lower, pres[2 * t], pres[2 * t + 1]) for t in range(lay.tiles)]
    message = jnp.concatenate(cols, axis=1).astype(BF16)
    for q in range(lay.group):
        out_ref[q] = message


def chain_kernel(lay, table, q_ref, w_ref, *refs):
    c_refs, x_refs = refs[: lay.y], refs[lay.y : 2 * lay.y]
    out_ref, along, slope, acts, backs, gram, cots, held = refs[2 * lay.y :]
    width_scale, rank_scale = 1.0 / math.sqrt(lay.width), 1.0 / math.sqrt(lay.rank)
    gram_at, pre_at = lay.ranks, lay.ranks + lay.gram
    each = lay.ranks // lay.group
    for q in range(lay.group):
        p, a = q // lay.y, q % lay.y
        rows = slice(a * lay.rows + p * lay.piece, a * lay.rows + (p + 1) * lay.piece)
        along[rows, :] = q_ref[q, :, 0:gram_at].astype(F32)
        gram[q * each : (q + 1) * each, :] = q_ref[q, :, gram_at:pre_at]
        pre = q_ref[q, :, pre_at:].astype(F32) * width_scale
        gate = 1.0 / (1.0 + jnp.exp(-pre))
        acts[rows, :] = (pre * gate).astype(BF16)
        slope[rows, :] = gate * (1.0 + pre * (1.0 - gate)) * rank_scale
    for i in range(lay.y):
        cots[table[0, lay.y + i]] = c_refs[i][...]
    tokens = lay.y * lay.rows
    last = lay.tiles - 1
    lower = lax.broadcasted_iota(jnp.int32, (tokens, LANES), 1) < lay.rank
    for s in range(lay.pipe - 1, -1, -1):
        t, odd = s // 2, s % 2 == 1
        tile = slice(t * LANES, (t + 1) * LANES)
        back = along[:, tile] * slope[:, tile]
        back = jnp.where(lower != odd, back, 0.0).astype(BF16)
        if odd:
            backs[t] = back
        else:
            backs[t] = backs[t] + back
        if s == 0:
            continue
        plain = t if t == last or not odd else t + 1
        if plain > 0:
            cols = slice(0, plain * LANES)
            along[:, cols] += width_scale * jnp.dot(
                back, gram[tile, cols], preferred_element_type=F32
            )
        if t == last and odd:
            along[:, tile] += width_scale * jnp.dot(
                back, gram[0:LANES, LANES : 2 * LANES], preferred_element_type=F32
            )
    acted = acts[...]
    back_all = jnp.concatenate([backs[t] for t in range(lay.tiles)], axis=1)
    cross = contract_first(acted, back_all)
    before = lax.broadcasted_iota(jnp.int32, cross.shape, 0) // lay.rank
    after = lax.broadcasted_iota(jnp.int32, cross.shape, 1) // lay.rank
    cross = jnp.where(before < after, cross * width_scale, 0.0).astype(BF16)
    cot_all = cots[...].reshape(tokens, lay.share)
    grad_up = contract_first(acted, cot_all) + jnp.dot(
        cross, section_maps(lay, w_ref, 0), preferred_element_type=F32
    )
    grad_up = (grad_up * rank_scale).astype(BF16)
    for s in range(lay.pipe):
        for j in range(lay.per):
            out_ref[s * lay.per + j, lay.rank :, :] = grad_up[
                s * lay.rank : (s + 1) * lay.rank, j * LANES : (j + 1) * LANES
            ]
    mine, odd = table[0, 2 * lay.y], table[0, 2 * lay.y + 1]
    total = None
    for k in range(lay.y):
        start = pl.multiple_of(table[0, k] * lay.rows, lay.rows)
        part = contract_first(backs[mine, pl.ds(start, lay.rows), :], x_refs[k][...])
        total = part if total is None else total + part
    held[...] = (total * width_scale).reshape(2, lay.rank, lay.span)
    grad_down = held[odd].astype(BF16)
    for b in range(lay.z):
        out_ref[b, 0 : lay.rank, :] = grad_down[:, b * LANES : (b + 1) * LANES]


def body(saved_inputs, cotangent, weights_bf16, master, moment1, moment2, valid_rows):
    pipe, dp = lax.axis_size("pipe"), lax.axis_size("dp")
    inputs, weights = saved_inputs[0], weights_bf16[0]
    lay = Layout(pipe, dp, inputs.shape[0], inputs.shape[1], weights.shape[1])
    both = ("pipe", "dp")
    p_index, d_index = lax.axis_index("pipe"), lax.axis_index("dp")
    y_index = d_index // lay.z
    table = lax.dynamic_slice(jnp.asarray(lay.table()), (p_index * dp + d_index, 0), (1, 16))

    x_pieces = []
    for k in range(lay.y):
        start = (y_index + k) % lay.y * lay.span
        piece = lax.dynamic_slice(inputs, (0, start), (lay.rows, lay.span))
        x_pieces.append(lax.ppermute(piece, "dp", lay.turn_y(k)) if k else piece)
    live_rows = jnp.arange(lay.rows, dtype=jnp.int32) < valid_rows[0]
    loss_grad = jnp.where(live_rows[:, None], cotangent, jnp.zeros_like(cotangent))
    c_pieces = []
    for i in range(lay.y):
        start = (y_index + i) % lay.y * lay.share
        piece = lax.dynamic_slice(loss_grad, (0, start), (lay.rows, lay.share))
        c_pieces.append(lax.ppermute(piece, both, lay.cotangent_turn(i)))

    maps = lax.all_gather(weights, "dp", axis_index_groups=lay.along_z)
    shared = lax.all_to_all(
        maps.reshape(pipe, lay.per, 2, lay.rank, LANES), "pipe", 0, 0
    )
    pre_part = call(
        functools.partial(pre_kernel, lay),
        jax.ShapeDtypeStruct((lay.y, lay.rows, LANES), BF16),
        (table, maps, *x_pieces),
        flops=2 * lay.y * lay.rows * lay.span * LANES,
    )
    message = lay.ranks + lay.gram + LANES
    parts = call(
        functools.partial(pack_kernel, lay),
        jax.ShapeDtypeStruct((lay.group, lay.piece, message), BF16),
        (table, shared, pre_part, *c_pieces),
        flops=4 * lay.y * lay.rows * lay.share * lay.ranks,
    )
    parts = lax.all_to_all(parts, both, 0, 0, axis_index_groups=lay.plane)
    reply = 2 * lay.ranks + lay.gram
    sums = call(
        functools.partial(sum_kernel, lay),
        jax.ShapeDtypeStruct((lay.group, lay.piece, reply), BF16),
        (table, parts),
    )
    sums = lax.all_to_all(sums, both, 0, 0, axis_index_groups=lay.plane)
    tokens = lay.y * lay.rows
    grads = call(
        functools.partial(chain_kernel, lay),
        jax.ShapeDtypeStruct((lay.z, 2 * lay.rank, LANES), BF16),
        (table, sums, shared, *c_pieces, *x_pieces),
        scratch=(
            pltpu.VMEM((tokens, lay.ranks), F32),
            pltpu.VMEM((tokens, lay.ranks), F32),
            pltpu.VMEM((tokens, lay.ranks), BF16),
            pltpu.VMEM((lay.tiles, tokens, LANES), BF16),
            pltpu.VMEM((lay.ranks, lay.gram), BF16),
            pltpu.VMEM((lay.y, lay.rows, lay.share), BF16),
            pltpu.VMEM((2, lay.rank, lay.span), F32),
        ),
        flops=8 * tokens * lay.ranks * lay.share,
    )
    grads = lax.all_to_all(grads, "dp", 0, 0, axis_index_groups=lay.along_z)
    grads = jnp.sum(grads.astype(F32), axis=0)
    squares = jnp.sum((grads * grads).reshape(-1, 8, LANES), axis=0)
    grad_up = lax.ppermute(grads[lay.rank :], both, lay.gradient_home())
    squares = jnp.broadcast_to(squares, (lay.group, 8, LANES))
    squares = lax.all_to_all(squares, both, 0, 0, axis_index_groups=lay.plane)
    squares = jnp.broadcast_to(jnp.sum(squares, axis=0), (lay.z, 8, LANES))
    squares = lax.all_to_all(squares, "dp", 0, 0, axis_index_groups=lay.along_z)
    square_sum = jnp.sum(squares)
    norm_limit = CLIP_RMS * math.sqrt(2.0 * pipe * lay.rank * lay.width)
    clip_factor = jnp.minimum(1.0, norm_limit / jnp.sqrt(square_sum + NORM_EPS))
    scaled = jnp.stack([grads[: lay.rank], grad_up]) * clip_factor
    new_moment1 = BETA_ONE * moment1[0] + (1.0 - BETA_ONE) * scaled
    new_moment2 = BETA_TWO * moment2[0] + (1.0 - BETA_TWO) * scaled * scaled
    new_master = master[0] - LEARN_RATE * (
        new_moment1 / (jnp.sqrt(new_moment2) + ADAM_EPS) + DECAY_RATE * master[0]
    )
    return (
        new_master[None],
        new_moment1[None],
        new_moment2[None],
        new_master.astype(BF16)[None],
    )


def solution(mesh):
    in_specs = (
        P("pipe", "dp", None),
        P("dp", "pipe"),
        P("pipe", None, None, "dp"),
        P("pipe", None, None, "dp"),
        P("pipe", None, None, "dp"),
        P("pipe", None, None, "dp"),
        P("dp"),
    )
    out_specs = (
        P("pipe", None, None, "dp"),
        P("pipe", None, None, "dp"),
        P("pipe", None, None, "dp"),
        P("pipe", None, None, "dp"),
    )
    return jax.shard_map(body, mesh=mesh, in_specs=in_specs, out_specs=out_specs, check_vma=False)
```

time: 1260 us -> 206 us (0.16)
  waiting for transfers between devices: 1010 us -> 6.47 us
  other arithmetic: 56.6 us -> 1.54 us
  starting transfers between devices: 25.1 us -> 51.7 us
  local copies, waits for them, and re-layouts: 29.1 us -> 4.84 us
  blocking collectives: 113 us -> 130 us
  between operations: 15.1 us -> 2.39 us
    reduce_scatter x1 -> x0, waiting for transfers between devices: 684 us -> none  [body(): lax.psum_scatter(gradients, 'dp', scatter_dimension=2, tiled=True)]
    all_gather x2 -> x0, waiting for transfers between devices: 165 us -> none  [the longest x1 126 us: body(): weights = lax.all_gather(weights_bf16[0], 'dp', axis=2, tiled=True)]
    ppermute x8, waiting for transfers between devices: 164 us -> 0.02 us  [the longest x4 0.01 us: body(): c_pieces.append(lax.ppermute(piece, both, lay.cotangent_turn(i)))]
    psum x1 -> x0, blocking collectives: 113 us -> none  [body(): square_sum = lax.psum(jnp.sum(grad_shard * grad_shard), ('pipe', 'dp'))]
    all_to_all x0 -> x4, blocking collectives: none -> 96.2 us  [the longest x1 29.4 us: body(): grads = lax.all_to_all(grads, 'dp', 0, 0, axis_index_groups=lay.along_z)]
    add x8 -> x0, other arithmetic: 46.2 us -> none  [chain_turn(): return (gradients + grad_part, received)]
    all_gather x0 -> x1, blocking collectives: none -> 33.8 us  [body(): maps = lax.all_gather(weights, 'dp', axis_index_groups=lay.along_z)]
    another operation x15 -> x1, local copies, waits for them, and re-layouts: 28.9 us -> 0.01 us  [body(): scaled = jnp.stack([grads[:lay.rank], grad_up]) * clip_factor]
  transfers between devices with their start and end apart: 11 -> 10, of which waited for: 11 -> 1; matrix products, arithmetic and copies ran while one was open for 4% -> 1% of each run, Pallas kernels for 0% -> 1%
where the time goes in v1:
time: 206 us; the launch traced here: 204 us
  blocking collectives  130 us (63%)
  starting transfers between devices  51.7 us (25%)
  Pallas kernels  7.15 us (3%)
  waiting for transfers between devices  6.47 us (3%)
  local copies, waits for them, and re-layouts  4.84 us (2%)
  between operations  2.39 us (1%)
    all_gather x1, blocking collectives, body(): maps = lax.all_gather(weights, 'dp', axis_index_groups=lay.along_z)  33.8 us
    all_to_all x1, blocking collectives, body(): grads = lax.all_to_all(grads, 'dp', 0, 0, axis_index_groups=lay.along_z)  29.4 us
    all_to_all x1, blocking collectives, body(): sums = lax.all_to_all(sums, both, 0, 0, axis_index_groups=lay.plane)  25.6 us
    all_to_all x1, blocking collectives, body(): parts = lax.all_to_all(parts, both, 0, 0, axis_index_groups=lay.plane)  23.3 us
    all_to_all x1, blocking collectives, body(): squares = lax.all_to_all(squares, both, 0, 0, axis_index_groups=lay.plane)  17.8 us
    ppermute x4, starting transfers between devices, body(): c_pieces.append(lax.ppermute(piece, both, lay.cotangent_turn(i)))  17.1 us
    all_to_all x1, starting transfers between devices, body(): lax.all_to_all(maps.reshape(pipe, lay.per, 2, lay.rank, LANES), 'pipe', 0...  11.9 us
    ppermute x3, starting transfers between devices, body(): x_pieces.append(lax.ppermute(piece, 'dp', lay.turn_y(k)) if k else piece)  11.5 us
  transfers between devices with their start and end apart: 10, of which 1 were waited for; matrix products, arithmetic and copies ran while one was open for 1% of the time, Pallas kernels for 1%

profile of v1, /device:TPU:1, one launch (start us, length us, event | category | flops | bytes accessed | tf_op | source)
XLA Modules:
  0.0 204.1 jit_solution(8947830017398900671)
XLA Ops:
  0.7 0.0 copy-start.4
  0.7 0.0 copy-start
  0.8 2.7 %dynamic-slice_bitcast_fusion = (bf16[128,2048]{1,0:T(8,128)(2,1)}, bf16[128,2048]{1,0:T(8,128)(2,1)}, bf16[128,2048]{1,0:T(8,128)(2,1)S(1)}, bf16[128,2048]{1,0:T(8,128)(2,1)S(1)}) fusion(bf16[1,128,8192]{2,1,0:T(8,128)(2,1)} %param.8, s32[]{:T(128)S(6)} %select_n.71, s32[]{:T(128)S(6)} %select_n.67, s32[]{:T(128)S(6)} %select_n.65, s32[]{:T(128)S(6)} %select_n.69), kind=kLoop, calls=%fused_computation.1 | loop fusion | bytes 4194320 | tf_op jit(solution)/shard_map/dynamic_slice | solution.py:267
  3.5 5.5 %collective-permute-start.2 = (bf16[128,2048]{1,0:T(8,128)(2,1)}, bf16[128,2048]{1,0:T(8,128)(2,1)S(1)}, u32[]{:S(2)}, u32[]{:S(2)}) collective-permute-start(bf16[128,2048]{1,0:T(8,128)(2,1)} %get-tuple-element.8), channel_id=1, source_target_pairs={{0,48},{1,49},{2,50},{3,51},{4,52},{5,53},{6,54},{7,55},{8,56},{9,... | collective-permute-start | bytes 1572872 | tf_op jit(solution)/shard_map/ppermute | solution.py:268
  9.0 1.9 collective-permute-start
  10.9 0.0 copy-done.4
  10.9 33.8 %all_gather.3.w_ref = bf16[16,2,64,128]{3,2,1,0:T(8,128)(2,1)} all-gather(bf16[1,2,64,128]{3,2,1,0:T(8,128)(2,1)S(1)} %copy-done.4), channel_id=1, replica_groups={{0,1,2,3,4,5,6,7,8,9,10,11,12,13,14,15},{16,17,18,19,20,21,22,23,24,25,..., dimensions={0}, use_global_device_ids=true | all-gather | bytes 557056 | tf_op jit(solution)/shard_map/all_gather | solution.py:277
  44.7 11.9 %all-to-all-start = ((bf16[8,2,2,64,128]{4,3,2,1,0:T(8,128)(2,1)}), bf16[8,2,2,64,128]{4,3,2,1,0:T(8,128)(2,1)S(1)}, u32[]{:S(2)}, u32[]{:S(2)}) async-start(bf16[8,2,2,64,128]{4,3,2,1,0:T(8,128)(2,1)} %bitcast), calls=%async_computation | async-start | bytes 1048576 | tf_op jit(solution)/shard_map/all_to_all | solution.py:278
  56.7 4.2 %collective-permute-start.1 = (bf16[128,2048]{1,0:T(8,128)(2,1)S(1)}, bf16[128,2048]{1,0:T(8,128)(2,1)S(1)}, u32[]{:S(2)}, u32[]{:S(2)}) collective-permute-start(bf16[128,2048]{1,0:T(8,128)(2,1)S(1)} %get-tuple-element.11), channel_id=1, source_target_pairs={{0,32},{1,33},{2,34},{3,35},{4,36},{5,37},{6,38},{7,39},{8,40},{9,... | collective-permute-start | bytes 1572872 | tf_op jit(solution)/shard_map/ppermute | solution.py:268
  61.5 0.0 copy-done
  61.6 0.1 broadcast_select_fusion
  61.6 0.7 constant_dynamic-slice_fusion
  62.4 4.5 %collective-permute-start.6 = (bf16[128,256]{1,0:T(8,128)(2,1)}, bf16[128,256]{1,0:T(8,128)(2,1)S(1)}, u32[]{:S(2)}, u32[]{:S(2)}) collective-permute-start(bf16[128,256]{1,0:T(8,128)(2,1)} %get-tuple-element.12), channel_id=1, source_target_pairs={{0,192},{1,193},{2,194},{3,195},{4,196},{5,197},{6,198},{7,199},{8... | collective-permute-start | bytes 196616 | tf_op jit(solution)/shard_map/ppermute | solution.py:275
  66.9 4.2 %collective-permute-start.5 = (bf16[128,256]{1,0:T(8,128)(2,1)}, bf16[128,256]{1,0:T(8,128)(2,1)S(1)}, u32[]{:S(2)}, u32[]{:S(2)}) collective-permute-start(bf16[128,256]{1,0:T(8,128)(2,1)} %get-tuple-element.13), channel_id=1, source_target_pairs={{0,128},{1,129},{2,130},{3,131},{4,132},{5,133},{6,134},{7,135},{8... | collective-permute-start | bytes 196616 | tf_op jit(solution)/shard_map/ppermute | solution.py:275
  71.1 0.0 collective-permute-done.2.refs_3_.refs_7_
  71.1 2.9 %collective-permute-start.4 = (bf16[128,256]{1,0:T(8,128)(2,1)}, bf16[128,256]{1,0:T(8,128)(2,1)S(1)}, u32[]{:S(2)}, u32[]{:S(2)}) collective-permute-start(bf16[128,256]{1,0:T(8,128)(2,1)} %get-tuple-element.14), channel_id=1, source_target_pairs={{0,64},{1,65},{2,66},{3,67},{4,68},{5,69},{6,70},{7,71},{8,72},{9,... | collective-permute-start | bytes 196616 | tf_op jit(solution)/shard_map/ppermute | solution.py:275
  74.0 0.0 collective-permute-done.refs_1_.refs_5_
  74.0 5.6 %collective-permute-start.3 = (bf16[128,256]{1,0:T(8,128)(2,1)}, bf16[128,256]{1,0:T(8,128)(2,1)S(1)}, u32[]{:S(2)}, u32[]{:S(2)}) collective-permute-start(bf16[128,256]{1,0:T(8,128)(2,1)} %get-tuple-element.15), channel_id=1, source_target_pairs={{0,0},{1,1},{2,2},{3,3},{4,4},{5,5},{6,6},{7,7},{8,8},{9,9},{10,10... | collective-permute-start | bytes 196616 | tf_op jit(solution)/shard_map/ppermute | solution.py:275
  79.6 0.7 constant_dynamic-slice_fusion.4.table
  80.3 0.0 collective-permute-done.1.refs_2_.refs_6_
  80.3 1.8 shard_map.111.pre_ref
  82.0 0.0 collective-permute-done.6.refs_3_
  82.0 0.0 collective-permute-done.5.refs_2_
  82.1 0.0 collective-permute-done.4.refs_1_
  82.1 0.0 collective-permute-done.3.refs_0_
  82.1 0.0 all-to-all-done.w_ref
  82.1 1.3 shard_map.112
  83.3 23.3 %all_to_all.30.r_ref = bf16[32,16,1024]{2,1,0:T(8,128)(2,1)S(1)} all-to-all(bf16[32,16,1024]{2,1,0:T(8,128)(2,1)S(1)} %shard_map.112), channel_id=1, replica_groups={{0,16,32,48,64,80,96,112,128,144,160,176,192,208,224,240,256,272,288,30..., dimensions={0} | all-to-all | bytes 2097152 | tf_op jit(solution)/shard_map/all_to_all | solution.py:294
  106.7 0.7 shard_map.113
  107.4 25.6 %all_to_all.31.q_ref = bf16[32,16,1408]{2,1,0:T(8,128)(2,1)S(1)} all-to-all(bf16[32,16,1408]{2,1,0:T(8,128)(2,1)S(1)} %shard_map.113), channel_id=1, replica_groups={{0,16,32,48,64,80,96,112,128,144,160,176,192,208,224,240,256,272,288,30..., dimensions={0} | all-to-all | bytes 2883584 | tf_op jit(solution)/shard_map/all_to_all | solution.py:301
  133.0 3.4 %shard_map.114 = bf16[16,128,128]{2,1,0:T(8,128)(2,1)S(1)} custom-call(s32[1,16]{1,0:T(1,128)S(1)} %constant_dynamic-slice_fusion.4.table, bf16[32,16,1408]{2,1,0:T(8,128)(2,1)S(1)} %all_to_all.31.q_ref, bf16[8,2,2,64,128]{4,3,2,1,0:T(8,128)(2,1)S(1)} %all-to-all-done.w_ref, bf16[128,256]{1,0:T(8,128)(2,1)S(1)} %collective-permute-done.3.refs_0_, ...), custom_call_target="tpu_custom_call" | custom-call | flops 536870912 | bytes 4849728 | tf_op jit(solution)/shard_map/pallas_call | solution.py:42
  136.4 0.0 copy-start.1
  136.5 0.0 copy-start.2
  136.5 0.0 copy-start.3
  136.5 29.4 %all_to_all.32 = bf16[16,128,128]{2,1,0:T(8,128)(2,1)S(1)} all-to-all(bf16[16,128,128]{2,1,0:T(8,128)(2,1)S(1)} %shard_map.114), channel_id=1, replica_groups={{0,1,2,3,4,5,6,7,8,9,10,11,12,13,14,15},{16,17,18,19,20,21,22,23,24,25,..., dimensions={0} | all-to-all | bytes 1048576 | tf_op jit(solution)/shard_map/all_to_all | solution.py:318
  165.9 0.1 convert_reduce_fusion
  166.0 17.8 %all_to_all.33 = f32[32,8,128]{2,1,0:T(8,128)S(1)} all-to-all(f32[32,8,128]{2,1,0:T(8,128)S(1)} %broadcast_in_dim.24), channel_id=1, replica_groups={{0,16,32,48,64,80,96,112,128,144,160,176,192,208,224,240,256,272,288,30..., dimensions={0} | all-to-all | bytes 262144 | tf_op jit(solution)/shard_map/all_to_all | solution.py:323
  183.9 0.6 broadcast_in_dim.25
  184.5 6.0 %all-to-all-start.5 = ((f32[16,8,128]{2,1,0:T(8,128)}), f32[16,8,128]{2,1,0:T(8,128)S(1)}, u32[]{:S(2)}, u32[]{:S(2)}) async-start(f32[16,8,128]{2,1,0:T(8,128)} %broadcast_in_dim.25), calls=%async_computation.5 | async-start | bytes 131072 | tf_op jit(solution)/shard_map/all_to_all | solution.py:325
  190.5 5.1 %collective-permute-start.7 = (f32[64,128]{1,0:T(8,128)S(1)}, f32[64,128]{1,0:T(8,128)S(1)}, u32[]{:S(2)}, u32[]{:S(2)}) collective-permute-start(f32[64,128]{1,0:T(8,128)S(1)} %get-tuple-element.17), channel_id=1, source_target_pairs={{0,0},{1,1},{2,64},{3,65},{4,128},{5,129},{6,192},{7,193},{8,256},... | collective-permute-start | bytes 98312 | tf_op jit(solution)/shard_map/ppermute | solution.py:321
  195.6 6.4 %all-to-all-done.5 = f32[16,8,128]{2,1,0:T(8,128)S(1)} async-done(((f32[16,8,128]{2,1,0:T(8,128)}), f32[16,8,128]{2,1,0:T(8,128)S(1)}, u32[]{:S(2)}, u32[]{:S(2)}) %all-to-all-start.5) | async-done | bytes 65568 | tf_op jit(solution)/shard_map/all_to_all | solution.py:325
  202.1 0.6 reduce_sum.39
  203.4 0.0 collective-permute-done.7
  203.4 0.0 copy-done.1
  203.4 0.0 copy-done.2
  203.4 0.0 copy-done.3
  203.4 0.7 fusion.1
  (5 shorter events, 0.1 us)
Async XLA Ops:
  0.7 10.2 %copy-start.4 = (bf16[1,2,64,128]{3,2,1,0:T(8,128)(2,1)S(1)}, bf16[1,2,64,128]{3,2,1,0:T(8,128)(2,1)}, u32[]{:S(2)}) copy-start(bf16[1,2,64,128]{3,2,1,0:T(8,128)(2,1)} %param.10) | copy-start | bytes 98308
  0.7 60.8 %copy-start = (bf16[128,1024]{1,0:T(8,128)(2,1)S(1)}, bf16[128,1024]{1,0:T(8,128)(2,1)}, u32[]{:S(2)}) copy-start(bf16[128,1024]{1,0:T(8,128)(2,1)} %param.9) | copy-start | bytes 786436
  3.5 67.6 %collective-permute-start.2 = (bf16[128,2048]{1,0:T(8,128)(2,1)}, bf16[128,2048]{1,0:T(8,128)(2,1)S(1)}, u32[]{:S(2)}, u32[]{:S(2)}) collective-permute-start(bf16[128,2048]{1,0:T(8,128)(2,1)} %get-tuple-element.8), channel_id=1, source_target_pairs={{0,48},{1,49},{2,50},{3,51},{4,52},{5,53},{6,54},{7,55},{8,56},{9,... | collective-permute-start | bytes 1572872 | tf_op jit(solution)/shard_map/ppermute | solution.py:268
  9.0 65.0 %collective-permute-start = (bf16[128,2048]{1,0:T(8,128)(2,1)}, bf16[128,2048]{1,0:T(8,128)(2,1)S(1)}, u32[]{:S(2)}, u32[]{:S(2)}) collective-permute-start(bf16[128,2048]{1,0:T(8,128)(2,1)} %get-tuple-element.9), channel_id=1, source_target_pairs={{0,16},{1,17},{2,18},{3,19},{4,20},{5,21},{6,22},{7,23},{8,24},{9,... | collective-permute-start | bytes 1572872 | tf_op jit(solution)/shard_map/ppermute | solution.py:268
  44.7 37.3 %all-to-all-start = ((bf16[8,2,2,64,128]{4,3,2,1,0:T(8,128)(2,1)}), bf16[8,2,2,64,128]{4,3,2,1,0:T(8,128)(2,1)S(1)}, u32[]{:S(2)}, u32[]{:S(2)}) async-start(bf16[8,2,2,64,128]{4,3,2,1,0:T(8,128)(2,1)} %bitcast), calls=%async_computation | async-start | bytes 1048576 | tf_op jit(solution)/shard_map/all_to_all | solution.py:278
  56.7 23.6 %collective-permute-start.1 = (bf16[128,2048]{1,0:T(8,128)(2,1)S(1)}, bf16[128,2048]{1,0:T(8,128)(2,1)S(1)}, u32[]{:S(2)}, u32[]{:S(2)}) collective-permute-start(bf16[128,2048]{1,0:T(8,128)(2,1)S(1)} %get-tuple-element.11), channel_id=1, source_target_pairs={{0,32},{1,33},{2,34},{3,35},{4,36},{5,37},{6,38},{7,39},{8,40},{9,... | collective-permute-start | bytes 1572872 | tf_op jit(solution)/shard_map/ppermute | solution.py:268
  62.4 19.7 %collective-permute-start.6 = (bf16[128,256]{1,0:T(8,128)(2,1)}, bf16[128,256]{1,0:T(8,128)(2,1)S(1)}, u32[]{:S(2)}, u32[]{:S(2)}) collective-permute-start(bf16[128,256]{1,0:T(8,128)(2,1)} %get-tuple-element.12), channel_id=1, source_target_pairs={{0,192},{1,193},{2,194},{3,195},{4,196},{5,197},{6,198},{7,199},{8... | collective-permute-start | bytes 196616 | tf_op jit(solution)/shard_map/ppermute | solution.py:275
  66.9 15.2 %collective-permute-start.5 = (bf16[128,256]{1,0:T(8,128)(2,1)}, bf16[128,256]{1,0:T(8,128)(2,1)S(1)}, u32[]{:S(2)}, u32[]{:S(2)}) collective-permute-start(bf16[128,256]{1,0:T(8,128)(2,1)} %get-tuple-element.13), channel_id=1, source_target_pairs={{0,128},{1,129},{2,130},{3,131},{4,132},{5,133},{6,134},{7,135},{8... | collective-permute-start | bytes 196616 | tf_op jit(solution)/shard_map/ppermute | solution.py:275
  71.1 11.0 %collective-permute-start.4 = (bf16[128,256]{1,0:T(8,128)(2,1)}, bf16[128,256]{1,0:T(8,128)(2,1)S(1)}, u32[]{:S(2)}, u32[]{:S(2)}) collective-permute-start(bf16[128,256]{1,0:T(8,128)(2,1)} %get-tuple-element.14), channel_id=1, source_target_pairs={{0,64},{1,65},{2,66},{3,67},{4,68},{5,69},{6,70},{7,71},{8,72},{9,... | collective-permute-start | bytes 196616 | tf_op jit(solution)/shard_map/ppermute | solution.py:275
  74.0 8.1 %collective-permute-start.3 = (bf16[128,256]{1,0:T(8,128)(2,1)}, bf16[128,256]{1,0:T(8,128)(2,1)S(1)}, u32[]{:S(2)}, u32[]{:S(2)}) collective-permute-start(bf16[128,256]{1,0:T(8,128)(2,1)} %get-tuple-element.15), channel_id=1, source_target_pairs={{0,0},{1,1},{2,2},{3,3},{4,4},{5,5},{6,6},{7,7},{8,8},{9,9},{10,10... | collective-permute-start | bytes 196616 | tf_op jit(solution)/shard_map/ppermute | solution.py:275
  136.4 67.0 %copy-start.1 = (f32[1,2,64,128]{3,2,1,0:T(8,128)S(1)}, f32[1,2,64,128]{3,2,1,0:T(8,128)}, u32[]{:S(2)}) copy-start(f32[1,2,64,128]{3,2,1,0:T(8,128)} %param.11) | copy-start | bytes 196612
  136.5 66.9 %copy-start.2 = (f32[1,2,64,128]{3,2,1,0:T(8,128)S(1)}, f32[1,2,64,128]{3,2,1,0:T(8,128)}, u32[]{:S(2)}) copy-start(f32[1,2,64,128]{3,2,1,0:T(8,128)} %param.13) | copy-start | bytes 196612
  136.5 66.9 %copy-start.3 = (f32[1,2,64,128]{3,2,1,0:T(8,128)S(1)}, f32[1,2,64,128]{3,2,1,0:T(8,128)}, u32[]{:S(2)}) copy-start(f32[1,2,64,128]{3,2,1,0:T(8,128)} %param.12) | copy-start | bytes 196612
  184.5 17.6 %all-to-all-start.5 = ((f32[16,8,128]{2,1,0:T(8,128)}), f32[16,8,128]{2,1,0:T(8,128)S(1)}, u32[]{:S(2)}, u32[]{:S(2)}) async-start(f32[16,8,128]{2,1,0:T(8,128)} %broadcast_in_dim.25), calls=%async_computation.5 | async-start | bytes 131072 | tf_op jit(solution)/shard_map/all_to_all | solution.py:325
  190.5 12.9 %collective-permute-start.7 = (f32[64,128]{1,0:T(8,128)S(1)}, f32[64,128]{1,0:T(8,128)S(1)}, u32[]{:S(2)}, u32[]{:S(2)}) collective-permute-start(f32[64,128]{1,0:T(8,128)S(1)} %get-tuple-element.17), channel_id=1, source_target_pairs={{0,0},{1,1},{2,64},{3,65},{4,128},{5,129},{6,192},{7,193},{8,256},... | collective-permute-start | bytes 98312 | tf_op jit(solution)/shard_map/ppermute | solution.py:321

commit v2 on v1

--- a/solution.py
+++ b/solution.py
@@ -3,7 +3,6 @@
 
 import jax
 import jax.numpy as jnp
-import numpy as np
 from jax import lax
 from jax.experimental import pallas as pl
 from jax.experimental.pallas import tpu as pltpu
@@ -78,18 +77,11 @@
     def everywhere(self):
         return [(p, a, b) for p in range(self.pipe) for a in range(self.y) for b in range(self.z)]
 
-    def turn_y(self, by):
-        return [
-            (a * self.z + b, (a + by) % self.y * self.z + b)
-            for a in range(self.y)
-            for b in range(self.z)
-        ]
-
-    def cotangent_turn(self, i):
+    def cotangent_turn(self):
         return [
             (
                 self.device(p, a, b),
-                self.device(self.y * (p % self.half) + (i + a) % self.y, p // self.half, b),
+                self.device(self.y * (p % self.half) + a, p // self.half, b),
             )
             for p, a, b in self.everywhere()
         ]
@@ -103,25 +95,42 @@
             for p, a, b in self.everywhere()
         ]
 
-    def table(self):
-        rows = []
-        for p, a, b in self.everywhere():
-            row = [(a - k) % self.y for k in range(self.y)]
-            row += [(p % self.y - i) % self.y for i in range(self.y)]
-            row += [p // 2, p % 2, 1 - p % 2]
-            rows.append(row + [0] * (16 - len(row)))
-        return np.asarray(rows, np.int32)
-
-
-def pre_kernel(lay, table, w_ref, *refs):
-    x_refs, out_ref = refs[: lay.y], refs[lay.y]
-    lower, upper = table[0, 2 * lay.y + 1], table[0, 2 * lay.y + 2]
+
+def sort_kernel(lay, valid, x_ref, c_ref, out_ref):
+    out_ref[0, :, 0 : lay.span] = x_ref[...]
+    cot = c_ref[...]
+    live = lax.broadcasted_iota(jnp.int32, cot.shape, 0) < valid[0]
+    out_ref[0, :, lay.span :] = jnp.where(live, cot, jnp.zeros_like(cot))
+
+
+def sort_columns(lay, valid_rows, inputs, cotangent):
+    both = lay.span + lay.share
+    return pl.pallas_call(
+        functools.partial(sort_kernel, lay),
+        grid=(lay.y,),
+        out_shape=jax.ShapeDtypeStruct((lay.y, lay.rows, both), BF16),
+        in_specs=[
+            pl.BlockSpec(memory_space=pltpu.SMEM),
+            pl.BlockSpec((lay.rows, lay.span), lambda a: (0, a)),
+            pl.BlockSpec((lay.rows, lay.share), lambda a: (0, a)),
+        ],
+        out_specs=pl.BlockSpec((1, lay.rows, both), lambda a: (a, 0, 0)),
+        compiler_params=pltpu.CompilerParams(vmem_limit_bytes=VMEM_LIMIT),
+        cost_estimate=pl.CostEstimate(
+            flops=0, bytes_accessed=4 * lay.y * lay.rows * both, transcendentals=0
+        ),
+        interpret=INTERPRET,
+    )(valid_rows, inputs, cotangent)
+
+
+def pre_kernel(lay, index, w_ref, x_ref, out_ref):
+    lower = index[0] % 2
     maps = jnp.concatenate(
-        [jnp.concatenate([w_ref[b, lower], w_ref[b, upper]], axis=0) for b in range(lay.z)],
+        [jnp.concatenate([w_ref[b, lower], w_ref[b, 1 - lower]], axis=0) for b in range(lay.z)],
         axis=1,
     )
-    for k in range(lay.y):
-        out_ref[table[0, k]] = contract_last(x_refs[k][...], maps).astype(BF16)
+    for a in range(lay.y):
+        out_ref[a] = contract_last(x_ref[a, :, 0 : lay.span], maps).astype(BF16)
 
 
 def section_maps(lay, w_ref, which):
@@ -134,19 +143,14 @@
     )
 
 
-def pack_kernel(lay, table, w_ref, pre_ref, *refs):
-    c_refs, out_ref = refs[: lay.y], refs[lay.y]
+def pack_kernel(lay, index, w_ref, pre_ref, c_ref, out_ref):
     down, up = section_maps(lay, w_ref, 0), section_maps(lay, w_ref, 1)
     gram_at, pre_at = lay.ranks, lay.ranks + lay.gram
-    for i in range(lay.y):
-        block = table[0, lay.y + i]
-        part = contract_last(c_refs[i][...], up).astype(BF16)
+    for a in range(lay.y):
+        part = contract_last(c_ref[a], up).astype(BF16)
         for p in range(lay.pipe):
             rows = slice(p * lay.piece, (p + 1) * lay.piece)
-            out_ref[p * lay.y + block, :, 0:gram_at] = part[rows]
-    for a in range(lay.y):
-        for p in range(lay.pipe):
-            rows = slice(p * lay.piece, (p + 1) * lay.piece)
+            out_ref[p * lay.y + a, :, 0:gram_at] = part[rows]
             out_ref[p * lay.y + a, :, pre_at:] = pre_ref[a, rows, :]
     last = lay.tiles - 1
     each = lay.ranks // lay.group
@@ -165,7 +169,7 @@
             out_ref[t * (LANES // each) + q, :, gram_at:pre_at] = full[q * each : (q + 1) * each]
 
 
-def sum_kernel(lay, table, r_ref, out_ref):
+def sum_kernel(lay, index, r_ref, out_ref):
     gram_end = lay.ranks + lay.gram
     total = r_ref[0, :, 0:gram_end].astype(F32)
     for q in range(1, lay.group):
@@ -183,9 +187,8 @@
         out_ref[q] = message
 
 
-def chain_kernel(lay, table, q_ref, w_ref, *refs):
-    c_refs, x_refs = refs[: lay.y], refs[lay.y : 2 * lay.y]
-    out_ref, along, slope, acts, backs, gram, cots, held = refs[2 * lay.y :]
+def chain_kernel(lay, index, q_ref, w_ref, c_ref, x_ref, out_ref, *scratch):
+    along, slope, acts, backs, gram, held = scratch
     width_scale, rank_scale = 1.0 / math.sqrt(lay.width), 1.0 / math.sqrt(lay.rank)
     gram_at, pre_at = lay.ranks, lay.ranks + lay.gram
     each = lay.ranks // lay.group
@@ -198,8 +201,6 @@
         gate = 1.0 / (1.0 + jnp.exp(-pre))
         acts[rows, :] = (pre * gate).astype(BF16)
         slope[rows, :] = gate * (1.0 + pre * (1.0 - gate)) * rank_scale
-    for i in range(lay.y):
-        cots[table[0, lay.y + i]] = c_refs[i][...]
     tokens = lay.y * lay.rows
     last = lay.tiles - 1
     lower = lax.broadcasted_iota(jnp.int32, (tokens, LANES), 1) < lay.rank
@@ -230,7 +231,7 @@
     before = lax.broadcasted_iota(jnp.int32, cross.shape, 0) // lay.rank
     after = lax.broadcasted_iota(jnp.int32, cross.shape, 1) // lay.rank
     cross = jnp.where(before < after, cross * width_scale, 0.0).astype(BF16)
-    cot_all = cots[...].reshape(tokens, lay.share)
+    cot_all = c_ref[...].reshape(tokens, lay.share)
     grad_up = contract_first(acted, cot_all) + jnp.dot(
         cross, section_maps(lay, w_ref, 0), preferred_element_type=F32
     )
@@ -240,11 +241,11 @@
             out_ref[s * lay.per + j, lay.rank :, :] = grad_up[
                 s * lay.rank : (s + 1) * lay.rank, j * LANES : (j + 1) * LANES
             ]
-    mine, odd = table[0, 2 * lay.y], table[0, 2 * lay.y + 1]
+    mine, odd = index[0] // 2, index[0] % 2
     total = None
-    for k in range(lay.y):
-        start = pl.multiple_of(table[0, k] * lay.rows, lay.rows)
-        part = contract_first(backs[mine, pl.ds(start, lay.rows), :], x_refs[k][...])
+    for a in range(lay.y):
+        rows = slice(a * lay.rows, (a + 1) * lay.rows)
+        part = contract_first(backs[mine, rows, :], x_ref[a, :, 0 : lay.span])
         total = part if total is None else total + part
     held[...] = (total * width_scale).reshape(2, lay.rank, lay.span)
     grad_down = held[odd].astype(BF16)
@@ -257,22 +258,11 @@
     inputs, weights = saved_inputs[0], weights_bf16[0]
     lay = Layout(pipe, dp, inputs.shape[0], inputs.shape[1], weights.shape[1])
     both = ("pipe", "dp")
-    p_index, d_index = lax.axis_index("pipe"), lax.axis_index("dp")
-    y_index = d_index // lay.z
-    table = lax.dynamic_slice(jnp.asarray(lay.table()), (p_index * dp + d_index, 0), (1, 16))
-
-    x_pieces = []
-    for k in range(lay.y):
-        start = (y_index + k) % lay.y * lay.span
-        piece = lax.dynamic_slice(inputs, (0, start), (lay.rows, lay.span))
-        x_pieces.append(lax.ppermute(piece, "dp", lay.turn_y(k)) if k else piece)
-    live_rows = jnp.arange(lay.rows, dtype=jnp.int32) < valid_rows[0]
-    loss_grad = jnp.where(live_rows[:, None], cotangent, jnp.zeros_like(cotangent))
-    c_pieces = []
-    for i in range(lay.y):
-        start = (y_index + i) % lay.y * lay.share
-        piece = lax.dynamic_slice(loss_grad, (0, start), (lay.rows, lay.share))
-        c_pieces.append(lax.ppermute(piece, both, lay.cotangent_turn(i)))
+    index = lax.axis_index("pipe").astype(jnp.int32).reshape(1)
+
+    by_column = sort_columns(lay, valid_rows, inputs, cotangent)
+    by_column = lax.all_to_all(by_column, "dp", 0, 0, axis_index_groups=lay.along_y)
+    cots = lax.ppermute(by_column[:, :, lay.span :], both, lay.cotangent_turn())
 
     maps = lax.all_gather(weights, "dp", axis_index_groups=lay.along_z)
     shared = lax.all_to_all(
@@ -281,14 +271,14 @@
     pre_part = call(
         functools.partial(pre_kernel, lay),
         jax.ShapeDtypeStruct((lay.y, lay.rows, LANES), BF16),
-        (table, maps, *x_pieces),
+        (index, maps, by_column),
         flops=2 * lay.y * lay.rows * lay.span * LANES,
     )
     message = lay.ranks + lay.gram + LANES
     parts = call(
         functools.partial(pack_kernel, lay),
         jax.ShapeDtypeStruct((lay.group, lay.piece, message), BF16),
-        (table, shared, pre_part, *c_pieces),
+        (index, shared, pre_part, cots),
         flops=4 * lay.y * lay.rows * lay.share * lay.ranks,
     )
     parts = lax.all_to_all(parts, both, 0, 0, axis_index_groups=lay.plane)
@@ -296,21 +286,20 @@
     sums = call(
         functools.partial(sum_kernel, lay),
         jax.ShapeDtypeStruct((lay.group, lay.piece, reply), BF16),
-        (table, parts),
+        (index, parts),
     )
     sums = lax.all_to_all(sums, both, 0, 0, axis_index_groups=lay.plane)
     tokens = lay.y * lay.rows
     grads = call(
         functools.partial(chain_kernel, lay),
         jax.ShapeDtypeStruct((lay.z, 2 * lay.rank, LANES), BF16),
-        (table, sums, shared, *c_pieces, *x_pieces),
+        (index, sums, shared, cots, by_column),
         scratch=(
             pltpu.VMEM((tokens, lay.ranks), F32),
             pltpu.VMEM((tokens, lay.ranks), F32),
             pltpu.VMEM((tokens, lay.ranks), BF16),
             pltpu.VMEM((lay.tiles, tokens, LANES), BF16),
             pltpu.VMEM((lay.ranks, lay.gram), BF16),
-            pltpu.VMEM((lay.y, lay.rows, lay.share), BF16),
             pltpu.VMEM((2, lay.rank, lay.span), F32),
         ),
         flops=8 * tokens * lay.ranks * lay.share,

time: 206 us -> 195 us (0.947)
  starting transfers between devices: 51.7 us -> 32.4 us
  blocking collectives: 130 us -> 137 us
  waiting for transfers between devices: 6.47 us -> 9.1 us
    ppermute x7 -> x1, starting transfers between devices: 28.7 us -> 5.05 us  [body(): cots = lax.ppermute(by_column[:, :, lay.span:], both, lay.cotangent_turn())]
    all_to_all x1, blocking collectives: 23.3 us -> 28.7 us  [body(): parts = lax.all_to_all(parts, both, 0, 0, axis_index_groups=lay.plane)]
    all_to_all x0 -> x1, starting transfers between devices: none -> 5.14 us  [body(): lax.all_to_all(by_column, 'dp', 0, 0, axis_index_groups=lay.along_y)]
    dynamic_slice x3 -> x0, local copies, waits for them, and re-layouts: 4.16 us -> none  [the longest x1 2.75 us: body(): piece = lax.dynamic_slice(inputs, (0, start), (lay.rows, lay.span))]
    unnamed x10 -> x14, local copies, waits for them, and re-layouts: 0.03 us -> 3.96 us
    all_to_all x1, waiting for transfers between devices: 0.01 us -> 2.65 us  [body(): lax.all_to_all(maps.reshape(pipe, lay.per, 2, lay.rank, LANES), 'pipe', 0...]
  transfers between devices with their start and end apart: 10 -> 5, of which waited for: 1 -> 2; matrix products, arithmetic and copies ran while one was open for 1% -> 0% of each run, Pallas kernels for 1% -> 1%
where the time goes in v2:
time: 195 us; the launch traced here: 192 us
  blocking collectives  137 us (70%)
  starting transfers between devices  32.4 us (17%)
  waiting for transfers between devices  9.1 us (5%)
  Pallas kernels  5.97 us (3%)
  local copies, waits for them, and re-layouts  4.64 us (2%)
  between operations  2.13 us (1%)
    all_gather x1, blocking collectives, body(): maps = lax.all_gather(weights, 'dp', axis_index_groups=lay.along_z)  34.6 us
    all_to_all x1, blocking collectives, body(): grads = lax.all_to_all(grads, 'dp', 0, 0, axis_index_groups=lay.along_z)  29.6 us
    all_to_all x1, blocking collectives, body(): parts = lax.all_to_all(parts, both, 0, 0, axis_index_groups=lay.plane)  28.7 us
    all_to_all x1, blocking collectives, body(): sums = lax.all_to_all(sums, both, 0, 0, axis_index_groups=lay.plane)  25.6 us
    all_to_all x1, blocking collectives, body(): squares = lax.all_to_all(squares, both, 0, 0, axis_index_groups=lay.plane)  17.9 us
    all_to_all x1, starting transfers between devices, body(): lax.all_to_all(maps.reshape(pipe, lay.per, 2, lay.rank, LANES), 'pipe', 0...  11.1 us
    all_to_all x1, waiting for transfers between devices, body(): squares = lax.all_to_all(squares, 'dp', 0, 0, axis_index_groups=lay.along_z)  6.44 us
    all_to_all x1, starting transfers between devices, body(): squares = lax.all_to_all(squares, 'dp', 0, 0, axis_index_groups=lay.along_z)  6 us
  transfers between devices with their start and end apart: 5, of which 2 were waited for; matrix products, arithmetic and copies ran while one was open for 0% of the time, Pallas kernels for 1%

profile of v2, /device:TPU:1, one launch (start us, length us, event | category | flops | bytes accessed | tf_op | source)
XLA Modules:
  0.0 192.2 jit_solution(16844113536329581408)
XLA Ops:
  1.3 0.0 copy-start.1
  1.3 1.6 copy-done.1
  2.9 0.0 copy-start.2
  2.9 0.9 copy-done.2
  3.8 0.4 shard_map.102
  4.3 0.0 copy-start
  4.3 1.4 copy-done
  5.7 0.0 copy-start.6
  5.7 5.1 %all-to-all-start.1 = ((bf16[4,128,2304]{2,1,0:T(8,128)(2,1)}), bf16[4,128,2304]{2,1,0:T(8,128)(2,1)S(1)}, u32[]{:S(2)}, u32[]{:S(2)}) async-start(bf16[4,128,2304]{2,1,0:T(8,128)(2,1)} %copy-done), calls=%async_computation.1 | async-start | bytes 4718592 | tf_op jit(solution)/shard_map/all_to_all | solution.py:264
  10.8 0.0 copy-done.6
  10.8 34.6 %all_gather.3.w_ref = bf16[16,2,64,128]{3,2,1,0:T(8,128)(2,1)} all-gather(bf16[1,2,64,128]{3,2,1,0:T(8,128)(2,1)S(1)} %copy-done.6), channel_id=1, replica_groups={{0,1,2,3,4,5,6,7,8,9,10,11,12,13,14,15},{16,17,18,19,20,21,22,23,24,25,..., dimensions={0}, use_global_device_ids=true | all-gather | bytes 557056 | tf_op jit(solution)/shard_map/all_gather | solution.py:267
  45.5 0.0 all-to-all-done.1.x_ref
  45.5 11.1 %all-to-all-start = ((bf16[8,2,2,64,128]{4,3,2,1,0:T(8,128)(2,1)}), bf16[8,2,2,64,128]{4,3,2,1,0:T(8,128)(2,1)S(1)}, u32[]{:S(2)}, u32[]{:S(2)}) async-start(bf16[8,2,2,64,128]{4,3,2,1,0:T(8,128)(2,1)} %bitcast.1), calls=%async_computation | async-start | bytes 1048576 | tf_op jit(solution)/shard_map/all_to_all | solution.py:268
  56.6 5.0 %collective-permute-start = (bf16[4,128,256]{2,1,0:T(8,128)(2,1)S(1)}, bf16[4,128,256]{2,1,0:T(8,128)(2,1)S(1)}, u32[]{:S(2)}, u32[]{:S(2)}) collective-permute-start(bf16[4,128,256]{2,1,0:T(8,128)(2,1)S(1)} %slice.12), channel_id=1, source_target_pairs={{0,0},{1,1},{2,2},{3,3},{4,4},{5,5},{6,6},{7,7},{8,8},{9,9},{10,10... | collective-permute-start | bytes 786440 | tf_op jit(solution)/shard_map/ppermute | solution.py:265
  61.7 1.7 shard_map.103.pre_ref
  63.4 2.6 %all-to-all-done.w_ref = bf16[8,2,2,64,128]{4,3,2,1,0:T(8,128)(2,1)S(1)} async-done(((bf16[8,2,2,64,128]{4,3,2,1,0:T(8,128)(2,1)}), bf16[8,2,2,64,128]{4,3,2,1,0:T(8,128)(2,1)S(1)}, u32[]{:S(2)}, u32[]{:S(2)}) %all-to-all-start) | async-done | bytes 524320 | tf_op jit(solution)/shard_map/all_to_all | solution.py:268
  66.1 0.0 collective-permute-done.c_ref
  66.1 0.7 shard_map.104
  66.8 28.7 %all_to_all.35.r_ref = bf16[32,16,1024]{2,1,0:T(8,128)(2,1)S(1)} all-to-all(bf16[32,16,1024]{2,1,0:T(8,128)(2,1)S(1)} %shard_map.104), channel_id=1, replica_groups={{0,16,32,48,64,80,96,112,128,144,160,176,192,208,224,240,256,272,288,30..., dimensions={0} | all-to-all | bytes 2097152 | tf_op jit(solution)/shard_map/all_to_all | solution.py:284
  95.5 0.2 shard_map.105
  95.7 25.6 %all_to_all.36.q_ref = bf16[32,16,1408]{2,1,0:T(8,128)(2,1)S(1)} all-to-all(bf16[32,16,1408]{2,1,0:T(8,128)(2,1)S(1)} %shard_map.105), channel_id=1, replica_groups={{0,16,32,48,64,80,96,112,128,144,160,176,192,208,224,240,256,272,288,30..., dimensions={0} | all-to-all | bytes 2883584 | tf_op jit(solution)/shard_map/all_to_all | solution.py:291
  121.3 2.9 %shard_map.106 = bf16[16,128,128]{2,1,0:T(8,128)(2,1)S(1)} custom-call(s32[1]{0:T(128)} %bitcast.index, bf16[32,16,1408]{2,1,0:T(8,128)(2,1)S(1)} %all_to_all.36.q_ref, bf16[8,2,2,64,128]{4,3,2,1,0:T(8,128)(2,1)S(1)} %all-to-all-done.w_ref, bf16[4,128,256]{2,1,0:T(8,128)(2,1)S(1)} %collective-permute-done.c_ref, bf16[4,128,2304]{2,1,0:T(8,128)(2,1)S(1)} %all-to-all-done.1.x_ref), custom_call_target="tpu_custom_call" | custom-call | flops 536870912 | bytes 5111812 | tf_op jit(solution)/shard_map/pallas_call | solution.py:41
  124.3 0.0 copy-start.3
  124.3 0.0 copy-start.4
  124.3 0.0 copy-start.5
  124.3 29.6 %all_to_all.37 = bf16[16,128,128]{2,1,0:T(8,128)(2,1)S(1)} all-to-all(bf16[16,128,128]{2,1,0:T(8,128)(2,1)S(1)} %shard_map.106), channel_id=1, replica_groups={{0,1,2,3,4,5,6,7,8,9,10,11,12,13,14,15},{16,17,18,19,20,21,22,23,24,25,..., dimensions={0} | all-to-all | bytes 1048576 | tf_op jit(solution)/shard_map/all_to_all | solution.py:307
  153.9 0.1 convert_reduce_fusion
  154.0 17.9 %all_to_all.38 = f32[32,8,128]{2,1,0:T(8,128)S(1)} all-to-all(f32[32,8,128]{2,1,0:T(8,128)S(1)} %broadcast_in_dim.4), channel_id=1, replica_groups={{0,16,32,48,64,80,96,112,128,144,160,176,192,208,224,240,256,272,288,30..., dimensions={0} | all-to-all | bytes 262144 | tf_op jit(solution)/shard_map/all_to_all | solution.py:312
  172.0 0.6 broadcast_in_dim.5
  172.6 6.0 %all-to-all-start.6 = ((f32[16,8,128]{2,1,0:T(8,128)}), f32[16,8,128]{2,1,0:T(8,128)S(1)}, u32[]{:S(2)}, u32[]{:S(2)}) async-start(f32[16,8,128]{2,1,0:T(8,128)} %broadcast_in_dim.5), calls=%async_computation.6 | async-start | bytes 131072 | tf_op jit(solution)/shard_map/all_to_all | solution.py:314
  178.6 5.1 %collective-permute-start.1 = (f32[64,128]{1,0:T(8,128)S(1)}, f32[64,128]{1,0:T(8,128)S(1)}, u32[]{:S(2)}, u32[]{:S(2)}) collective-permute-start(f32[64,128]{1,0:T(8,128)S(1)} %get-tuple-element.9), channel_id=1, source_target_pairs={{0,0},{1,1},{2,64},{3,65},{4,128},{5,129},{6,192},{7,193},{8,256},... | collective-permute-start | bytes 98312 | tf_op jit(solution)/shard_map/ppermute | solution.py:310
  183.7 6.4 %all-to-all-done.6 = f32[16,8,128]{2,1,0:T(8,128)S(1)} async-done(((f32[16,8,128]{2,1,0:T(8,128)}), f32[16,8,128]{2,1,0:T(8,128)S(1)}, u32[]{:S(2)}, u32[]{:S(2)}) %all-to-all-start.6) | async-done | bytes 65568 | tf_op jit(solution)/shard_map/all_to_all | solution.py:314
  190.2 0.6 reduce_sum.39
  191.5 0.0 collective-permute-done.1
  191.5 0.0 copy-done.3
  191.5 0.0 copy-done.4
  191.5 0.0 copy-done.5
  191.5 0.7 fusion.1
  (5 shorter events, 0.1 us)
Async XLA Ops:
  1.3 1.6 copy-start.1
  2.9 0.9 copy-start.2
  4.3 1.4 copy-start
  5.7 5.1 %copy-start.6 = (bf16[1,2,64,128]{3,2,1,0:T(8,128)(2,1)S(1)}, bf16[1,2,64,128]{3,2,1,0:T(8,128)(2,1)}, u32[]{:S(2)}) copy-start(bf16[1,2,64,128]{3,2,1,0:T(8,128)(2,1)} %param.9) | copy-start | bytes 98308
  5.7 39.8 %all-to-all-start.1 = ((bf16[4,128,2304]{2,1,0:T(8,128)(2,1)}), bf16[4,128,2304]{2,1,0:T(8,128)(2,1)S(1)}, u32[]{:S(2)}, u32[]{:S(2)}) async-start(bf16[4,128,2304]{2,1,0:T(8,128)(2,1)} %copy-done), calls=%async_computation.1 | async-start | bytes 4718592 | tf_op jit(solution)/shard_map/all_to_all | solution.py:264
  45.5 20.6 %all-to-all-start = ((bf16[8,2,2,64,128]{4,3,2,1,0:T(8,128)(2,1)}), bf16[8,2,2,64,128]{4,3,2,1,0:T(8,128)(2,1)S(1)}, u32[]{:S(2)}, u32[]{:S(2)}) async-start(bf16[8,2,2,64,128]{4,3,2,1,0:T(8,128)(2,1)} %bitcast.1), calls=%async_computation | async-start | bytes 1048576 | tf_op jit(solution)/shard_map/all_to_all | solution.py:268
  56.6 9.5 %collective-permute-start = (bf16[4,128,256]{2,1,0:T(8,128)(2,1)S(1)}, bf16[4,128,256]{2,1,0:T(8,128)(2,1)S(1)}, u32[]{:S(2)}, u32[]{:S(2)}) collective-permute-start(bf16[4,128,256]{2,1,0:T(8,128)(2,1)S(1)} %slice.12), channel_id=1, source_target_pairs={{0,0},{1,1},{2,2},{3,3},{4,4},{5,5},{6,6},{7,7},{8,8},{9,9},{10,10... | collective-permute-start | bytes 786440 | tf_op jit(solution)/shard_map/ppermute | solution.py:265
  124.3 67.2 %copy-start.3 = (f32[1,2,64,128]{3,2,1,0:T(8,128)S(1)}, f32[1,2,64,128]{3,2,1,0:T(8,128)}, u32[]{:S(2)}) copy-start(f32[1,2,64,128]{3,2,1,0:T(8,128)} %param.10) | copy-start | bytes 196612
  124.3 67.2 %copy-start.4 = (f32[1,2,64,128]{3,2,1,0:T(8,128)S(1)}, f32[1,2,64,128]{3,2,1,0:T(8,128)}, u32[]{:S(2)}) copy-start(f32[1,2,64,128]{3,2,1,0:T(8,128)} %param.12) | copy-start | bytes 196612
  124.3 67.2 %copy-start.5 = (f32[1,2,64,128]{3,2,1,0:T(8,128)S(1)}, f32[1,2,64,128]{3,2,1,0:T(8,128)}, u32[]{:S(2)}) copy-start(f32[1,2,64,128]{3,2,1,0:T(8,128)} %param.11) | copy-start | bytes 196612
  172.6 17.6 %all-to-all-start.6 = ((f32[16,8,128]{2,1,0:T(8,128)}), f32[16,8,128]{2,1,0:T(8,128)S(1)}, u32[]{:S(2)}, u32[]{:S(2)}) async-start(f32[16,8,128]{2,1,0:T(8,128)} %broadcast_in_dim.5), calls=%async_computation.6 | async-start | bytes 131072 | tf_op jit(solution)/shard_map/all_to_all | solution.py:314
  178.6 12.9 %collective-permute-start.1 = (f32[64,128]{1,0:T(8,128)S(1)}, f32[64,128]{1,0:T(8,128)S(1)}, u32[]{:S(2)}, u32[]{:S(2)}) collective-permute-start(f32[64,128]{1,0:T(8,128)S(1)} %get-tuple-element.9), channel_id=1, source_target_pairs={{0,0},{1,1},{2,64},{3,65},{4,128},{5,129},{6,192},{7,193},{8,256},... | collective-permute-start | bytes 98312 | tf_op jit(solution)/shard_map/ppermute | solution.py:310

commit v3 on v1

--- a/solution.py
+++ b/solution.py
@@ -258,23 +258,25 @@
     lay = Layout(pipe, dp, inputs.shape[0], inputs.shape[1], weights.shape[1])
     both = ("pipe", "dp")
     p_index, d_index = lax.axis_index("pipe"), lax.axis_index("dp")
-    y_index = d_index // lay.z
+    y_index = lax.div(d_index, lay.z)
     table = lax.dynamic_slice(jnp.asarray(lay.table()), (p_index * dp + d_index, 0), (1, 16))
 
     x_pieces = []
     for k in range(lay.y):
-        start = (y_index + k) % lay.y * lay.span
+        start = lax.rem(y_index + k, lay.y) * lay.span
         piece = lax.dynamic_slice(inputs, (0, start), (lay.rows, lay.span))
         x_pieces.append(lax.ppermute(piece, "dp", lay.turn_y(k)) if k else piece)
     live_rows = jnp.arange(lay.rows, dtype=jnp.int32) < valid_rows[0]
     loss_grad = jnp.where(live_rows[:, None], cotangent, jnp.zeros_like(cotangent))
     c_pieces = []
     for i in range(lay.y):
-        start = (y_index + i) % lay.y * lay.share
+        start = lax.rem(y_index + i, lay.y) * lay.share
         piece = lax.dynamic_slice(loss_grad, (0, start), (lay.rows, lay.share))
         c_pieces.append(lax.ppermute(piece, both, lay.cotangent_turn(i)))
 
-    maps = lax.all_gather(weights, "dp", axis_index_groups=lay.along_z)
+    maps = jnp.broadcast_to(weights, (lay.z, *weights.shape))
+    maps = lax.all_to_all(maps, "dp", 0, 0, axis_index_groups=lay.along_z)
+    maps, *c_pieces = lax.optimization_barrier((maps, *c_pieces))
     shared = lax.all_to_all(
         maps.reshape(pipe, lay.per, 2, lay.rank, LANES), "pipe", 0, 0
     )

time: 206 us -> 204 us (level)
  blocking collectives: 130 us -> 101 us
  waiting for transfers between devices: 6.47 us -> 22.4 us
  starting transfers between devices: 51.7 us -> 62.1 us
    all_gather x1 -> x0, blocking collectives: 33.8 us -> none  [body(): maps = lax.all_gather(weights, 'dp', axis_index_groups=lay.along_z)]
    all_to_all x0 -> x1, starting transfers between devices: none -> 15.8 us  [body(): maps = lax.all_to_all(maps, 'dp', 0, 0, axis_index_groups=lay.along_z)]
    ppermute x4, waiting for transfers between devices: 0.01 us -> 8.94 us  [body(): c_pieces.append(lax.ppermute(piece, both, lay.cotangent_turn(i)))]
    all_to_all x1, waiting for transfers between devices: 0.01 us -> 7 us  [body(): lax.all_to_all(maps.reshape(pipe, lay.per, 2, lay.rank, LANES), 'pipe', 0...]
    all_to_all x1, blocking collectives: 29.4 us -> 34.2 us  [body(): grads = lax.all_to_all(grads, 'dp', 0, 0, axis_index_groups=lay.along_z)]
    all_to_all x1, starting transfers between devices: 11.9 us -> 7.25 us  [body(): lax.all_to_all(maps.reshape(pipe, lay.per, 2, lay.rank, LANES), 'pipe', 0...]
    ppermute x3, starting transfers between devices: 11.5 us -> 9.44 us  [body(): x_pieces.append(lax.ppermute(piece, 'dp', lay.turn_y(k)) if k else piece)]
  transfers between devices with their start and end apart: 10 -> 11, of which waited for: 1 -> 3; matrix products, arithmetic and copies ran while one was open for 1% -> 2% of each run, Pallas kernels for 1% -> 1%
where the time goes in v3:
time: 204 us; the launch traced here: 202 us
  blocking collectives  101 us (50%)
  starting transfers between devices  62.1 us (30%)
  waiting for transfers between devices  22.4 us (11%)
  Pallas kernels  7.14 us (4%)
  local copies, waits for them, and re-layouts  4.45 us (2%)
  other arithmetic  2.49 us (1%)
  between operations  2.32 us (1%)
    all_to_all x1, blocking collectives, body(): grads = lax.all_to_all(grads, 'dp', 0, 0, axis_index_groups=lay.along_z)  34.2 us
    all_to_all x1, blocking collectives, body(): sums = lax.all_to_all(sums, both, 0, 0, axis_index_groups=lay.plane)  25.6 us
    all_to_all x1, blocking collectives, body(): parts = lax.all_to_all(parts, both, 0, 0, axis_index_groups=lay.plane)  23.3 us
    ppermute x4, starting transfers between devices, body(): c_pieces.append(lax.ppermute(piece, both, lay.cotangent_turn(i)))  18.5 us
    all_to_all x1, blocking collectives, body(): squares = lax.all_to_all(squares, both, 0, 0, axis_index_groups=lay.plane)  17.8 us
    all_to_all x1, starting transfers between devices, body(): maps = lax.all_to_all(maps, 'dp', 0, 0, axis_index_groups=lay.along_z)  15.8 us
    ppermute x3, starting transfers between devices, body(): x_pieces.append(lax.ppermute(piece, 'dp', lay.turn_y(k)) if k else piece)  9.44 us
    ppermute x4, waiting for transfers between devices, body(): c_pieces.append(lax.ppermute(piece, both, lay.cotangent_turn(i)))  8.94 us
  transfers between devices with their start and end apart: 11, of which 3 were waited for; matrix products, arithmetic and copies ran while one was open for 2% of the time, Pallas kernels for 1%

profile of v3, /device:TPU:1, one launch (start us, length us, event | category | flops | bytes accessed | tf_op | source)
XLA Modules:
  0.0 201.9 jit_solution(13655635835895348547)
XLA Ops:
  0.6 0.0 copy-start
  0.6 1.8 broadcast_in_dim.25
  2.4 15.8 %all-to-all-start = ((bf16[16,2,64,128]{3,2,1,0:T(8,128)(2,1)}), bf16[16,2,64,128]{3,2,1,0:T(8,128)(2,1)}, u32[]{:S(2)}, u32[]{:S(2)}) async-start(bf16[16,2,64,128]{3,2,1,0:T(8,128)(2,1)} %broadcast_in_dim.25), calls=%async_computation | async-start | bytes 1048576 | tf_op jit(solution)/shard_map/all_to_all | solution.py:278
  19.0 1.0 broadcast_select_fusion
  20.1 4.4 %collective-permute-start.3 = (bf16[128,256]{1,0:T(8,128)(2,1)S(1)}, bf16[128,256]{1,0:T(8,128)(2,1)S(1)}, u32[]{:S(2)}, u32[]{:S(2)}) collective-permute-start(bf16[128,256]{1,0:T(8,128)(2,1)S(1)} %get-tuple-element.22), channel_id=1, source_target_pairs={{0,192},{1,193},{2,194},{3,195},{4,196},{5,197},{6,198},{7,199},{8... | collective-permute-start | bytes 196616 | tf_op jit(solution)/shard_map/ppermute | solution.py:275
  24.5 5.8 %collective-permute-start.2 = (bf16[128,256]{1,0:T(8,128)(2,1)S(1)}, bf16[128,256]{1,0:T(8,128)(2,1)S(1)}, u32[]{:S(2)}, u32[]{:S(2)}) collective-permute-start(bf16[128,256]{1,0:T(8,128)(2,1)S(1)} %get-tuple-element.23), channel_id=1, source_target_pairs={{0,128},{1,129},{2,130},{3,131},{4,132},{5,133},{6,134},{7,135},{8... | collective-permute-start | bytes 196616 | tf_op jit(solution)/shard_map/ppermute | solution.py:275
  30.3 0.0 copy-done
  30.3 1.2 dynamic-slice_bitcast_fusion
  31.5 4.2 %collective-permute-start.6 = (bf16[128,2048]{1,0:T(8,128)(2,1)}, bf16[128,2048]{1,0:T(8,128)(2,1)S(1)}, u32[]{:S(2)}, u32[]{:S(2)}) collective-permute-start(bf16[128,2048]{1,0:T(8,128)(2,1)} %get-tuple-element.18), channel_id=1, source_target_pairs={{0,48},{1,49},{2,50},{3,51},{4,52},{5,53},{6,54},{7,55},{8,56},{9,... | collective-permute-start | bytes 1572872 | tf_op jit(solution)/shard_map/ppermute | solution.py:268
  35.8 1.9 collective-permute-start.4
  37.7 3.3 %collective-permute-start.5 = (bf16[128,2048]{1,0:T(8,128)(2,1)S(1)}, bf16[128,2048]{1,0:T(8,128)(2,1)S(1)}, u32[]{:S(2)}, u32[]{:S(2)}) collective-permute-start(bf16[128,2048]{1,0:T(8,128)(2,1)S(1)} %get-tuple-element.21), channel_id=1, source_target_pairs={{0,32},{1,33},{2,34},{3,35},{4,36},{5,37},{6,38},{7,39},{8,40},{9,... | collective-permute-start | bytes 1572872 | tf_op jit(solution)/shard_map/ppermute | solution.py:268
  41.0 0.0 collective-permute-done.3.refs_3_
  41.0 1.9 collective-permute-start.1
  42.9 0.0 collective-permute-done.2.refs_2_
  42.9 6.5 %collective-permute-start = (bf16[128,256]{1,0:T(8,128)(2,1)S(1)}, bf16[128,256]{1,0:T(8,128)(2,1)S(1)}, u32[]{:S(2)}, u32[]{:S(2)}) collective-permute-start(bf16[128,256]{1,0:T(8,128)(2,1)S(1)} %get-tuple-element.25), channel_id=1, source_target_pairs={{0,0},{1,1},{2,2},{3,3},{4,4},{5,5},{6,6},{7,7},{8,8},{9,9},{10,10... | collective-permute-start | bytes 196616 | tf_op jit(solution)/shard_map/ppermute | solution.py:275
  49.4 0.0 collective-permute-done.1.refs_1_
  49.4 8.9 %collective-permute-done.refs_0_ = bf16[128,256]{1,0:T(8,128)(2,1)S(1)} collective-permute-done((bf16[128,256]{1,0:T(8,128)(2,1)S(1)}, bf16[128,256]{1,0:T(8,128)(2,1)S(1)}, u32[]{:S(2)}, u32[]{:S(2)}) %collective-permute-start) | collective-permute-done | bytes 65568 | tf_op jit(solution)/shard_map/ppermute | solution.py:275
  58.3 0.0 all-to-all-done.w_ref
  58.3 7.3 %all-to-all-start.1 = ((bf16[8,2,2,64,128]{4,3,2,1,0:T(8,128)(2,1)}), bf16[8,2,2,64,128]{4,3,2,1,0:T(8,128)(2,1)S(1)}, u32[]{:S(2)}, u32[]{:S(2)}) async-start(bf16[8,2,2,64,128]{4,3,2,1,0:T(8,128)(2,1)} %bitcast.2), calls=%async_computation.1 | async-start | bytes 1048576 | tf_op jit(solution)/shard_map/all_to_all | solution.py:280
  65.6 0.7 constant_dynamic-slice_fusion.4.table
  66.3 0.0 collective-permute-done.6.refs_3_.refs_7_
  66.3 0.0 collective-permute-done.4.refs_1_.refs_5_
  66.3 0.0 collective-permute-done.5.refs_2_.refs_6_
  66.3 1.8 shard_map.111.pre_ref
  68.1 7.0 %all-to-all-done.1.w_ref = bf16[8,2,2,64,128]{4,3,2,1,0:T(8,128)(2,1)S(1)} async-done(((bf16[8,2,2,64,128]{4,3,2,1,0:T(8,128)(2,1)}), bf16[8,2,2,64,128]{4,3,2,1,0:T(8,128)(2,1)S(1)}, u32[]{:S(2)}, u32[]{:S(2)}) %all-to-all-start.1) | async-done | bytes 524320 | tf_op jit(solution)/shard_map/all_to_all | solution.py:280
  75.1 1.3 shard_map.112
  76.3 23.3 %all_to_all.35.r_ref = bf16[32,16,1024]{2,1,0:T(8,128)(2,1)S(1)} all-to-all(bf16[32,16,1024]{2,1,0:T(8,128)(2,1)S(1)} %shard_map.112), channel_id=1, replica_groups={{0,16,32,48,64,80,96,112,128,144,160,176,192,208,224,240,256,272,288,30..., dimensions={0} | all-to-all | bytes 2097152 | tf_op jit(solution)/shard_map/all_to_all | solution.py:296
  99.6 0.7 shard_map.113
  100.4 25.6 %all_to_all.36.q_ref = bf16[32,16,1408]{2,1,0:T(8,128)(2,1)S(1)} all-to-all(bf16[32,16,1408]{2,1,0:T(8,128)(2,1)S(1)} %shard_map.113), channel_id=1, replica_groups={{0,16,32,48,64,80,96,112,128,144,160,176,192,208,224,240,256,272,288,30..., dimensions={0} | all-to-all | bytes 2883584 | tf_op jit(solution)/shard_map/all_to_all | solution.py:303
  126.0 3.4 %shard_map.114 = bf16[16,128,128]{2,1,0:T(8,128)(2,1)S(1)} custom-call(s32[1,16]{1,0:T(1,128)S(1)} %constant_dynamic-slice_fusion.4.table, bf16[32,16,1408]{2,1,0:T(8,128)(2,1)S(1)} %all_to_all.36.q_ref, bf16[8,2,2,64,128]{4,3,2,1,0:T(8,128)(2,1)S(1)} %all-to-all-done.1.w_ref, bf16[128,256]{1,0:T(8,128)(2,1)S(1)} %collective-permute-done.refs_0_, ...), custom_call_target="tpu_custom_call" | custom-call | flops 536870912 | bytes 4849728 | tf_op jit(solution)/shard_map/pallas_call | solution.py:42
  129.4 0.0 copy-start.1
  129.4 0.0 copy-start.2
  129.4 0.0 copy-start.3
  129.4 34.2 %all_to_all.37 = bf16[16,128,128]{2,1,0:T(8,128)(2,1)S(1)} all-to-all(bf16[16,128,128]{2,1,0:T(8,128)(2,1)S(1)} %shard_map.114), channel_id=1, replica_groups={{0,1,2,3,4,5,6,7,8,9,10,11,12,13,14,15},{16,17,18,19,20,21,22,23,24,25,..., dimensions={0} | all-to-all | bytes 1048576 | tf_op jit(solution)/shard_map/all_to_all | solution.py:320
  163.6 0.1 convert_reduce_fusion
  163.8 17.8 %all_to_all.38 = f32[32,8,128]{2,1,0:T(8,128)S(1)} all-to-all(f32[32,8,128]{2,1,0:T(8,128)S(1)} %broadcast_in_dim.28), channel_id=1, replica_groups={{0,16,32,48,64,80,96,112,128,144,160,176,192,208,224,240,256,272,288,30..., dimensions={0} | all-to-all | bytes 262144 | tf_op jit(solution)/shard_map/all_to_all | solution.py:325
  181.6 0.6 broadcast_in_dim.29
  182.2 6.0 %all-to-all-start.6 = ((f32[16,8,128]{2,1,0:T(8,128)}), f32[16,8,128]{2,1,0:T(8,128)S(1)}, u32[]{:S(2)}, u32[]{:S(2)}) async-start(f32[16,8,128]{2,1,0:T(8,128)} %broadcast_in_dim.29), calls=%async_computation.6 | async-start | bytes 131072 | tf_op jit(solution)/shard_map/all_to_all | solution.py:327
  188.3 5.1 %collective-permute-start.7 = (f32[64,128]{1,0:T(8,128)S(1)}, f32[64,128]{1,0:T(8,128)S(1)}, u32[]{:S(2)}, u32[]{:S(2)}) collective-permute-start(f32[64,128]{1,0:T(8,128)S(1)} %get-tuple-element.27), channel_id=1, source_target_pairs={{0,0},{1,1},{2,64},{3,65},{4,128},{5,129},{6,192},{7,193},{8,256},... | collective-permute-start | bytes 98312 | tf_op jit(solution)/shard_map/ppermute | solution.py:323
  193.4 6.4 %all-to-all-done.6 = f32[16,8,128]{2,1,0:T(8,128)S(1)} async-done(((f32[16,8,128]{2,1,0:T(8,128)}), f32[16,8,128]{2,1,0:T(8,128)S(1)}, u32[]{:S(2)}, u32[]{:S(2)}) %all-to-all-start.6) | async-done | bytes 65568 | tf_op jit(solution)/shard_map/all_to_all | solution.py:327
  199.8 0.6 reduce_sum.39
  201.1 0.0 collective-permute-done.7
  201.1 0.0 copy-done.1
  201.1 0.0 copy-done.2
  201.1 0.0 copy-done.3
  201.2 0.7 fusion.1
  (6 shorter events, 0.1 us)
Async XLA Ops:
  0.6 29.6 %copy-start = (bf16[1,128,8192]{2,1,0:T(8,128)(2,1)S(1)}, bf16[1,128,8192]{2,1,0:T(8,128)(2,1)}, u32[]{:S(2)}) copy-start(bf16[1,128,8192]{2,1,0:T(8,128)(2,1)} %param.8) | copy-start | bytes 6291460
  2.4 55.9 %all-to-all-start = ((bf16[16,2,64,128]{3,2,1,0:T(8,128)(2,1)}), bf16[16,2,64,128]{3,2,1,0:T(8,128)(2,1)}, u32[]{:S(2)}, u32[]{:S(2)}) async-start(bf16[16,2,64,128]{3,2,1,0:T(8,128)(2,1)} %broadcast_in_dim.25), calls=%async_computation | async-start | bytes 1048576 | tf_op jit(solution)/shard_map/all_to_all | solution.py:278
  20.1 20.9 %collective-permute-start.3 = (bf16[128,256]{1,0:T(8,128)(2,1)S(1)}, bf16[128,256]{1,0:T(8,128)(2,1)S(1)}, u32[]{:S(2)}, u32[]{:S(2)}) collective-permute-start(bf16[128,256]{1,0:T(8,128)(2,1)S(1)} %get-tuple-element.22), channel_id=1, source_target_pairs={{0,192},{1,193},{2,194},{3,195},{4,196},{5,197},{6,198},{7,199},{8... | collective-permute-start | bytes 196616 | tf_op jit(solution)/shard_map/ppermute | solution.py:275
  24.5 18.4 %collective-permute-start.2 = (bf16[128,256]{1,0:T(8,128)(2,1)S(1)}, bf16[128,256]{1,0:T(8,128)(2,1)S(1)}, u32[]{:S(2)}, u32[]{:S(2)}) collective-permute-start(bf16[128,256]{1,0:T(8,128)(2,1)S(1)} %get-tuple-element.23), channel_id=1, source_target_pairs={{0,128},{1,129},{2,130},{3,131},{4,132},{5,133},{6,134},{7,135},{8... | collective-permute-start | bytes 196616 | tf_op jit(solution)/shard_map/ppermute | solution.py:275
  31.5 34.8 %collective-permute-start.6 = (bf16[128,2048]{1,0:T(8,128)(2,1)}, bf16[128,2048]{1,0:T(8,128)(2,1)S(1)}, u32[]{:S(2)}, u32[]{:S(2)}) collective-permute-start(bf16[128,2048]{1,0:T(8,128)(2,1)} %get-tuple-element.18), channel_id=1, source_target_pairs={{0,48},{1,49},{2,50},{3,51},{4,52},{5,53},{6,54},{7,55},{8,56},{9,... | collective-permute-start | bytes 1572872 | tf_op jit(solution)/shard_map/ppermute | solution.py:268
  35.8 30.5 %collective-permute-start.4 = (bf16[128,2048]{1,0:T(8,128)(2,1)}, bf16[128,2048]{1,0:T(8,128)(2,1)S(1)}, u32[]{:S(2)}, u32[]{:S(2)}) collective-permute-start(bf16[128,2048]{1,0:T(8,128)(2,1)} %get-tuple-element.19), channel_id=1, source_target_pairs={{0,16},{1,17},{2,18},{3,19},{4,20},{5,21},{6,22},{7,23},{8,24},{9,... | collective-permute-start | bytes 1572872 | tf_op jit(solution)/shard_map/ppermute | solution.py:268
  37.7 28.6 %collective-permute-start.5 = (bf16[128,2048]{1,0:T(8,128)(2,1)S(1)}, bf16[128,2048]{1,0:T(8,128)(2,1)S(1)}, u32[]{:S(2)}, u32[]{:S(2)}) collective-permute-start(bf16[128,2048]{1,0:T(8,128)(2,1)S(1)} %get-tuple-element.21), channel_id=1, source_target_pairs={{0,32},{1,33},{2,34},{3,35},{4,36},{5,37},{6,38},{7,39},{8,40},{9,... | collective-permute-start | bytes 1572872 | tf_op jit(solution)/shard_map/ppermute | solution.py:268
  41.0 8.4 %collective-permute-start.1 = (bf16[128,256]{1,0:T(8,128)(2,1)S(1)}, bf16[128,256]{1,0:T(8,128)(2,1)S(1)}, u32[]{:S(2)}, u32[]{:S(2)}) collective-permute-start(bf16[128,256]{1,0:T(8,128)(2,1)S(1)} %get-tuple-element.24), channel_id=1, source_target_pairs={{0,64},{1,65},{2,66},{3,67},{4,68},{5,69},{6,70},{7,71},{8,72},{9,... | collective-permute-start | bytes 196616 | tf_op jit(solution)/shard_map/ppermute | solution.py:275
  42.9 15.4 %collective-permute-start = (bf16[128,256]{1,0:T(8,128)(2,1)S(1)}, bf16[128,256]{1,0:T(8,128)(2,1)S(1)}, u32[]{:S(2)}, u32[]{:S(2)}) collective-permute-start(bf16[128,256]{1,0:T(8,128)(2,1)S(1)} %get-tuple-element.25), channel_id=1, source_target_pairs={{0,0},{1,1},{2,2},{3,3},{4,4},{5,5},{6,6},{7,7},{8,8},{9,9},{10,10... | collective-permute-start | bytes 196616 | tf_op jit(solution)/shard_map/ppermute | solution.py:275
  58.3 16.7 %all-to-all-start.1 = ((bf16[8,2,2,64,128]{4,3,2,1,0:T(8,128)(2,1)}), bf16[8,2,2,64,128]{4,3,2,1,0:T(8,128)(2,1)S(1)}, u32[]{:S(2)}, u32[]{:S(2)}) async-start(bf16[8,2,2,64,128]{4,3,2,1,0:T(8,128)(2,1)} %bitcast.2), calls=%async_computation.1 | async-start | bytes 1048576 | tf_op jit(solution)/shard_map/all_to_all | solution.py:280
  129.4 71.7 %copy-start.1 = (f32[1,2,64,128]{3,2,1,0:T(8,128)S(1)}, f32[1,2,64,128]{3,2,1,0:T(8,128)}, u32[]{:S(2)}) copy-start(f32[1,2,64,128]{3,2,1,0:T(8,128)} %param.11) | copy-start | bytes 196612
  129.4 71.7 %copy-start.2 = (f32[1,2,64,128]{3,2,1,0:T(8,128)S(1)}, f32[1,2,64,128]{3,2,1,0:T(8,128)}, u32[]{:S(2)}) copy-start(f32[1,2,64,128]{3,2,1,0:T(8,128)} %param.13) | copy-start | bytes 196612
  129.4 71.7 %copy-start.3 = (f32[1,2,64,128]{3,2,1,0:T(8,128)S(1)}, f32[1,2,64,128]{3,2,1,0:T(8,128)}, u32[]{:S(2)}) copy-start(f32[1,2,64,128]{3,2,1,0:T(8,128)} %param.12) | copy-start | bytes 196612
  182.2 17.6 %all-to-all-start.6 = ((f32[16,8,128]{2,1,0:T(8,128)}), f32[16,8,128]{2,1,0:T(8,128)S(1)}, u32[]{:S(2)}, u32[]{:S(2)}) async-start(f32[16,8,128]{2,1,0:T(8,128)} %broadcast_in_dim.29), calls=%async_computation.6 | async-start | bytes 131072 | tf_op jit(solution)/shard_map/all_to_all | solution.py:327
  188.3 12.9 %collective-permute-start.7 = (f32[64,128]{1,0:T(8,128)S(1)}, f32[64,128]{1,0:T(8,128)S(1)}, u32[]{:S(2)}, u32[]{:S(2)}) collective-permute-start(f32[64,128]{1,0:T(8,128)S(1)} %get-tuple-element.27), channel_id=1, source_target_pairs={{0,0},{1,1},{2,64},{3,65},{4,128},{5,129},{6,192},{7,193},{8,256},... | collective-permute-start | bytes 98312 | tf_op jit(solution)/shard_map/ppermute | solution.py:323

commit v4 on v2

--- a/solution.py
+++ b/solution.py
@@ -19,6 +19,8 @@
 LANES = 128
 Y_SIZE = 4
 VMEM_LIMIT = 48 * 1024 * 1024
+SORT_LIMIT = 63 * 1024 * 1024
+PRE_WEIGHT = 12
 INTERPRET = False
 BF16 = jnp.bfloat16
 F32 = jnp.float32
@@ -63,7 +65,11 @@
         self.piece = rows // pipe
         self.tiles = pipe * rank // LANES
         self.ranks = pipe * rank
-        self.gram = max(self.tiles - 1, 2) * LANES
+        self.gram = 2 * LANES
+        self.slots = {(a, b): (a, b) for a in range(1, self.tiles) for b in range(min(a, 2))}
+        spare = [(a, 1) for a in range(1, self.tiles) if (a, 1) not in self.slots]
+        rest = [(a, b) for a in range(1, self.tiles) for b in range(2, a)]
+        self.slots.update(zip(rest, spare))
         y, z = self.y, self.z
         self.along_z = [[a * z + b for b in range(z)] for a in range(y)]
         self.along_y = [[a * z + b for a in range(y)] for b in range(z)]
@@ -96,26 +102,50 @@
         ]
 
 
-def sort_kernel(lay, valid, x_ref, c_ref, out_ref):
-    out_ref[0, :, 0 : lay.span] = x_ref[...]
+def sort_kernel(lay, valid, x_ref, c_ref, out_ref, cots, sems):
+    copies = [
+        pltpu.make_async_copy(
+            x_ref.at[:, pl.ds(a * lay.span, lay.span)],
+            out_ref.at[a, :, pl.ds(0, lay.span)],
+            sems.at[a],
+        )
+        for a in range(lay.y)
+    ]
+    for copy in copies:
+        copy.start()
     cot = c_ref[...]
     live = lax.broadcasted_iota(jnp.int32, cot.shape, 0) < valid[0]
-    out_ref[0, :, lay.span :] = jnp.where(live, cot, jnp.zeros_like(cot))
+    cots[...] = jnp.where(live, cot, jnp.zeros_like(cot))
+    copies += [
+        pltpu.make_async_copy(
+            cots.at[:, pl.ds(a * lay.share, lay.share)],
+            out_ref.at[a, :, pl.ds(lay.span, lay.share)],
+            sems.at[lay.y + a],
+        )
+        for a in range(lay.y)
+    ]
+    for copy in copies[lay.y :]:
+        copy.start()
+    for copy in copies:
+        copy.wait()
 
 
 def sort_columns(lay, valid_rows, inputs, cotangent):
     both = lay.span + lay.share
     return pl.pallas_call(
         functools.partial(sort_kernel, lay),
-        grid=(lay.y,),
         out_shape=jax.ShapeDtypeStruct((lay.y, lay.rows, both), BF16),
         in_specs=[
             pl.BlockSpec(memory_space=pltpu.SMEM),
-            pl.BlockSpec((lay.rows, lay.span), lambda a: (0, a)),
-            pl.BlockSpec((lay.rows, lay.share), lambda a: (0, a)),
+            pl.BlockSpec(memory_space=pltpu.HBM),
+            pl.BlockSpec(memory_space=pltpu.VMEM),
         ],
-        out_specs=pl.BlockSpec((1, lay.rows, both), lambda a: (a, 0, 0)),
-        compiler_params=pltpu.CompilerParams(vmem_limit_bytes=VMEM_LIMIT),
+        out_specs=pl.BlockSpec(memory_space=pltpu.HBM),
+        scratch_shapes=[
+            pltpu.VMEM(cotangent.shape, BF16),
+            pltpu.SemaphoreType.DMA((2 * lay.y,)),
+        ],
+        compiler_params=pltpu.CompilerParams(vmem_limit_bytes=SORT_LIMIT),
         cost_estimate=pl.CostEstimate(
             flops=0, bytes_accessed=4 * lay.y * lay.rows * both, transcendentals=0
         ),
@@ -141,6 +171,25 @@
         ],
         axis=0,
     )
+
+
+def gram_tile(down, up, row, col):
+    rows, cols = slice(row * LANES, (row + 1) * LANES), slice(col * LANES, (col + 1) * LANES)
+    return contract_last(down[rows], up[cols]).astype(BF16)
+
+
+def diagonal_tile(lay, down, up):
+    rank = lay.rank
+    lower = lax.broadcasted_iota(jnp.int32, (rank, LANES), 1) < rank
+    blocks = []
+    for t in range(lay.tiles):
+        odd = down[t * LANES + rank : (t + 1) * LANES]
+        block = contract_last(odd, up[t * LANES : (t + 1) * LANES])
+        blocks.append(block if t % 2 == 0 else pltpu.roll(block, rank, 1))
+    halves = [jnp.where(lower, blocks[t], blocks[t + 1]) for t in range(0, lay.tiles, 2)]
+    if len(halves) == 1:
+        halves.append(halves[0])
+    return jnp.concatenate(halves[::-1], axis=0).astype(BF16)
 
 
 def pack_kernel(lay, index, w_ref, pre_ref, c_ref, out_ref):
@@ -152,21 +201,16 @@
             rows = slice(p * lay.piece, (p + 1) * lay.piece)
             out_ref[p * lay.y + a, :, 0:gram_at] = part[rows]
             out_ref[p * lay.y + a, :, pre_at:] = pre_ref[a, rows, :]
-    last = lay.tiles - 1
+    grams = {spot: gram_tile(down, up, *tile) for tile, spot in lay.slots.items()}
+    grams[0, 0] = diagonal_tile(lay, down, up)
     each = lay.ranks // lay.group
+    count = LANES // each
     for t in range(lay.tiles):
-        rows = down[t * LANES : (t + 1) * LANES]
-        wide = min(t + 1, last if last >= 2 else t + 1) if t < last else last
-        cols = [contract_last(rows, up[: wide * LANES]).astype(BF16)]
-        if t == 0:
-            corner = slice(last * LANES, (last + 1) * LANES)
-            cols.append(contract_last(down[corner], up[corner]).astype(BF16))
-            wide += 1
-        if wide * LANES < lay.gram:
-            cols.append(jnp.zeros((LANES, lay.gram - wide * LANES), BF16))
-        full = jnp.concatenate(cols, axis=1) if len(cols) > 1 else cols[0]
-        for q in range(LANES // each):
-            out_ref[t * (LANES // each) + q, :, gram_at:pre_at] = full[q * each : (q + 1) * each]
+        for side in range(2):
+            cols = slice(gram_at + side * LANES, gram_at + (side + 1) * LANES)
+            tile = grams.get((t, side), jnp.zeros((LANES, LANES), BF16))
+            for q in range(count):
+                out_ref[t * count + q, :, cols] = tile[q * each : (q + 1) * each]
 
 
 def sum_kernel(lay, index, r_ref, out_ref):
@@ -202,7 +246,6 @@
         acts[rows, :] = (pre * gate).astype(BF16)
         slope[rows, :] = gate * (1.0 + pre * (1.0 - gate)) * rank_scale
     tokens = lay.y * lay.rows
-    last = lay.tiles - 1
     lower = lax.broadcasted_iota(jnp.int32, (tokens, LANES), 1) < lay.rank
     for s in range(lay.pipe - 1, -1, -1):
         t, odd = s // 2, s % 2 == 1
@@ -215,15 +258,28 @@
             backs[t] = backs[t] + back
         if s == 0:
             continue
-        plain = t if t == last or not odd else t + 1
-        if plain > 0:
-            cols = slice(0, plain * LANES)
+        wide = min(t, 2)
+        if wide:
+            cols = slice(0, wide * LANES)
             along[:, cols] += width_scale * jnp.dot(
                 back, gram[tile, cols], preferred_element_type=F32
             )
-        if t == last and odd:
+        for c in range(2, t):
+            cols = slice(c * LANES, (c + 1) * LANES)
+            row, side = lay.slots[t, c]
+            along[:, cols] += width_scale * jnp.dot(
+                back,
+                gram[row * LANES : (row + 1) * LANES, side * LANES : (side + 1) * LANES],
+                preferred_element_type=F32,
+            )
+        if odd:
+            pair = gram[0:LANES, 0:LANES].astype(F32)
+            if t % 2 == 1:
+                pair = pltpu.roll(pair, lay.rank, 1)
+            if t >= 2:
+                pair = jnp.concatenate([pair[lay.rank :], pair[: lay.rank]], axis=0)
             along[:, tile] += width_scale * jnp.dot(
-                back, gram[0:LANES, LANES : 2 * LANES], preferred_element_type=F32
+                back, pair.astype(BF16), preferred_element_type=F32
             )
     acted = acts[...]
     back_all = jnp.concatenate([backs[t] for t in range(lay.tiles)], axis=1)
@@ -262,17 +318,16 @@
 
     by_column = sort_columns(lay, valid_rows, inputs, cotangent)
     by_column = lax.all_to_all(by_column, "dp", 0, 0, axis_index_groups=lay.along_y)
-    cots = lax.ppermute(by_column[:, :, lay.span :], both, lay.cotangent_turn())
-
     maps = lax.all_gather(weights, "dp", axis_index_groups=lay.along_z)
-    shared = lax.all_to_all(
-        maps.reshape(pipe, lay.per, 2, lay.rank, LANES), "pipe", 0, 0
-    )
+    cots, maps = lax.optimization_barrier((by_column[:, :, lay.span :], maps))
+    cots = lax.ppermute(cots, both, lay.cotangent_turn())
+    shared = lax.all_to_all(maps.reshape(pipe, lay.per, 2, lay.rank, LANES), "pipe", 0, 0)
+    by_column, cots = lax.optimization_barrier((by_column, cots))
     pre_part = call(
         functools.partial(pre_kernel, lay),
         jax.ShapeDtypeStruct((lay.y, lay.rows, LANES), BF16),
         (index, maps, by_column),
-        flops=2 * lay.y * lay.rows * lay.span * LANES,
+        flops=PRE_WEIGHT * 2 * lay.y * lay.rows * lay.span * LANES,
     )
     message = lay.ranks + lay.gram + LANES
     parts = call(

time: 195 us -> 250 us (1.28)
  Pallas kernels: 5.97 us -> 71.1 us
  blocking collectives: 137 us -> 125 us
  waiting for transfers between devices: 9.1 us -> 14.2 us
  local copies, waits for them, and re-layouts: 4.64 us -> 0.7 us
    pallas_call x1, Pallas kernels: 0.45 us -> 65.7 us  [sort_columns(): pl.pallas_call(functools.partial(sort_kernel, lay), out_shape=jax.ShapeDt...]
    all_to_all x1, blocking collectives: 28.7 us -> 19.3 us  [body(): parts = lax.all_to_all(parts, both, 0, 0, axis_index_groups=lay.plane)]
    ppermute x1, starting transfers between devices: 5.05 us -> 11.3 us  [body(): cots = lax.ppermute(cots, both, lay.cotangent_turn())]
    all_to_all x1, starting transfers between devices: 11.1 us -> 5.44 us  [body(): lax.all_to_all(maps.reshape(pipe, lay.per, 2, lay.rank, LANES), 'pipe', 0...]
    all_to_all x1, waiting for transfers between devices: 2.65 us -> 7.75 us  [body(): lax.all_to_all(maps.reshape(pipe, lay.per, 2, lay.rank, LANES), 'pipe', 0...]
    unnamed x14 -> x8, local copies, waits for them, and re-layouts: 3.96 us -> 0.03 us
where the time goes in v4:
time: 250 us; the launch traced here: 248 us
  blocking collectives  125 us (50%)
  Pallas kernels  71.1 us (28%)
  starting transfers between devices  32.9 us (13%)
  waiting for transfers between devices  14.2 us (6%)
    pallas_call x1, Pallas kernels, sort_columns(): pl.pallas_call(functools.partial(sort_kernel, lay), out_shape=jax.ShapeDt...  65.7 us
    all_gather x1, blocking collectives, body(): maps = lax.all_gather(weights, 'dp', axis_index_groups=lay.along_z)  34.6 us
    all_to_all x1, blocking collectives, body(): grads = lax.all_to_all(grads, 'dp', 0, 0, axis_index_groups=lay.along_z)  29.3 us
    all_to_all x1, blocking collectives, body(): sums = lax.all_to_all(sums, both, 0, 0, axis_index_groups=lay.plane)  24.4 us
    all_to_all x1, blocking collectives, body(): parts = lax.all_to_all(parts, both, 0, 0, axis_index_groups=lay.plane)  19.3 us
    all_to_all x1, blocking collectives, body(): squares = lax.all_to_all(squares, both, 0, 0, axis_index_groups=lay.plane)  17.7 us
    ppermute x1, starting transfers between devices, body(): cots = lax.ppermute(cots, both, lay.cotangent_turn())  11.3 us
    all_to_all x1, waiting for transfers between devices, body(): lax.all_to_all(maps.reshape(pipe, lay.per, 2, lay.rank, LANES), 'pipe', 0...  7.75 us
  transfers between devices with their start and end apart: 5, of which 2 were waited for; matrix products, arithmetic and copies ran while one was open for 0% of the time, Pallas kernels for 1%

profile of v4, /device:TPU:1, one launch (start us, length us, event | category | flops | bytes accessed | tf_op | source)
XLA Modules:
  0.0 247.8 jit_solution(2660743561639991042)
XLA Ops:
  1.3 65.7 %shard_map.102 = bf16[4,128,2304]{2,1,0:T(8,128)(2,1)} custom-call(s32[1]{0:T(128)S(6)} %copy.11.valid, bf16[128,8192]{1,0:T(8,128)(2,1)} %bitcast.8, bf16[128,1024]{1,0:T(8,128)(2,1)} %c_ref.1), custom_call_target="tpu_custom_call" | custom-call | bytes 4718592 | tf_op jit(solution)/shard_map/pallas_call | solution.py:135
  66.9 0.0 copy-start.3
  67.0 5.0 %all-to-all-start = ((bf16[4,128,2304]{2,1,0:T(8,128)(2,1)}), bf16[4,128,2304]{2,1,0:T(8,128)(2,1)S(1)}, u32[]{:S(2)}, u32[]{:S(2)}) async-start(bf16[4,128,2304]{2,1,0:T(8,128)(2,1)} %shard_map.102), calls=%async_computation | async-start | bytes 4718592 | tf_op jit(solution)/shard_map/all_to_all | solution.py:320
  72.0 0.0 copy-done.3
  72.0 34.6 %all_gather.3.w_ref = bf16[16,2,64,128]{3,2,1,0:T(8,128)(2,1)} all-gather(bf16[1,2,64,128]{3,2,1,0:T(8,128)(2,1)S(1)} %copy-done.3), channel_id=1, replica_groups={{0,1,2,3,4,5,6,7,8,9,10,11,12,13,14,15},{16,17,18,19,20,21,22,23,24,25,..., dimensions={0}, use_global_device_ids=true | all-gather | bytes 557056 | tf_op jit(solution)/shard_map/all_gather | solution.py:321
  106.6 0.0 all-to-all-done.x_ref
  106.7 11.3 %collective-permute-start = (bf16[4,128,256]{2,1,0:T(8,128)(2,1)S(1)}, bf16[4,128,256]{2,1,0:T(8,128)(2,1)S(1)}, u32[]{:S(2)}, u32[]{:S(2)}) collective-permute-start(bf16[4,128,256]{2,1,0:T(8,128)(2,1)S(1)} %slice.12), channel_id=1, source_target_pairs={{0,0},{1,1},{2,2},{3,3},{4,4},{5,5},{6,6},{7,7},{8,8},{9,9},{10,10... | collective-permute-start | bytes 786440 | tf_op jit(solution)/shard_map/ppermute | solution.py:323
  118.0 5.4 %all-to-all-start.1 = ((bf16[8,2,2,64,128]{4,3,2,1,0:T(8,128)(2,1)}), bf16[8,2,2,64,128]{4,3,2,1,0:T(8,128)(2,1)S(1)}, u32[]{:S(2)}, u32[]{:S(2)}) async-start(bf16[8,2,2,64,128]{4,3,2,1,0:T(8,128)(2,1)} %bitcast.2), calls=%async_computation.1 | async-start | bytes 1048576 | tf_op jit(solution)/shard_map/all_to_all | solution.py:324
  123.4 0.0 collective-permute-done.c_ref
  123.5 1.8 shard_map.103.pre_ref
  125.2 7.7 %all-to-all-done.1.w_ref = bf16[8,2,2,64,128]{4,3,2,1,0:T(8,128)(2,1)S(1)} async-done(((bf16[8,2,2,64,128]{4,3,2,1,0:T(8,128)(2,1)}), bf16[8,2,2,64,128]{4,3,2,1,0:T(8,128)(2,1)S(1)}, u32[]{:S(2)}, u32[]{:S(2)}) %all-to-all-start.1) | async-done | bytes 524320 | tf_op jit(solution)/shard_map/all_to_all | solution.py:324
  133.0 0.7 shard_map.104
  133.7 19.3 %all_to_all.35.r_ref = bf16[32,16,896]{2,1,0:T(8,128)(2,1)S(1)} all-to-all(bf16[32,16,896]{2,1,0:T(8,128)(2,1)S(1)} %shard_map.104), channel_id=1, replica_groups={{0,16,32,48,64,80,96,112,128,144,160,176,192,208,224,240,256,272,288,30..., dimensions={0} | all-to-all | bytes 1835008 | tf_op jit(solution)/shard_map/all_to_all | solution.py:339
  153.0 0.2 shard_map.105
  153.1 24.4 %all_to_all.36.q_ref = bf16[32,16,1280]{2,1,0:T(8,128)(2,1)S(1)} all-to-all(bf16[32,16,1280]{2,1,0:T(8,128)(2,1)S(1)} %shard_map.105), channel_id=1, replica_groups={{0,16,32,48,64,80,96,112,128,144,160,176,192,208,224,240,256,272,288,30..., dimensions={0} | all-to-all | bytes 2621440 | tf_op jit(solution)/shard_map/all_to_all | solution.py:346
  177.6 2.8 %shard_map.106 = bf16[16,128,128]{2,1,0:T(8,128)(2,1)S(1)} custom-call(s32[1]{0:T(128)} %bitcast.index, bf16[32,16,1280]{2,1,0:T(8,128)(2,1)S(1)} %all_to_all.36.q_ref, bf16[8,2,2,64,128]{4,3,2,1,0:T(8,128)(2,1)S(1)} %all-to-all-done.1.w_ref, bf16[4,128,256]{2,1,0:T(8,128)(2,1)S(1)} %collective-permute-done.c_ref, bf16[4,128,2304]{2,1,0:T(8,128)(2,1)S(1)} %all-to-all-done.x_ref), custom_call_target="tpu_custom_call" | custom-call | flops 536870912 | bytes 4980740 | tf_op jit(solution)/shard_map/pallas_call | solution.py:43
  180.4 0.0 copy-start
  180.4 0.0 copy-start.1
  180.4 0.0 copy-start.2
  180.4 29.3 %all_to_all.37 = bf16[16,128,128]{2,1,0:T(8,128)(2,1)S(1)} all-to-all(bf16[16,128,128]{2,1,0:T(8,128)(2,1)S(1)} %shard_map.106), channel_id=1, replica_groups={{0,1,2,3,4,5,6,7,8,9,10,11,12,13,14,15},{16,17,18,19,20,21,22,23,24,25,..., dimensions={0} | all-to-all | bytes 1048576 | tf_op jit(solution)/shard_map/all_to_all | solution.py:362
  209.7 0.1 convert_reduce_fusion
  209.8 17.7 %all_to_all.38 = f32[32,8,128]{2,1,0:T(8,128)S(1)} all-to-all(f32[32,8,128]{2,1,0:T(8,128)S(1)} %broadcast_in_dim.4), channel_id=1, replica_groups={{0,16,32,48,64,80,96,112,128,144,160,176,192,208,224,240,256,272,288,30..., dimensions={0} | all-to-all | bytes 262144 | tf_op jit(solution)/shard_map/all_to_all | solution.py:367
  227.6 0.6 broadcast_in_dim.5
  228.2 6.0 %all-to-all-start.6 = ((f32[16,8,128]{2,1,0:T(8,128)}), f32[16,8,128]{2,1,0:T(8,128)S(1)}, u32[]{:S(2)}, u32[]{:S(2)}) async-start(f32[16,8,128]{2,1,0:T(8,128)} %broadcast_in_dim.5), calls=%async_computation.6 | async-start | bytes 131072 | tf_op jit(solution)/shard_map/all_to_all | solution.py:369
  234.2 5.1 %collective-permute-start.1 = (f32[64,128]{1,0:T(8,128)S(1)}, f32[64,128]{1,0:T(8,128)S(1)}, u32[]{:S(2)}, u32[]{:S(2)}) collective-permute-start(f32[64,128]{1,0:T(8,128)S(1)} %get-tuple-element.17), channel_id=1, source_target_pairs={{0,0},{1,1},{2,64},{3,65},{4,128},{5,129},{6,192},{7,193},{8,256},... | collective-permute-start | bytes 98312 | tf_op jit(solution)/shard_map/ppermute | solution.py:365
  239.3 6.4 %all-to-all-done.6 = f32[16,8,128]{2,1,0:T(8,128)S(1)} async-done(((f32[16,8,128]{2,1,0:T(8,128)}), f32[16,8,128]{2,1,0:T(8,128)S(1)}, u32[]{:S(2)}, u32[]{:S(2)}) %all-to-all-start.6) | async-done | bytes 65568 | tf_op jit(solution)/shard_map/all_to_all | solution.py:369
  245.8 0.6 reduce_sum.39
  247.1 0.0 collective-permute-done.1
  247.1 0.0 copy-done
  247.1 0.0 copy-done.1
  247.1 0.0 copy-done.2
  247.1 0.7 fusion.1
  (5 shorter events, 0.1 us)
Async XLA Ops:
  66.9 5.0 %copy-start.3 = (bf16[1,2,64,128]{3,2,1,0:T(8,128)(2,1)S(1)}, bf16[1,2,64,128]{3,2,1,0:T(8,128)(2,1)}, u32[]{:S(2)}) copy-start(bf16[1,2,64,128]{3,2,1,0:T(8,128)(2,1)} %param.9) | copy-start | bytes 98308
  67.0 39.7 %all-to-all-start = ((bf16[4,128,2304]{2,1,0:T(8,128)(2,1)}), bf16[4,128,2304]{2,1,0:T(8,128)(2,1)S(1)}, u32[]{:S(2)}, u32[]{:S(2)}) async-start(bf16[4,128,2304]{2,1,0:T(8,128)(2,1)} %shard_map.102), calls=%async_computation | async-start | bytes 4718592 | tf_op jit(solution)/shard_map/all_to_all | solution.py:320
  106.7 16.8 %collective-permute-start = (bf16[4,128,256]{2,1,0:T(8,128)(2,1)S(1)}, bf16[4,128,256]{2,1,0:T(8,128)(2,1)S(1)}, u32[]{:S(2)}, u32[]{:S(2)}) collective-permute-start(bf16[4,128,256]{2,1,0:T(8,128)(2,1)S(1)} %slice.12), channel_id=1, source_target_pairs={{0,0},{1,1},{2,2},{3,3},{4,4},{5,5},{6,6},{7,7},{8,8},{9,9},{10,10... | collective-permute-start | bytes 786440 | tf_op jit(solution)/shard_map/ppermute | solution.py:323
  118.0 15.0 %all-to-all-start.1 = ((bf16[8,2,2,64,128]{4,3,2,1,0:T(8,128)(2,1)}), bf16[8,2,2,64,128]{4,3,2,1,0:T(8,128)(2,1)S(1)}, u32[]{:S(2)}, u32[]{:S(2)}) async-start(bf16[8,2,2,64,128]{4,3,2,1,0:T(8,128)(2,1)} %bitcast.2), calls=%async_computation.1 | async-start | bytes 1048576 | tf_op jit(solution)/shard_map/all_to_all | solution.py:324
  180.4 66.7 %copy-start = (f32[1,2,64,128]{3,2,1,0:T(8,128)S(1)}, f32[1,2,64,128]{3,2,1,0:T(8,128)}, u32[]{:S(2)}) copy-start(f32[1,2,64,128]{3,2,1,0:T(8,128)} %param.10) | copy-start | bytes 196612
  180.4 66.7 %copy-start.1 = (f32[1,2,64,128]{3,2,1,0:T(8,128)S(1)}, f32[1,2,64,128]{3,2,1,0:T(8,128)}, u32[]{:S(2)}) copy-start(f32[1,2,64,128]{3,2,1,0:T(8,128)} %param.12) | copy-start | bytes 196612
  180.4 66.7 %copy-start.2 = (f32[1,2,64,128]{3,2,1,0:T(8,128)S(1)}, f32[1,2,64,128]{3,2,1,0:T(8,128)}, u32[]{:S(2)}) copy-start(f32[1,2,64,128]{3,2,1,0:T(8,128)} %param.11) | copy-start | bytes 196612
  228.2 17.6 %all-to-all-start.6 = ((f32[16,8,128]{2,1,0:T(8,128)}), f32[16,8,128]{2,1,0:T(8,128)S(1)}, u32[]{:S(2)}, u32[]{:S(2)}) async-start(f32[16,8,128]{2,1,0:T(8,128)} %broadcast_in_dim.5), calls=%async_computation.6 | async-start | bytes 131072 | tf_op jit(solution)/shard_map/all_to_all | solution.py:369
  234.2 12.9 %collective-permute-start.1 = (f32[64,128]{1,0:T(8,128)S(1)}, f32[64,128]{1,0:T(8,128)S(1)}, u32[]{:S(2)}, u32[]{:S(2)}) collective-permute-start(f32[64,128]{1,0:T(8,128)S(1)} %get-tuple-element.17), channel_id=1, source_target_pairs={{0,0},{1,1},{2,64},{3,65},{4,128},{5,129},{6,192},{7,193},{8,256},... | collective-permute-start | bytes 98312 | tf_op jit(solution)/shard_map/ppermute | solution.py:365

commit v5 on v4

--- a/solution.py
+++ b/solution.py
@@ -102,32 +102,34 @@
         ]
 
 
-def sort_kernel(lay, valid, x_ref, c_ref, out_ref, cots, sems):
-    copies = [
-        pltpu.make_async_copy(
-            x_ref.at[:, pl.ds(a * lay.span, lay.span)],
-            out_ref.at[a, :, pl.ds(0, lay.span)],
-            sems.at[a],
+def sort_kernel(lay, valid, x_ref, c_ref, out_ref, held, cots, sems):
+    loads, stores = [], []
+    for a in range(lay.y):
+        cols = pl.ds(a * lay.span, lay.span)
+        loads.append(pltpu.make_async_copy(x_ref.at[:, cols], held.at[a], sems.at[a]))
+        stores.append(
+            pltpu.make_async_copy(
+                held.at[a], out_ref.at[a, :, pl.ds(0, lay.span)], sems.at[lay.y + a]
+            )
         )
-        for a in range(lay.y)
-    ]
-    for copy in copies:
-        copy.start()
+        loads[a].start()
     cot = c_ref[...]
     live = lax.broadcasted_iota(jnp.int32, cot.shape, 0) < valid[0]
     cots[...] = jnp.where(live, cot, jnp.zeros_like(cot))
-    copies += [
-        pltpu.make_async_copy(
-            cots.at[:, pl.ds(a * lay.share, lay.share)],
-            out_ref.at[a, :, pl.ds(lay.span, lay.share)],
-            sems.at[lay.y + a],
+    for a in range(lay.y):
+        stores.append(
+            pltpu.make_async_copy(
+                cots.at[:, pl.ds(a * lay.share, lay.share)],
+                out_ref.at[a, :, pl.ds(lay.span, lay.share)],
+                sems.at[2 * lay.y + a],
+            )
         )
-        for a in range(lay.y)
-    ]
-    for copy in copies[lay.y :]:
-        copy.start()
-    for copy in copies:
-        copy.wait()
+        stores[lay.y + a].start()
+    for a in range(lay.y):
+        loads[a].wait()
+        stores[a].start()
+    for store in stores:
+        store.wait()
 
 
 def sort_columns(lay, valid_rows, inputs, cotangent):
@@ -142,8 +144,9 @@
         ],
         out_specs=pl.BlockSpec(memory_space=pltpu.HBM),
         scratch_shapes=[
+            pltpu.VMEM((lay.y, lay.rows, lay.span), BF16),
             pltpu.VMEM(cotangent.shape, BF16),
-            pltpu.SemaphoreType.DMA((2 * lay.y,)),
+            pltpu.SemaphoreType.DMA((3 * lay.y,)),
         ],
         compiler_params=pltpu.CompilerParams(vmem_limit_bytes=SORT_LIMIT),
         cost_estimate=pl.CostEstimate(

time: 250 us -> 188 us (0.75)
  Pallas kernels: 71.1 us -> 9.02 us
    pallas_call x1, Pallas kernels: 65.7 us -> 3.58 us  [sort_columns(): pl.pallas_call(functools.partial(sort_kernel, lay), out_shape=jax.ShapeDt...]
where the time goes in v5:
time: 188 us; the launch traced here: 186 us
  blocking collectives  125 us (66%)
  starting transfers between devices  32.9 us (18%)
  waiting for transfers between devices  14.2 us (8%)
  Pallas kernels  9.02 us (5%)
  between operations  2.12 us (1%)
    all_gather x1, blocking collectives, body(): maps = lax.all_gather(weights, 'dp', axis_index_groups=lay.along_z)  34.6 us
    all_to_all x1, blocking collectives, body(): grads = lax.all_to_all(grads, 'dp', 0, 0, axis_index_groups=lay.along_z)  29.3 us
    all_to_all x1, blocking collectives, body(): sums = lax.all_to_all(sums, both, 0, 0, axis_index_groups=lay.plane)  24.4 us
    all_to_all x1, blocking collectives, body(): parts = lax.all_to_all(parts, both, 0, 0, axis_index_groups=lay.plane)  19.3 us
    all_to_all x1, blocking collectives, body(): squares = lax.all_to_all(squares, both, 0, 0, axis_index_groups=lay.plane)  17.7 us
    ppermute x1, starting transfers between devices, body(): cots = lax.ppermute(cots, both, lay.cotangent_turn())  11.3 us
    all_to_all x1, waiting for transfers between devices, body(): lax.all_to_all(maps.reshape(pipe, lay.per, 2, lay.rank, LANES), 'pipe', 0...  7.74 us
    all_to_all x1, waiting for transfers between devices, body(): squares = lax.all_to_all(squares, 'dp', 0, 0, axis_index_groups=lay.along_z)  6.44 us
  transfers between devices with their start and end apart: 5, of which 2 were waited for; matrix products, arithmetic and copies ran while one was open for 0% of the time, Pallas kernels for 1%

profile of v5, /device:TPU:1, one launch (start us, length us, event | category | flops | bytes accessed | tf_op | source)
XLA Modules:
  0.0 185.8 jit_solution(8449051983949663931)
XLA Ops:
  1.3 3.6 %shard_map.102 = bf16[4,128,2304]{2,1,0:T(8,128)(2,1)} custom-call(s32[1]{0:T(128)S(6)} %copy.11.valid, bf16[128,8192]{1,0:T(8,128)(2,1)} %bitcast.8, bf16[128,1024]{1,0:T(8,128)(2,1)} %c_ref.1), custom_call_target="tpu_custom_call" | custom-call | bytes 4718592 | tf_op jit(solution)/shard_map/pallas_call | solution.py:137
  4.9 0.0 copy-start.3
  4.9 5.0 %all-to-all-start = ((bf16[4,128,2304]{2,1,0:T(8,128)(2,1)}), bf16[4,128,2304]{2,1,0:T(8,128)(2,1)S(1)}, u32[]{:S(2)}, u32[]{:S(2)}) async-start(bf16[4,128,2304]{2,1,0:T(8,128)(2,1)} %shard_map.102), calls=%async_computation | async-start | bytes 4718592 | tf_op jit(solution)/shard_map/all_to_all | solution.py:323
  9.9 0.0 copy-done.3
  9.9 34.6 %all_gather.3.w_ref = bf16[16,2,64,128]{3,2,1,0:T(8,128)(2,1)} all-gather(bf16[1,2,64,128]{3,2,1,0:T(8,128)(2,1)S(1)} %copy-done.3), channel_id=1, replica_groups={{0,1,2,3,4,5,6,7,8,9,10,11,12,13,14,15},{16,17,18,19,20,21,22,23,24,25,..., dimensions={0}, use_global_device_ids=true | all-gather | bytes 557056 | tf_op jit(solution)/shard_map/all_gather | solution.py:324
  44.5 0.0 all-to-all-done.x_ref
  44.6 11.3 %collective-permute-start = (bf16[4,128,256]{2,1,0:T(8,128)(2,1)S(1)}, bf16[4,128,256]{2,1,0:T(8,128)(2,1)S(1)}, u32[]{:S(2)}, u32[]{:S(2)}) collective-permute-start(bf16[4,128,256]{2,1,0:T(8,128)(2,1)S(1)} %slice.12), channel_id=1, source_target_pairs={{0,0},{1,1},{2,2},{3,3},{4,4},{5,5},{6,6},{7,7},{8,8},{9,9},{10,10... | collective-permute-start | bytes 786440 | tf_op jit(solution)/shard_map/ppermute | solution.py:326
  55.9 5.4 %all-to-all-start.1 = ((bf16[8,2,2,64,128]{4,3,2,1,0:T(8,128)(2,1)}), bf16[8,2,2,64,128]{4,3,2,1,0:T(8,128)(2,1)S(1)}, u32[]{:S(2)}, u32[]{:S(2)}) async-start(bf16[8,2,2,64,128]{4,3,2,1,0:T(8,128)(2,1)} %bitcast.2), calls=%async_computation.1 | async-start | bytes 1048576 | tf_op jit(solution)/shard_map/all_to_all | solution.py:327
  61.4 0.0 collective-permute-done.c_ref
  61.4 1.8 shard_map.103.pre_ref
  63.2 7.7 %all-to-all-done.1.w_ref = bf16[8,2,2,64,128]{4,3,2,1,0:T(8,128)(2,1)S(1)} async-done(((bf16[8,2,2,64,128]{4,3,2,1,0:T(8,128)(2,1)}), bf16[8,2,2,64,128]{4,3,2,1,0:T(8,128)(2,1)S(1)}, u32[]{:S(2)}, u32[]{:S(2)}) %all-to-all-start.1) | async-done | bytes 524320 | tf_op jit(solution)/shard_map/all_to_all | solution.py:327
  70.9 0.7 shard_map.104
  71.6 19.3 %all_to_all.35.r_ref = bf16[32,16,896]{2,1,0:T(8,128)(2,1)S(1)} all-to-all(bf16[32,16,896]{2,1,0:T(8,128)(2,1)S(1)} %shard_map.104), channel_id=1, replica_groups={{0,16,32,48,64,80,96,112,128,144,160,176,192,208,224,240,256,272,288,30..., dimensions={0} | all-to-all | bytes 1835008 | tf_op jit(solution)/shard_map/all_to_all | solution.py:342
  90.9 0.2 shard_map.105
  91.0 24.4 %all_to_all.36.q_ref = bf16[32,16,1280]{2,1,0:T(8,128)(2,1)S(1)} all-to-all(bf16[32,16,1280]{2,1,0:T(8,128)(2,1)S(1)} %shard_map.105), channel_id=1, replica_groups={{0,16,32,48,64,80,96,112,128,144,160,176,192,208,224,240,256,272,288,30..., dimensions={0} | all-to-all | bytes 2621440 | tf_op jit(solution)/shard_map/all_to_all | solution.py:349
  115.5 2.8 %shard_map.106 = bf16[16,128,128]{2,1,0:T(8,128)(2,1)S(1)} custom-call(s32[1]{0:T(128)} %bitcast.index, bf16[32,16,1280]{2,1,0:T(8,128)(2,1)S(1)} %all_to_all.36.q_ref, bf16[8,2,2,64,128]{4,3,2,1,0:T(8,128)(2,1)S(1)} %all-to-all-done.1.w_ref, bf16[4,128,256]{2,1,0:T(8,128)(2,1)S(1)} %collective-permute-done.c_ref, bf16[4,128,2304]{2,1,0:T(8,128)(2,1)S(1)} %all-to-all-done.x_ref), custom_call_target="tpu_custom_call" | custom-call | flops 536870912 | bytes 4980740 | tf_op jit(solution)/shard_map/pallas_call | solution.py:43
  118.3 0.0 copy-start
  118.3 0.0 copy-start.1
  118.3 0.0 copy-start.2
  118.3 29.3 %all_to_all.37 = bf16[16,128,128]{2,1,0:T(8,128)(2,1)S(1)} all-to-all(bf16[16,128,128]{2,1,0:T(8,128)(2,1)S(1)} %shard_map.106), channel_id=1, replica_groups={{0,1,2,3,4,5,6,7,8,9,10,11,12,13,14,15},{16,17,18,19,20,21,22,23,24,25,..., dimensions={0} | all-to-all | bytes 1048576 | tf_op jit(solution)/shard_map/all_to_all | solution.py:365
  147.6 0.1 convert_reduce_fusion
  147.7 17.7 %all_to_all.38 = f32[32,8,128]{2,1,0:T(8,128)S(1)} all-to-all(f32[32,8,128]{2,1,0:T(8,128)S(1)} %broadcast_in_dim.4), channel_id=1, replica_groups={{0,16,32,48,64,80,96,112,128,144,160,176,192,208,224,240,256,272,288,30..., dimensions={0} | all-to-all | bytes 262144 | tf_op jit(solution)/shard_map/all_to_all | solution.py:370
  165.5 0.6 broadcast_in_dim.5
  166.1 6.0 %all-to-all-start.6 = ((f32[16,8,128]{2,1,0:T(8,128)}), f32[16,8,128]{2,1,0:T(8,128)S(1)}, u32[]{:S(2)}, u32[]{:S(2)}) async-start(f32[16,8,128]{2,1,0:T(8,128)} %broadcast_in_dim.5), calls=%async_computation.6 | async-start | bytes 131072 | tf_op jit(solution)/shard_map/all_to_all | solution.py:372
  172.2 5.1 %collective-permute-start.1 = (f32[64,128]{1,0:T(8,128)S(1)}, f32[64,128]{1,0:T(8,128)S(1)}, u32[]{:S(2)}, u32[]{:S(2)}) collective-permute-start(f32[64,128]{1,0:T(8,128)S(1)} %get-tuple-element.17), channel_id=1, source_target_pairs={{0,0},{1,1},{2,64},{3,65},{4,128},{5,129},{6,192},{7,193},{8,256},... | collective-permute-start | bytes 98312 | tf_op jit(solution)/shard_map/ppermute | solution.py:368
  177.3 6.4 %all-to-all-done.6 = f32[16,8,128]{2,1,0:T(8,128)S(1)} async-done(((f32[16,8,128]{2,1,0:T(8,128)}), f32[16,8,128]{2,1,0:T(8,128)S(1)}, u32[]{:S(2)}, u32[]{:S(2)}) %all-to-all-start.6) | async-done | bytes 65568 | tf_op jit(solution)/shard_map/all_to_all | solution.py:372
  183.7 0.6 reduce_sum.39
  185.0 0.0 collective-permute-done.1
  185.0 0.0 copy-done
  185.0 0.0 copy-done.1
  185.0 0.0 copy-done.2
  185.1 0.7 fusion.1
  (5 shorter events, 0.1 us)
Async XLA Ops:
  4.9 5.0 %copy-start.3 = (bf16[1,2,64,128]{3,2,1,0:T(8,128)(2,1)S(1)}, bf16[1,2,64,128]{3,2,1,0:T(8,128)(2,1)}, u32[]{:S(2)}) copy-start(bf16[1,2,64,128]{3,2,1,0:T(8,128)(2,1)} %param.9) | copy-start | bytes 98308
  4.9 39.7 %all-to-all-start = ((bf16[4,128,2304]{2,1,0:T(8,128)(2,1)}), bf16[4,128,2304]{2,1,0:T(8,128)(2,1)S(1)}, u32[]{:S(2)}, u32[]{:S(2)}) async-start(bf16[4,128,2304]{2,1,0:T(8,128)(2,1)} %shard_map.102), calls=%async_computation | async-start | bytes 4718592 | tf_op jit(solution)/shard_map/all_to_all | solution.py:323
  44.6 16.8 %collective-permute-start = (bf16[4,128,256]{2,1,0:T(8,128)(2,1)S(1)}, bf16[4,128,256]{2,1,0:T(8,128)(2,1)S(1)}, u32[]{:S(2)}, u32[]{:S(2)}) collective-permute-start(bf16[4,128,256]{2,1,0:T(8,128)(2,1)S(1)} %slice.12), channel_id=1, source_target_pairs={{0,0},{1,1},{2,2},{3,3},{4,4},{5,5},{6,6},{7,7},{8,8},{9,9},{10,10... | collective-permute-start | bytes 786440 | tf_op jit(solution)/shard_map/ppermute | solution.py:326
  55.9 15.0 %all-to-all-start.1 = ((bf16[8,2,2,64,128]{4,3,2,1,0:T(8,128)(2,1)}), bf16[8,2,2,64,128]{4,3,2,1,0:T(8,128)(2,1)S(1)}, u32[]{:S(2)}, u32[]{:S(2)}) async-start(bf16[8,2,2,64,128]{4,3,2,1,0:T(8,128)(2,1)} %bitcast.2), calls=%async_computation.1 | async-start | bytes 1048576 | tf_op jit(solution)/shard_map/all_to_all | solution.py:327
  118.3 66.7 %copy-start = (f32[1,2,64,128]{3,2,1,0:T(8,128)S(1)}, f32[1,2,64,128]{3,2,1,0:T(8,128)}, u32[]{:S(2)}) copy-start(f32[1,2,64,128]{3,2,1,0:T(8,128)} %param.10) | copy-start | bytes 196612
  118.3 66.7 %copy-start.1 = (f32[1,2,64,128]{3,2,1,0:T(8,128)S(1)}, f32[1,2,64,128]{3,2,1,0:T(8,128)}, u32[]{:S(2)}) copy-start(f32[1,2,64,128]{3,2,1,0:T(8,128)} %param.12) | copy-start | bytes 196612
  118.3 66.7 %copy-start.2 = (f32[1,2,64,128]{3,2,1,0:T(8,128)S(1)}, f32[1,2,64,128]{3,2,1,0:T(8,128)}, u32[]{:S(2)}) copy-start(f32[1,2,64,128]{3,2,1,0:T(8,128)} %param.11) | copy-start | bytes 196612
  166.1 17.6 %all-to-all-start.6 = ((f32[16,8,128]{2,1,0:T(8,128)}), f32[16,8,128]{2,1,0:T(8,128)S(1)}, u32[]{:S(2)}, u32[]{:S(2)}) async-start(f32[16,8,128]{2,1,0:T(8,128)} %broadcast_in_dim.5), calls=%async_computation.6 | async-start | bytes 131072 | tf_op jit(solution)/shard_map/all_to_all | solution.py:372
  172.2 12.9 %collective-permute-start.1 = (f32[64,128]{1,0:T(8,128)S(1)}, f32[64,128]{1,0:T(8,128)S(1)}, u32[]{:S(2)}, u32[]{:S(2)}) collective-permute-start(f32[64,128]{1,0:T(8,128)S(1)} %get-tuple-element.17), channel_id=1, source_target_pairs={{0,0},{1,1},{2,64},{3,65},{4,128},{5,129},{6,192},{7,193},{8,256},... | collective-permute-start | bytes 98312 | tf_op jit(solution)/shard_map/ppermute | solution.py:368

commit v6 on v5

--- a/solution.py
+++ b/solution.py
@@ -20,7 +20,6 @@
 Y_SIZE = 4
 VMEM_LIMIT = 48 * 1024 * 1024
 SORT_LIMIT = 63 * 1024 * 1024
-PRE_WEIGHT = 12
 INTERPRET = False
 BF16 = jnp.bfloat16
 F32 = jnp.float32
@@ -71,6 +70,9 @@
         rest = [(a, b) for a in range(1, self.tiles) for b in range(2, a)]
         self.slots.update(zip(rest, spare))
         y, z = self.y, self.z
+        half = self.half
+        self.order = [half * m + h for h in range(half) for m in range(y)]
+        self.across = [[half * m + h for m in range(y)] for h in range(half)]
         self.along_z = [[a * z + b for b in range(z)] for a in range(y)]
         self.along_y = [[a * z + b for a in range(y)] for b in range(z)]
         self.plane = [
@@ -83,26 +85,25 @@
     def everywhere(self):
         return [(p, a, b) for p in range(self.pipe) for a in range(self.y) for b in range(self.z)]
 
-    def cotangent_turn(self):
-        return [
-            (
-                self.device(p, a, b),
-                self.device(self.y * (p % self.half) + a, p // self.half, b),
-            )
-            for p, a, b in self.everywhere()
-        ]
-
     def gradient_home(self):
         return [
             (
                 self.device(p, a, b),
-                self.device(b // self.per, a, p * self.per + b % self.per),
+                self.device(b // self.per, a, self.order.index(p) * self.per + b % self.per),
             )
             for p, a, b in self.everywhere()
         ]
 
 
-def sort_kernel(lay, valid, x_ref, c_ref, out_ref, held, cots, sems):
+def split_kernel(lay, valid, c_ref, out_ref):
+    cot = c_ref[...]
+    live = lax.broadcasted_iota(jnp.int32, cot.shape, 0) < valid[0]
+    cot = jnp.where(live, cot, jnp.zeros_like(cot))
+    for m in range(lay.y):
+        out_ref[m] = cot[:, m * lay.share : (m + 1) * lay.share]
+
+
+def sort_kernel(lay, x_ref, out_ref, held, sems):
     loads, stores = [], []
     for a in range(lay.y):
         cols = pl.ds(a * lay.span, lay.span)
@@ -113,18 +114,6 @@
             )
         )
         loads[a].start()
-    cot = c_ref[...]
-    live = lax.broadcasted_iota(jnp.int32, cot.shape, 0) < valid[0]
-    cots[...] = jnp.where(live, cot, jnp.zeros_like(cot))
-    for a in range(lay.y):
-        stores.append(
-            pltpu.make_async_copy(
-                cots.at[:, pl.ds(a * lay.share, lay.share)],
-                out_ref.at[a, :, pl.ds(lay.span, lay.share)],
-                sems.at[2 * lay.y + a],
-            )
-        )
-        stores[lay.y + a].start()
     for a in range(lay.y):
         loads[a].wait()
         stores[a].start()
@@ -132,28 +121,48 @@
         store.wait()
 
 
-def sort_columns(lay, valid_rows, inputs, cotangent):
+def sort_columns(lay, inputs):
     both = lay.span + lay.share
     return pl.pallas_call(
         functools.partial(sort_kernel, lay),
         out_shape=jax.ShapeDtypeStruct((lay.y, lay.rows, both), BF16),
-        in_specs=[
-            pl.BlockSpec(memory_space=pltpu.SMEM),
-            pl.BlockSpec(memory_space=pltpu.HBM),
-            pl.BlockSpec(memory_space=pltpu.VMEM),
-        ],
+        in_specs=[pl.BlockSpec(memory_space=pltpu.HBM)],
         out_specs=pl.BlockSpec(memory_space=pltpu.HBM),
         scratch_shapes=[
             pltpu.VMEM((lay.y, lay.rows, lay.span), BF16),
-            pltpu.VMEM(cotangent.shape, BF16),
-            pltpu.SemaphoreType.DMA((3 * lay.y,)),
+            pltpu.SemaphoreType.DMA((2 * lay.y,)),
         ],
         compiler_params=pltpu.CompilerParams(vmem_limit_bytes=SORT_LIMIT),
         cost_estimate=pl.CostEstimate(
             flops=0, bytes_accessed=4 * lay.y * lay.rows * both, transcendentals=0
         ),
         interpret=INTERPRET,
-    )(valid_rows, inputs, cotangent)
+    )(inputs)
+
+
+def join_kernel(lay, by_column, c_ref, out_ref, sem):
+    copy = pltpu.make_async_copy(c_ref, out_ref.at[:, :, pl.ds(lay.span, lay.share)], sem)
+    copy.start()
+    copy.wait()
+
+
+def join_columns(lay, by_column, cots):
+    return pl.pallas_call(
+        functools.partial(join_kernel, lay),
+        out_shape=jax.ShapeDtypeStruct(by_column.shape, BF16),
+        in_specs=[
+            pl.BlockSpec(memory_space=pltpu.HBM),
+            pl.BlockSpec(memory_space=pltpu.VMEM),
+        ],
+        out_specs=pl.BlockSpec(memory_space=pltpu.HBM),
+        input_output_aliases={0: 0},
+        scratch_shapes=[pltpu.SemaphoreType.DMA],
+        compiler_params=pltpu.CompilerParams(vmem_limit_bytes=SORT_LIMIT),
+        cost_estimate=pl.CostEstimate(
+            flops=0, bytes_accessed=4 * math.prod(cots.shape), transcendentals=0
+        ),
+        interpret=INTERPRET,
+    )(by_column, cots)
 
 
 def pre_kernel(lay, index, w_ref, x_ref, out_ref):
@@ -169,7 +178,7 @@
 def section_maps(lay, w_ref, which):
     return jnp.concatenate(
         [
-            jnp.concatenate([w_ref[s, j, which] for j in range(lay.per)], axis=1)
+            jnp.concatenate([w_ref[lay.order.index(s), j, which] for j in range(lay.per)], axis=1)
             for s in range(lay.pipe)
         ],
         axis=0,
@@ -199,7 +208,7 @@
     down, up = section_maps(lay, w_ref, 0), section_maps(lay, w_ref, 1)
     gram_at, pre_at = lay.ranks, lay.ranks + lay.gram
     for a in range(lay.y):
-        part = contract_last(c_ref[a], up).astype(BF16)
+        part = contract_last(c_ref[a, :, lay.span :], up).astype(BF16)
         for p in range(lay.pipe):
             rows = slice(p * lay.piece, (p + 1) * lay.piece)
             out_ref[p * lay.y + a, :, 0:gram_at] = part[rows]
@@ -234,7 +243,7 @@
         out_ref[q] = message
 
 
-def chain_kernel(lay, index, q_ref, w_ref, c_ref, x_ref, out_ref, *scratch):
+def chain_kernel(lay, index, q_ref, w_ref, x_ref, out_ref, *scratch):
     along, slope, acts, backs, gram, held = scratch
     width_scale, rank_scale = 1.0 / math.sqrt(lay.width), 1.0 / math.sqrt(lay.rank)
     gram_at, pre_at = lay.ranks, lay.ranks + lay.gram
@@ -290,7 +299,7 @@
     before = lax.broadcasted_iota(jnp.int32, cross.shape, 0) // lay.rank
     after = lax.broadcasted_iota(jnp.int32, cross.shape, 1) // lay.rank
     cross = jnp.where(before < after, cross * width_scale, 0.0).astype(BF16)
-    cot_all = c_ref[...].reshape(tokens, lay.share)
+    cot_all = x_ref[:, :, lay.span :].reshape(tokens, lay.share)
     grad_up = contract_first(acted, cot_all) + jnp.dot(
         cross, section_maps(lay, w_ref, 0), preferred_element_type=F32
     )
@@ -319,24 +328,33 @@
     both = ("pipe", "dp")
     index = lax.axis_index("pipe").astype(jnp.int32).reshape(1)
 
-    by_column = sort_columns(lay, valid_rows, inputs, cotangent)
+    cots = call(
+        functools.partial(split_kernel, lay),
+        jax.ShapeDtypeStruct((lay.y, lay.rows, lay.share), BF16),
+        (valid_rows, cotangent),
+    )
+    cots = lax.all_to_all(cots, "pipe", 0, 0, axis_index_groups=lay.across)
+    by_column = join_columns(lay, sort_columns(lay, inputs), cots)
     by_column = lax.all_to_all(by_column, "dp", 0, 0, axis_index_groups=lay.along_y)
     maps = lax.all_gather(weights, "dp", axis_index_groups=lay.along_z)
-    cots, maps = lax.optimization_barrier((by_column[:, :, lay.span :], maps))
-    cots = lax.ppermute(cots, both, lay.cotangent_turn())
-    shared = lax.all_to_all(maps.reshape(pipe, lay.per, 2, lay.rank, LANES), "pipe", 0, 0)
-    by_column, cots = lax.optimization_barrier((by_column, cots))
+    shared = lax.all_to_all(
+        maps.reshape(pipe, lay.per, 2, lay.rank, LANES),
+        "pipe",
+        0,
+        0,
+        axis_index_groups=[lay.order],
+    )
     pre_part = call(
         functools.partial(pre_kernel, lay),
         jax.ShapeDtypeStruct((lay.y, lay.rows, LANES), BF16),
         (index, maps, by_column),
-        flops=PRE_WEIGHT * 2 * lay.y * lay.rows * lay.span * LANES,
+        flops=2 * lay.y * lay.rows * lay.span * LANES,
     )
     message = lay.ranks + lay.gram + LANES
     parts = call(
         functools.partial(pack_kernel, lay),
         jax.ShapeDtypeStruct((lay.group, lay.piece, message), BF16),
-        (index, shared, pre_part, cots),
+        (index, shared, pre_part, by_column),
         flops=4 * lay.y * lay.rows * lay.share * lay.ranks,
     )
     parts = lax.all_to_all(parts, both, 0, 0, axis_index_groups=lay.plane)
@@ -351,7 +369,7 @@
     grads = call(
         functools.partial(chain_kernel, lay),
         jax.ShapeDtypeStruct((lay.z, 2 * lay.rank, LANES), BF16),
-        (index, sums, shared, cots, by_column),
+        (index, sums, shared, by_column),
         scratch=(
             pltpu.VMEM((tokens, lay.ranks), F32),
             pltpu.VMEM((tokens, lay.ranks), F32),

time: 188 us -> 195 us (1.037)
  starting transfers between devices: 32.9 us -> 39.4 us
  waiting for transfers between devices: 14.2 us -> 10.7 us
  blocking collectives: 125 us -> 128 us
    ppermute x1 -> x0, starting transfers between devices: 11.3 us -> none  [body(): cots = lax.ppermute(cots, both, lay.cotangent_turn())]
    ppermute x1, starting transfers between devices: 5.1 us -> 12.9 us  [body(): grad_up = lax.ppermute(grads[lay.rank:], both, lay.gradient_home())]
    all_to_all x1, waiting for transfers between devices: 6.44 us -> 0.01 us  [body(): squares = lax.all_to_all(squares, 'dp', 0, 0, axis_index_groups=lay.along_z)]
    all_to_all x1, starting transfers between devices: 5.44 us -> 11.5 us  [body(): lax.all_to_all(maps.reshape(pipe, lay.per, 2, lay.rank, LANES), 'pipe', 0...]
    all_to_all x0 -> x1, starting transfers between devices: none -> 4.84 us  [body(): cots = lax.all_to_all(cots, 'pipe', 0, 0, axis_index_groups=lay.across)]
    all_to_all x0 -> x1, waiting for transfers between devices: none -> 3.07 us  [body(): cots = lax.all_to_all(cots, 'pipe', 0, 0, axis_index_groups=lay.across)]
    pallas_call x4 -> x5, Pallas kernels: 5.45 us -> 6.17 us  [call(): pl.pallas_call(kernel, out_shape=out_shape, in_specs=[pl.BlockSpec(memory...]
  transfers between devices with their start and end apart: 5 -> 5, of which waited for: 2 -> 2; matrix products, arithmetic and copies ran while one was open for 0% -> 0% of each run, Pallas kernels for 1% -> 2%
where the time goes in v6:
time: 195 us; the launch traced here: 194 us
  blocking collectives  128 us (66%)
  starting transfers between devices  39.4 us (20%)
  waiting for transfers between devices  10.7 us (5%)
  Pallas kernels  10.3 us (5%)
  local copies, waits for them, and re-layouts  2.33 us (1%)
  between operations  2.13 us (1%)
    all_gather x1, blocking collectives, body(): maps = lax.all_gather(weights, 'dp', axis_index_groups=lay.along_z)  35.1 us
    all_to_all x1, blocking collectives, body(): grads = lax.all_to_all(grads, 'dp', 0, 0, axis_index_groups=lay.along_z)  29.3 us
    all_to_all x1, blocking collectives, body(): sums = lax.all_to_all(sums, both, 0, 0, axis_index_groups=lay.plane)  24.4 us
    all_to_all x1, blocking collectives, body(): parts = lax.all_to_all(parts, both, 0, 0, axis_index_groups=lay.plane)  21.1 us
    all_to_all x1, blocking collectives, body(): squares = lax.all_to_all(squares, both, 0, 0, axis_index_groups=lay.plane)  17.7 us
    ppermute x1, starting transfers between devices, body(): grad_up = lax.ppermute(grads[lay.rank:], both, lay.gradient_home())  12.9 us
    all_to_all x1, starting transfers between devices, body(): lax.all_to_all(maps.reshape(pipe, lay.per, 2, lay.rank, LANES), 'pipe', 0...  11.5 us
    all_to_all x1, waiting for transfers between devices, body(): lax.all_to_all(maps.reshape(pipe, lay.per, 2, lay.rank, LANES), 'pipe', 0...  7.59 us
  transfers between devices with their start and end apart: 5, of which 2 were waited for; matrix products, arithmetic and copies ran while one was open for 0% of the time, Pallas kernels for 2%

profile of v6, /device:TPU:1, one launch (start us, length us, event | category | flops | bytes accessed | tf_op | source)
XLA Modules:
  0.0 194.0 jit_solution(18260834155654994304)
XLA Ops:
  1.3 0.0 copy-start
  1.3 0.9 copy-done
  2.2 0.7 shard_map.103
  3.0 4.8 %all-to-all-start.1 = ((bf16[4,128,256]{2,1,0:T(8,128)(2,1)}), bf16[4,128,256]{2,1,0:T(8,128)(2,1)S(1)}, u32[]{:S(2)}, u32[]{:S(2)}) async-start(bf16[4,128,256]{2,1,0:T(8,128)(2,1)} %shard_map.103), calls=%async_computation.1 | async-start | bytes 524288 | tf_op jit(solution)/shard_map/all_to_all | solution.py:336
  7.8 2.4 %shard_map.102.by_column = bf16[4,128,2304]{2,1,0:T(8,128)(2,1)} custom-call(bf16[128,8192]{1,0:T(8,128)(2,1)} %bitcast.8), custom_call_target="tpu_custom_call" | custom-call | bytes 4718592 | tf_op jit(solution)/shard_map/pallas_call | solution.py:126
  10.3 3.1 %all-to-all-done.1.c_ref = bf16[4,128,256]{2,1,0:T(8,128)(2,1)S(1)} async-done(((bf16[4,128,256]{2,1,0:T(8,128)(2,1)}), bf16[4,128,256]{2,1,0:T(8,128)(2,1)S(1)}, u32[]{:S(2)}, u32[]{:S(2)}) %all-to-all-start.1) | async-done | bytes 262176 | tf_op jit(solution)/shard_map/all_to_all | solution.py:336
  13.3 0.0 copy-start.1
  13.3 0.7 copy-done.1
  14.0 1.7 shard_map.104
  15.7 0.0 copy-start.5
  15.7 4.2 %all-to-all-start.2 = ((bf16[4,128,2304]{2,1,0:T(8,128)(2,1)}), bf16[4,128,2304]{2,1,0:T(8,128)(2,1)S(1)}, u32[]{:S(2)}, u32[]{:S(2)}) async-start(bf16[4,128,2304]{2,1,0:T(8,128)(2,1)} %shard_map.104), calls=%async_computation.2 | async-start | bytes 4718592 | tf_op jit(solution)/shard_map/all_to_all | solution.py:338
  20.0 0.0 copy-done.5
  20.0 35.1 %all_gather.3.w_ref = bf16[16,2,64,128]{3,2,1,0:T(8,128)(2,1)} all-gather(bf16[1,2,64,128]{3,2,1,0:T(8,128)(2,1)S(1)} %copy-done.5), channel_id=1, replica_groups={{0,1,2,3,4,5,6,7,8,9,10,11,12,13,14,15},{16,17,18,19,20,21,22,23,24,25,..., dimensions={0}, use_global_device_ids=true | all-gather | bytes 557056 | tf_op jit(solution)/shard_map/all_gather | solution.py:339
  55.1 0.0 all-to-all-done.2.x_ref.c_ref
  55.1 11.5 %all-to-all-start = ((bf16[8,2,2,64,128]{4,3,2,1,0:T(8,128)(2,1)}), bf16[8,2,2,64,128]{4,3,2,1,0:T(8,128)(2,1)S(1)}, u32[]{:S(2)}, u32[]{:S(2)}) async-start(bf16[8,2,2,64,128]{4,3,2,1,0:T(8,128)(2,1)} %bitcast.1), calls=%async_computation | async-start | bytes 1048576 | tf_op jit(solution)/shard_map/all_to_all | solution.py:340
  66.5 1.8 shard_map.105.pre_ref
  68.3 7.6 %all-to-all-done.w_ref = bf16[8,2,2,64,128]{4,3,2,1,0:T(8,128)(2,1)S(1)} async-done(((bf16[8,2,2,64,128]{4,3,2,1,0:T(8,128)(2,1)}), bf16[8,2,2,64,128]{4,3,2,1,0:T(8,128)(2,1)S(1)}, u32[]{:S(2)}, u32[]{:S(2)}) %all-to-all-start) | async-done | bytes 524320 | tf_op jit(solution)/shard_map/all_to_all | solution.py:340
  75.9 0.7 shard_map.106
  76.6 21.1 %all_to_all.40.r_ref = bf16[32,16,896]{2,1,0:T(8,128)(2,1)S(1)} all-to-all(bf16[32,16,896]{2,1,0:T(8,128)(2,1)S(1)} %shard_map.106), channel_id=1, replica_groups={{0,16,32,48,64,80,96,112,128,144,160,176,192,208,224,240,256,272,288,30..., dimensions={0} | all-to-all | bytes 1835008 | tf_op jit(solution)/shard_map/all_to_all | solution.py:360
  97.7 0.2 shard_map.107
  97.8 24.4 %all_to_all.41.q_ref = bf16[32,16,1280]{2,1,0:T(8,128)(2,1)S(1)} all-to-all(bf16[32,16,1280]{2,1,0:T(8,128)(2,1)S(1)} %shard_map.107), channel_id=1, replica_groups={{0,16,32,48,64,80,96,112,128,144,160,176,192,208,224,240,256,272,288,30..., dimensions={0} | all-to-all | bytes 2621440 | tf_op jit(solution)/shard_map/all_to_all | solution.py:367
  122.3 2.8 %shard_map.108 = bf16[16,128,128]{2,1,0:T(8,128)(2,1)S(1)} custom-call(s32[1]{0:T(128)} %bitcast.index, bf16[32,16,1280]{2,1,0:T(8,128)(2,1)S(1)} %all_to_all.41.q_ref, bf16[8,2,2,64,128]{4,3,2,1,0:T(8,128)(2,1)S(1)} %all-to-all-done.w_ref, bf16[4,128,2304]{2,1,0:T(8,128)(2,1)S(1)} %all-to-all-done.2.x_ref.c_ref), custom_call_target="tpu_custom_call" | custom-call | flops 536870912 | bytes 4718596 | tf_op jit(solution)/shard_map/pallas_call | solution.py:42
  125.1 0.0 copy-start.2
  125.1 0.0 copy-start.3
  125.1 0.0 copy-start.4
  125.2 29.3 %all_to_all.42 = bf16[16,128,128]{2,1,0:T(8,128)(2,1)S(1)} all-to-all(bf16[16,128,128]{2,1,0:T(8,128)(2,1)S(1)} %shard_map.108), channel_id=1, replica_groups={{0,1,2,3,4,5,6,7,8,9,10,11,12,13,14,15},{16,17,18,19,20,21,22,23,24,25,..., dimensions={0} | all-to-all | bytes 1048576 | tf_op jit(solution)/shard_map/all_to_all | solution.py:383
  154.5 0.1 convert_reduce_fusion
  154.6 17.7 %all_to_all.43 = f32[32,8,128]{2,1,0:T(8,128)S(1)} all-to-all(f32[32,8,128]{2,1,0:T(8,128)S(1)} %broadcast_in_dim.4), channel_id=1, replica_groups={{0,16,32,48,64,80,96,112,128,144,160,176,192,208,224,240,256,272,288,30..., dimensions={0} | all-to-all | bytes 262144 | tf_op jit(solution)/shard_map/all_to_all | solution.py:388
  172.3 0.6 broadcast_in_dim.5
  173.0 6.0 %all-to-all-start.7 = ((f32[16,8,128]{2,1,0:T(8,128)}), f32[16,8,128]{2,1,0:T(8,128)S(1)}, u32[]{:S(2)}, u32[]{:S(2)}) async-start(f32[16,8,128]{2,1,0:T(8,128)} %broadcast_in_dim.5), calls=%async_computation.7 | async-start | bytes 131072 | tf_op jit(solution)/shard_map/all_to_all | solution.py:390
  179.0 12.9 %collective-permute-start = (f32[64,128]{1,0:T(8,128)S(1)}, f32[64,128]{1,0:T(8,128)S(1)}, u32[]{:S(2)}, u32[]{:S(2)}) collective-permute-start(f32[64,128]{1,0:T(8,128)S(1)} %get-tuple-element.9), channel_id=1, source_target_pairs={{0,0},{1,1},{2,64},{3,65},{4,128},{5,129},{6,192},{7,193},{8,256},... | collective-permute-start | bytes 98312 | tf_op jit(solution)/shard_map/ppermute | solution.py:386
  191.9 0.0 all-to-all-done.7
  191.9 0.6 reduce_sum.39
  193.2 0.0 collective-permute-done
  193.2 0.0 copy-done.2
  193.2 0.0 copy-done.3
  193.2 0.0 copy-done.4
  193.3 0.7 fusion.1
  (4 shorter events, 0.1 us)
Async XLA Ops:
  1.3 1.0 copy-start
  3.0 10.4 %all-to-all-start.1 = ((bf16[4,128,256]{2,1,0:T(8,128)(2,1)}), bf16[4,128,256]{2,1,0:T(8,128)(2,1)S(1)}, u32[]{:S(2)}, u32[]{:S(2)}) async-start(bf16[4,128,256]{2,1,0:T(8,128)(2,1)} %shard_map.103), calls=%async_computation.1 | async-start | bytes 524288 | tf_op jit(solution)/shard_map/all_to_all | solution.py:336
  13.3 0.7 copy-start.1
  15.7 4.2 %copy-start.5 = (bf16[1,2,64,128]{3,2,1,0:T(8,128)(2,1)S(1)}, bf16[1,2,64,128]{3,2,1,0:T(8,128)(2,1)}, u32[]{:S(2)}) copy-start(bf16[1,2,64,128]{3,2,1,0:T(8,128)(2,1)} %param.9) | copy-start | bytes 98308
  15.7 39.3 %all-to-all-start.2 = ((bf16[4,128,2304]{2,1,0:T(8,128)(2,1)}), bf16[4,128,2304]{2,1,0:T(8,128)(2,1)S(1)}, u32[]{:S(2)}, u32[]{:S(2)}) async-start(bf16[4,128,2304]{2,1,0:T(8,128)(2,1)} %shard_map.104), calls=%async_computation.2 | async-start | bytes 4718592 | tf_op jit(solution)/shard_map/all_to_all | solution.py:338
  55.1 20.8 %all-to-all-start = ((bf16[8,2,2,64,128]{4,3,2,1,0:T(8,128)(2,1)}), bf16[8,2,2,64,128]{4,3,2,1,0:T(8,128)(2,1)S(1)}, u32[]{:S(2)}, u32[]{:S(2)}) async-start(bf16[8,2,2,64,128]{4,3,2,1,0:T(8,128)(2,1)} %bitcast.1), calls=%async_computation | async-start | bytes 1048576 | tf_op jit(solution)/shard_map/all_to_all | solution.py:340
  125.1 68.1 %copy-start.2 = (f32[1,2,64,128]{3,2,1,0:T(8,128)S(1)}, f32[1,2,64,128]{3,2,1,0:T(8,128)}, u32[]{:S(2)}) copy-start(f32[1,2,64,128]{3,2,1,0:T(8,128)} %param.10) | copy-start | bytes 196612
  125.1 68.1 %copy-start.3 = (f32[1,2,64,128]{3,2,1,0:T(8,128)S(1)}, f32[1,2,64,128]{3,2,1,0:T(8,128)}, u32[]{:S(2)}) copy-start(f32[1,2,64,128]{3,2,1,0:T(8,128)} %param.12) | copy-start | bytes 196612
  125.1 68.1 %copy-start.4 = (f32[1,2,64,128]{3,2,1,0:T(8,128)S(1)}, f32[1,2,64,128]{3,2,1,0:T(8,128)}, u32[]{:S(2)}) copy-start(f32[1,2,64,128]{3,2,1,0:T(8,128)} %param.11) | copy-start | bytes 196612
  173.0 18.9 %all-to-all-start.7 = ((f32[16,8,128]{2,1,0:T(8,128)}), f32[16,8,128]{2,1,0:T(8,128)S(1)}, u32[]{:S(2)}, u32[]{:S(2)}) async-start(f32[16,8,128]{2,1,0:T(8,128)} %broadcast_in_dim.5), calls=%async_computation.7 | async-start | bytes 131072 | tf_op jit(solution)/shard_map/all_to_all | solution.py:390
  179.0 14.3 %collective-permute-start = (f32[64,128]{1,0:T(8,128)S(1)}, f32[64,128]{1,0:T(8,128)S(1)}, u32[]{:S(2)}, u32[]{:S(2)}) collective-permute-start(f32[64,128]{1,0:T(8,128)S(1)} %get-tuple-element.9), channel_id=1, source_target_pairs={{0,0},{1,1},{2,64},{3,65},{4,128},{5,129},{6,192},{7,193},{8,256},... | collective-permute-start | bytes 98312 | tf_op jit(solution)/shard_map/ppermute | solution.py:386

commit v7 on v5

--- a/solution.py
+++ b/solution.py
@@ -104,6 +104,8 @@
 
 def sort_kernel(lay, valid, x_ref, c_ref, out_ref, held, cots, sems):
     loads, stores = [], []
+    fetch = pltpu.make_async_copy(c_ref, cots, sems.at[3 * lay.y])
+    fetch.start()
     for a in range(lay.y):
         cols = pl.ds(a * lay.span, lay.span)
         loads.append(pltpu.make_async_copy(x_ref.at[:, cols], held.at[a], sems.at[a]))
@@ -113,7 +115,8 @@
             )
         )
         loads[a].start()
-    cot = c_ref[...]
+    fetch.wait()
+    cot = cots[...]
     live = lax.broadcasted_iota(jnp.int32, cot.shape, 0) < valid[0]
     cots[...] = jnp.where(live, cot, jnp.zeros_like(cot))
     for a in range(lay.y):
@@ -140,13 +143,13 @@
         in_specs=[
             pl.BlockSpec(memory_space=pltpu.SMEM),
             pl.BlockSpec(memory_space=pltpu.HBM),
-            pl.BlockSpec(memory_space=pltpu.VMEM),
+            pl.BlockSpec(memory_space=pltpu.HBM),
         ],
         out_specs=pl.BlockSpec(memory_space=pltpu.HBM),
         scratch_shapes=[
             pltpu.VMEM((lay.y, lay.rows, lay.span), BF16),
             pltpu.VMEM(cotangent.shape, BF16),
-            pltpu.SemaphoreType.DMA((3 * lay.y,)),
+            pltpu.SemaphoreType.DMA((3 * lay.y + 1,)),
         ],
         compiler_params=pltpu.CompilerParams(vmem_limit_bytes=SORT_LIMIT),
         cost_estimate=pl.CostEstimate(
@@ -312,6 +315,23 @@
         out_ref[b, 0 : lay.rank, :] = grad_down[:, b * LANES : (b + 1) * LANES]
 
 
+def update_kernel(norm_limit, squares, grads, grad_up, master, moment1, moment2, *outs):
+    new_master, new_moment1, new_moment2, new_weights = outs
+    rank = grad_up.shape[0]
+    square_sum = jnp.sum(jnp.sum(squares[...], axis=0), keepdims=True)
+    clip_factor = jnp.minimum(1.0, norm_limit / jnp.sqrt(square_sum + NORM_EPS))
+    for side, grad in enumerate((grads[0:rank, :], grad_up[...])):
+        scaled = grad * clip_factor
+        first = BETA_ONE * moment1[0, side] + (1.0 - BETA_ONE) * scaled
+        second = BETA_TWO * moment2[0, side] + (1.0 - BETA_TWO) * scaled * scaled
+        old = master[0, side]
+        new = old - LEARN_RATE * (first / (jnp.sqrt(second) + ADAM_EPS) + DECAY_RATE * old)
+        new_moment1[0, side] = first
+        new_moment2[0, side] = second
+        new_master[0, side] = new
+        new_weights[0, side] = new.astype(BF16)
+
+
 def body(saved_inputs, cotangent, weights_bf16, master, moment1, moment2, valid_rows):
     pipe, dp = lax.axis_size("pipe"), lax.axis_size("dp")
     inputs, weights = saved_inputs[0], weights_bf16[0]
@@ -368,23 +388,22 @@
     grad_up = lax.ppermute(grads[lay.rank :], both, lay.gradient_home())
     squares = jnp.broadcast_to(squares, (lay.group, 8, LANES))
     squares = lax.all_to_all(squares, both, 0, 0, axis_index_groups=lay.plane)
-    squares = jnp.broadcast_to(jnp.sum(squares, axis=0), (lay.z, 8, LANES))
+    squares, grad_up = lax.optimization_barrier((jnp.sum(squares, axis=0), grad_up))
+    squares = jnp.broadcast_to(squares, (lay.z, 8, LANES))
     squares = lax.all_to_all(squares, "dp", 0, 0, axis_index_groups=lay.along_z)
-    square_sum = jnp.sum(squares)
     norm_limit = CLIP_RMS * math.sqrt(2.0 * pipe * lay.rank * lay.width)
-    clip_factor = jnp.minimum(1.0, norm_limit / jnp.sqrt(square_sum + NORM_EPS))
-    scaled = jnp.stack([grads[: lay.rank], grad_up]) * clip_factor
-    new_moment1 = BETA_ONE * moment1[0] + (1.0 - BETA_ONE) * scaled
-    new_moment2 = BETA_TWO * moment2[0] + (1.0 - BETA_TWO) * scaled * scaled
-    new_master = master[0] - LEARN_RATE * (
-        new_moment1 / (jnp.sqrt(new_moment2) + ADAM_EPS) + DECAY_RATE * master[0]
-    )
-    return (
-        new_master[None],
-        new_moment1[None],
-        new_moment2[None],
-        new_master.astype(BF16)[None],
-    )
+    state = jax.ShapeDtypeStruct(master.shape, F32)
+    return pl.pallas_call(
+        functools.partial(update_kernel, norm_limit),
+        out_shape=(state, state, state, jax.ShapeDtypeStruct(master.shape, BF16)),
+        in_specs=vmem_specs(6),
+        out_specs=tuple(vmem_specs(4)),
+        compiler_params=pltpu.CompilerParams(vmem_limit_bytes=8 * 1024 * 1024),
+        cost_estimate=pl.CostEstimate(
+            flops=0, bytes_accessed=30 * math.prod(master.shape), transcendentals=0
+        ),
+        interpret=INTERPRET,
+    )(squares, grads, grad_up, master, moment1, moment2)
 
 
 def solution(mesh):

time: 188 us -> 195 us (1.037)
  blocking collectives: 125 us -> 133 us
  starting transfers between devices: 32.9 us -> 35.5 us
    all_to_all x1, blocking collectives: 17.7 us -> 25.5 us  [body(): squares = lax.all_to_all(squares, 'dp', 0, 0, axis_index_groups=lay.along_z)]
    all_to_all x1, starting transfers between devices: 6 us -> 10.7 us  [body(): squares = lax.all_to_all(squares, both, 0, 0, axis_index_groups=lay.plane)]
    ppermute x1, starting transfers between devices: 5.1 us -> 2.99 us  [body(): grad_up = lax.ppermute(grads[lay.rank:], both, lay.gradient_home())]
where the time goes in v7:
time: 195 us; the launch traced here: 192 us
  blocking collectives  133 us (68%)
  starting transfers between devices  35.5 us (18%)
  waiting for transfers between devices  12.4 us (6%)
  Pallas kernels  8.92 us (5%)
    all_gather x1, blocking collectives, body(): maps = lax.all_gather(weights, 'dp', axis_index_groups=lay.along_z)  34.6 us
    all_to_all x1, blocking collectives, body(): grads = lax.all_to_all(grads, 'dp', 0, 0, axis_index_groups=lay.along_z)  29.3 us
    all_to_all x1, blocking collectives, body(): squares = lax.all_to_all(squares, 'dp', 0, 0, axis_index_groups=lay.along_z)  25.5 us
    all_to_all x1, blocking collectives, body(): sums = lax.all_to_all(sums, both, 0, 0, axis_index_groups=lay.plane)  24.4 us
    all_to_all x1, blocking collectives, body(): parts = lax.all_to_all(parts, both, 0, 0, axis_index_groups=lay.plane)  19.3 us
    ppermute x1, starting transfers between devices, body(): cots = lax.ppermute(cots, both, lay.cotangent_turn())  11.3 us
    all_to_all x1, starting transfers between devices, body(): squares = lax.all_to_all(squares, both, 0, 0, axis_index_groups=lay.plane)  10.7 us
    all_to_all x1, waiting for transfers between devices, body(): lax.all_to_all(maps.reshape(pipe, lay.per, 2, lay.rank, LANES), 'pipe', 0...  7.74 us
  transfers between devices with their start and end apart: 5, of which 2 were waited for; matrix products, arithmetic and copies ran while one was open for 0% of the time, Pallas kernels for 1%

profile of v7, /device:TPU:1, one launch (start us, length us, event | category | flops | bytes accessed | tf_op | source)
XLA Modules:
  0.0 192.2 jit_solution(13175084408132236369)
XLA Ops:
  1.3 2.6 %shard_map.102 = bf16[4,128,2304]{2,1,0:T(8,128)(2,1)} custom-call(s32[1]{0:T(128)S(6)} %copy.11.valid, bf16[128,8192]{1,0:T(8,128)(2,1)} %bitcast.5, bf16[128,1024]{1,0:T(8,128)(2,1)} %c_ref.1), custom_call_target="tpu_custom_call" | custom-call | bytes 4718592 | tf_op jit(solution)/shard_map/pallas_call | solution.py:140
  3.9 0.0 copy-start.3
  3.9 5.0 %all-to-all-start = ((bf16[4,128,2304]{2,1,0:T(8,128)(2,1)}), bf16[4,128,2304]{2,1,0:T(8,128)(2,1)S(1)}, u32[]{:S(2)}, u32[]{:S(2)}) async-start(bf16[4,128,2304]{2,1,0:T(8,128)(2,1)} %shard_map.102), calls=%async_computation | async-start | bytes 4718592 | tf_op jit(solution)/shard_map/all_to_all | solution.py:343
  9.0 0.0 copy-done.3
  9.0 34.6 %all_gather.3.w_ref = bf16[16,2,64,128]{3,2,1,0:T(8,128)(2,1)} all-gather(bf16[1,2,64,128]{3,2,1,0:T(8,128)(2,1)S(1)} %copy-done.3), channel_id=1, replica_groups={{0,1,2,3,4,5,6,7,8,9,10,11,12,13,14,15},{16,17,18,19,20,21,22,23,24,25,..., dimensions={0}, use_global_device_ids=true | all-gather | bytes 557056 | tf_op jit(solution)/shard_map/all_gather | solution.py:344
  43.6 0.0 all-to-all-done.x_ref
  43.6 11.3 %collective-permute-start = (bf16[4,128,256]{2,1,0:T(8,128)(2,1)S(1)}, bf16[4,128,256]{2,1,0:T(8,128)(2,1)S(1)}, u32[]{:S(2)}, u32[]{:S(2)}) collective-permute-start(bf16[4,128,256]{2,1,0:T(8,128)(2,1)S(1)} %slice.8), channel_id=1, source_target_pairs={{0,0},{1,1},{2,2},{3,3},{4,4},{5,5},{6,6},{7,7},{8,8},{9,9},{10,10... | collective-permute-start | bytes 786440 | tf_op jit(solution)/shard_map/ppermute | solution.py:346
  55.0 5.4 %all-to-all-start.1 = ((bf16[8,2,2,64,128]{4,3,2,1,0:T(8,128)(2,1)}), bf16[8,2,2,64,128]{4,3,2,1,0:T(8,128)(2,1)S(1)}, u32[]{:S(2)}, u32[]{:S(2)}) async-start(bf16[8,2,2,64,128]{4,3,2,1,0:T(8,128)(2,1)} %bitcast.2), calls=%async_computation.1 | async-start | bytes 1048576 | tf_op jit(solution)/shard_map/all_to_all | solution.py:347
  60.4 0.0 collective-permute-done.c_ref
  60.4 1.8 shard_map.103.pre_ref
  62.2 7.7 %all-to-all-done.1.w_ref = bf16[8,2,2,64,128]{4,3,2,1,0:T(8,128)(2,1)S(1)} async-done(((bf16[8,2,2,64,128]{4,3,2,1,0:T(8,128)(2,1)}), bf16[8,2,2,64,128]{4,3,2,1,0:T(8,128)(2,1)S(1)}, u32[]{:S(2)}, u32[]{:S(2)}) %all-to-all-start.1) | async-done | bytes 524320 | tf_op jit(solution)/shard_map/all_to_all | solution.py:347
  69.9 0.7 shard_map.104
  70.6 19.3 %all_to_all.35.r_ref = bf16[32,16,896]{2,1,0:T(8,128)(2,1)S(1)} all-to-all(bf16[32,16,896]{2,1,0:T(8,128)(2,1)S(1)} %shard_map.104), channel_id=1, replica_groups={{0,16,32,48,64,80,96,112,128,144,160,176,192,208,224,240,256,272,288,30..., dimensions={0} | all-to-all | bytes 1835008 | tf_op jit(solution)/shard_map/all_to_all | solution.py:362
  89.9 0.2 shard_map.105
  90.1 24.4 %all_to_all.36.q_ref = bf16[32,16,1280]{2,1,0:T(8,128)(2,1)S(1)} all-to-all(bf16[32,16,1280]{2,1,0:T(8,128)(2,1)S(1)} %shard_map.105), channel_id=1, replica_groups={{0,16,32,48,64,80,96,112,128,144,160,176,192,208,224,240,256,272,288,30..., dimensions={0} | all-to-all | bytes 2621440 | tf_op jit(solution)/shard_map/all_to_all | solution.py:369
  114.5 2.8 %shard_map.106 = bf16[16,128,128]{2,1,0:T(8,128)(2,1)S(1)} custom-call(s32[1]{0:T(128)} %bitcast.index, bf16[32,16,1280]{2,1,0:T(8,128)(2,1)S(1)} %all_to_all.36.q_ref, bf16[8,2,2,64,128]{4,3,2,1,0:T(8,128)(2,1)S(1)} %all-to-all-done.1.w_ref, bf16[4,128,256]{2,1,0:T(8,128)(2,1)S(1)} %collective-permute-done.c_ref, bf16[4,128,2304]{2,1,0:T(8,128)(2,1)S(1)} %all-to-all-done.x_ref), custom_call_target="tpu_custom_call" | custom-call | flops 536870912 | bytes 4980740 | tf_op jit(solution)/shard_map/pallas_call | solution.py:43
  117.4 0.0 copy-start
  117.4 0.0 copy-start.1
  117.4 0.0 copy-start.2
  117.4 29.3 %all_to_all.37 = bf16[16,128,128]{2,1,0:T(8,128)(2,1)S(1)} all-to-all(bf16[16,128,128]{2,1,0:T(8,128)(2,1)S(1)} %shard_map.106), channel_id=1, replica_groups={{0,1,2,3,4,5,6,7,8,9,10,11,12,13,14,15},{16,17,18,19,20,21,22,23,24,25,..., dimensions={0} | all-to-all | bytes 1048576 | tf_op jit(solution)/shard_map/all_to_all | solution.py:385
  146.7 0.1 convert_reduce_fusion.grads
  146.8 0.7 broadcast_in_dim.6
  147.4 10.7 %all-to-all-start.5 = ((f32[32,8,128]{2,1,0:T(8,128)}), f32[32,8,128]{2,1,0:T(8,128)S(1)}, u32[]{:S(2)}, u32[]{:S(2)}) async-start(f32[32,8,128]{2,1,0:T(8,128)} %broadcast_in_dim.6), calls=%async_computation.5 | async-start | bytes 262144 | tf_op jit(solution)/shard_map/all_to_all | solution.py:390
  158.2 3.0 %collective-permute-start.1 = (f32[64,128]{1,0:T(8,128)S(1)}, f32[64,128]{1,0:T(8,128)S(1)}, u32[]{:S(2)}, u32[]{:S(2)}) collective-permute-start(f32[64,128]{1,0:T(8,128)S(1)} %slice.9), channel_id=1, source_target_pairs={{0,0},{1,1},{2,64},{3,65},{4,128},{5,129},{6,192},{7,193},{8,256},... | collective-permute-start | bytes 98312 | tf_op jit(solution)/shard_map/ppermute | solution.py:388
  161.2 4.7 %all-to-all-done.5 = f32[32,8,128]{2,1,0:T(8,128)S(1)} async-done(((f32[32,8,128]{2,1,0:T(8,128)}), f32[32,8,128]{2,1,0:T(8,128)S(1)}, u32[]{:S(2)}, u32[]{:S(2)}) %all-to-all-start.5) | async-done | bytes 131104 | tf_op jit(solution)/shard_map/all_to_all | solution.py:390
  165.9 0.0 collective-permute-done.1.grad_up
  165.9 25.5 %all_to_all.38.squares = f32[16,8,128]{2,1,0:T(8,128)S(1)} all-to-all(f32[16,8,128]{2,1,0:T(8,128)S(1)} %broadcast_in_dim.7), channel_id=1, replica_groups={{0,1,2,3,4,5,6,7,8,9,10,11,12,13,14,15},{16,17,18,19,20,21,22,23,24,25,..., dimensions={0} | all-to-all | bytes 131072 | tf_op jit(solution)/shard_map/all_to_all | solution.py:393
  191.4 0.0 copy-done
  191.4 0.0 copy-done.1
  191.4 0.0 copy-done.2
  191.4 0.8 shard_map.107
  (5 shorter events, 0.1 us)
Async XLA Ops:
  3.9 5.0 %copy-start.3 = (bf16[1,2,64,128]{3,2,1,0:T(8,128)(2,1)S(1)}, bf16[1,2,64,128]{3,2,1,0:T(8,128)(2,1)}, u32[]{:S(2)}) copy-start(bf16[1,2,64,128]{3,2,1,0:T(8,128)(2,1)} %param.9) | copy-start | bytes 98308
  3.9 39.7 %all-to-all-start = ((bf16[4,128,2304]{2,1,0:T(8,128)(2,1)}), bf16[4,128,2304]{2,1,0:T(8,128)(2,1)S(1)}, u32[]{:S(2)}, u32[]{:S(2)}) async-start(bf16[4,128,2304]{2,1,0:T(8,128)(2,1)} %shard_map.102), calls=%async_computation | async-start | bytes 4718592 | tf_op jit(solution)/shard_map/all_to_all | solution.py:343
  43.6 16.8 %collective-permute-start = (bf16[4,128,256]{2,1,0:T(8,128)(2,1)S(1)}, bf16[4,128,256]{2,1,0:T(8,128)(2,1)S(1)}, u32[]{:S(2)}, u32[]{:S(2)}) collective-permute-start(bf16[4,128,256]{2,1,0:T(8,128)(2,1)S(1)} %slice.8), channel_id=1, source_target_pairs={{0,0},{1,1},{2,2},{3,3},{4,4},{5,5},{6,6},{7,7},{8,8},{9,9},{10,10... | collective-permute-start | bytes 786440 | tf_op jit(solution)/shard_map/ppermute | solution.py:346
  55.0 15.0 %all-to-all-start.1 = ((bf16[8,2,2,64,128]{4,3,2,1,0:T(8,128)(2,1)}), bf16[8,2,2,64,128]{4,3,2,1,0:T(8,128)(2,1)S(1)}, u32[]{:S(2)}, u32[]{:S(2)}) async-start(bf16[8,2,2,64,128]{4,3,2,1,0:T(8,128)(2,1)} %bitcast.2), calls=%async_computation.1 | async-start | bytes 1048576 | tf_op jit(solution)/shard_map/all_to_all | solution.py:347
  117.4 74.0 %copy-start = (f32[1,2,64,128]{3,2,1,0:T(8,128)S(1)}, f32[1,2,64,128]{3,2,1,0:T(8,128)}, u32[]{:S(2)}) copy-start(f32[1,2,64,128]{3,2,1,0:T(8,128)} %master.1) | copy-start | bytes 196612
  117.4 74.0 %copy-start.1 = (f32[1,2,64,128]{3,2,1,0:T(8,128)S(1)}, f32[1,2,64,128]{3,2,1,0:T(8,128)}, u32[]{:S(2)}) copy-start(f32[1,2,64,128]{3,2,1,0:T(8,128)} %moment1.1) | copy-start | bytes 196612
  117.4 74.0 %copy-start.2 = (f32[1,2,64,128]{3,2,1,0:T(8,128)S(1)}, f32[1,2,64,128]{3,2,1,0:T(8,128)}, u32[]{:S(2)}) copy-start(f32[1,2,64,128]{3,2,1,0:T(8,128)} %moment2.1) | copy-start | bytes 196612
  147.4 18.4 %all-to-all-start.5 = ((f32[32,8,128]{2,1,0:T(8,128)}), f32[32,8,128]{2,1,0:T(8,128)S(1)}, u32[]{:S(2)}, u32[]{:S(2)}) async-start(f32[32,8,128]{2,1,0:T(8,128)} %broadcast_in_dim.6), calls=%async_computation.5 | async-start | bytes 262144 | tf_op jit(solution)/shard_map/all_to_all | solution.py:390
  158.2 7.7 %collective-permute-start.1 = (f32[64,128]{1,0:T(8,128)S(1)}, f32[64,128]{1,0:T(8,128)S(1)}, u32[]{:S(2)}, u32[]{:S(2)}) collective-permute-start(f32[64,128]{1,0:T(8,128)S(1)} %slice.9), channel_id=1, source_target_pairs={{0,0},{1,1},{2,64},{3,65},{4,128},{5,129},{6,192},{7,193},{8,256},... | collective-permute-start | bytes 98312 | tf_op jit(solution)/shard_map/ppermute | solution.py:388

commit v8 on v7

--- a/solution.py
+++ b/solution.py
@@ -386,11 +386,11 @@
     grads = jnp.sum(grads.astype(F32), axis=0)
     squares = jnp.sum((grads * grads).reshape(-1, 8, LANES), axis=0)
     grad_up = lax.ppermute(grads[lay.rank :], both, lay.gradient_home())
+    squares = jnp.broadcast_to(squares, (lay.z, 8, LANES))
+    squares = lax.all_to_all(squares, "dp", 0, 0, axis_index_groups=lay.along_z)
+    squares, grad_up = lax.optimization_barrier((jnp.sum(squares, axis=0), grad_up))
     squares = jnp.broadcast_to(squares, (lay.group, 8, LANES))
     squares = lax.all_to_all(squares, both, 0, 0, axis_index_groups=lay.plane)
-    squares, grad_up = lax.optimization_barrier((jnp.sum(squares, axis=0), grad_up))
-    squares = jnp.broadcast_to(squares, (lay.z, 8, LANES))
-    squares = lax.all_to_all(squares, "dp", 0, 0, axis_index_groups=lay.along_z)
     norm_limit = CLIP_RMS * math.sqrt(2.0 * pipe * lay.rank * lay.width)
     state = jax.ShapeDtypeStruct(master.shape, F32)
     return pl.pallas_call(

time: 195 us -> 190 us (0.974)
  blocking collectives: 133 us -> 124 us
  starting transfers between devices: 35.5 us -> 39.7 us
    all_to_all x1, blocking collectives: 25.5 us -> 16.5 us  [body(): squares = lax.all_to_all(squares, both, 0, 0, axis_index_groups=lay.plane)]
    ppermute x1, starting transfers between devices: 2.99 us -> 5.17 us  [body(): grad_up = lax.ppermute(grads[lay.rank:], both, lay.gradient_home())]
    all_to_all x1, starting transfers between devices: 10.7 us -> 12.7 us  [body(): squares = lax.all_to_all(squares, 'dp', 0, 0, axis_index_groups=lay.along_z)]
where the time goes in v8:
time: 190 us; the launch traced here: 189 us
  blocking collectives  124 us (65%)
  starting transfers between devices  39.7 us (21%)
  waiting for transfers between devices  14.1 us (7%)
  Pallas kernels  8.94 us (5%)
    all_gather x1, blocking collectives, body(): maps = lax.all_gather(weights, 'dp', axis_index_groups=lay.along_z)  34.6 us
    all_to_all x1, blocking collectives, body(): grads = lax.all_to_all(grads, 'dp', 0, 0, axis_index_groups=lay.along_z)  29.3 us
    all_to_all x1, blocking collectives, body(): sums = lax.all_to_all(sums, both, 0, 0, axis_index_groups=lay.plane)  24.4 us
    all_to_all x1, blocking collectives, body(): parts = lax.all_to_all(parts, both, 0, 0, axis_index_groups=lay.plane)  19.3 us
    all_to_all x1, blocking collectives, body(): squares = lax.all_to_all(squares, both, 0, 0, axis_index_groups=lay.plane)  16.5 us
    all_to_all x1, starting transfers between devices, body(): squares = lax.all_to_all(squares, 'dp', 0, 0, axis_index_groups=lay.along_z)  12.7 us
    ppermute x1, starting transfers between devices, body(): cots = lax.ppermute(cots, both, lay.cotangent_turn())  11.3 us
    all_to_all x1, waiting for transfers between devices, body(): lax.all_to_all(maps.reshape(pipe, lay.per, 2, lay.rank, LANES), 'pipe', 0...  7.73 us
  transfers between devices with their start and end apart: 5, of which 2 were waited for; matrix products, arithmetic and copies ran while one was open for 0% of the time, Pallas kernels for 1%

profile of v8, /device:TPU:1, one launch (start us, length us, event | category | flops | bytes accessed | tf_op | source)
XLA Modules:
  0.0 189.1 jit_solution(17126328581755768710)
XLA Ops:
  1.3 2.6 %shard_map.102 = bf16[4,128,2304]{2,1,0:T(8,128)(2,1)} custom-call(s32[1]{0:T(128)S(6)} %copy.11.valid, bf16[128,8192]{1,0:T(8,128)(2,1)} %bitcast.5, bf16[128,1024]{1,0:T(8,128)(2,1)} %c_ref.1), custom_call_target="tpu_custom_call" | custom-call | bytes 4718592 | tf_op jit(solution)/shard_map/pallas_call | solution.py:140
  3.9 0.0 copy-start.3
  3.9 5.0 %all-to-all-start = ((bf16[4,128,2304]{2,1,0:T(8,128)(2,1)}), bf16[4,128,2304]{2,1,0:T(8,128)(2,1)S(1)}, u32[]{:S(2)}, u32[]{:S(2)}) async-start(bf16[4,128,2304]{2,1,0:T(8,128)(2,1)} %shard_map.102), calls=%async_computation | async-start | bytes 4718592 | tf_op jit(solution)/shard_map/all_to_all | solution.py:343
  9.0 0.0 copy-done.3
  9.0 34.6 %all_gather.3.w_ref = bf16[16,2,64,128]{3,2,1,0:T(8,128)(2,1)} all-gather(bf16[1,2,64,128]{3,2,1,0:T(8,128)(2,1)S(1)} %copy-done.3), channel_id=1, replica_groups={{0,1,2,3,4,5,6,7,8,9,10,11,12,13,14,15},{16,17,18,19,20,21,22,23,24,25,..., dimensions={0}, use_global_device_ids=true | all-gather | bytes 557056 | tf_op jit(solution)/shard_map/all_gather | solution.py:344
  43.6 0.0 all-to-all-done.x_ref
  43.6 11.3 %collective-permute-start = (bf16[4,128,256]{2,1,0:T(8,128)(2,1)S(1)}, bf16[4,128,256]{2,1,0:T(8,128)(2,1)S(1)}, u32[]{:S(2)}, u32[]{:S(2)}) collective-permute-start(bf16[4,128,256]{2,1,0:T(8,128)(2,1)S(1)} %slice.8), channel_id=1, source_target_pairs={{0,0},{1,1},{2,2},{3,3},{4,4},{5,5},{6,6},{7,7},{8,8},{9,9},{10,10... | collective-permute-start | bytes 786440 | tf_op jit(solution)/shard_map/ppermute | solution.py:346
  55.0 5.4 %all-to-all-start.1 = ((bf16[8,2,2,64,128]{4,3,2,1,0:T(8,128)(2,1)}), bf16[8,2,2,64,128]{4,3,2,1,0:T(8,128)(2,1)S(1)}, u32[]{:S(2)}, u32[]{:S(2)}) async-start(bf16[8,2,2,64,128]{4,3,2,1,0:T(8,128)(2,1)} %bitcast.2), calls=%async_computation.1 | async-start | bytes 1048576 | tf_op jit(solution)/shard_map/all_to_all | solution.py:347
  60.4 0.0 collective-permute-done.c_ref
  60.4 1.8 shard_map.103.pre_ref
  62.2 7.7 %all-to-all-done.1.w_ref = bf16[8,2,2,64,128]{4,3,2,1,0:T(8,128)(2,1)S(1)} async-done(((bf16[8,2,2,64,128]{4,3,2,1,0:T(8,128)(2,1)}), bf16[8,2,2,64,128]{4,3,2,1,0:T(8,128)(2,1)S(1)}, u32[]{:S(2)}, u32[]{:S(2)}) %all-to-all-start.1) | async-done | bytes 524320 | tf_op jit(solution)/shard_map/all_to_all | solution.py:347
  69.9 0.7 shard_map.104
  70.6 19.3 %all_to_all.35.r_ref = bf16[32,16,896]{2,1,0:T(8,128)(2,1)S(1)} all-to-all(bf16[32,16,896]{2,1,0:T(8,128)(2,1)S(1)} %shard_map.104), channel_id=1, replica_groups={{0,16,32,48,64,80,96,112,128,144,160,176,192,208,224,240,256,272,288,30..., dimensions={0} | all-to-all | bytes 1835008 | tf_op jit(solution)/shard_map/all_to_all | solution.py:362
  89.9 0.2 shard_map.105
  90.1 24.4 %all_to_all.36.q_ref = bf16[32,16,1280]{2,1,0:T(8,128)(2,1)S(1)} all-to-all(bf16[32,16,1280]{2,1,0:T(8,128)(2,1)S(1)} %shard_map.105), channel_id=1, replica_groups={{0,16,32,48,64,80,96,112,128,144,160,176,192,208,224,240,256,272,288,30..., dimensions={0} | all-to-all | bytes 2621440 | tf_op jit(solution)/shard_map/all_to_all | solution.py:369
  114.5 2.8 %shard_map.106 = bf16[16,128,128]{2,1,0:T(8,128)(2,1)S(1)} custom-call(s32[1]{0:T(128)} %bitcast.index, bf16[32,16,1280]{2,1,0:T(8,128)(2,1)S(1)} %all_to_all.36.q_ref, bf16[8,2,2,64,128]{4,3,2,1,0:T(8,128)(2,1)S(1)} %all-to-all-done.1.w_ref, bf16[4,128,256]{2,1,0:T(8,128)(2,1)S(1)} %collective-permute-done.c_ref, bf16[4,128,2304]{2,1,0:T(8,128)(2,1)S(1)} %all-to-all-done.x_ref), custom_call_target="tpu_custom_call" | custom-call | flops 536870912 | bytes 4980740 | tf_op jit(solution)/shard_map/pallas_call | solution.py:43
  117.4 0.0 copy-start
  117.4 0.0 copy-start.1
  117.4 0.0 copy-start.2
  117.4 29.3 %all_to_all.37 = bf16[16,128,128]{2,1,0:T(8,128)(2,1)S(1)} all-to-all(bf16[16,128,128]{2,1,0:T(8,128)(2,1)S(1)} %shard_map.106), channel_id=1, replica_groups={{0,1,2,3,4,5,6,7,8,9,10,11,12,13,14,15},{16,17,18,19,20,21,22,23,24,25,..., dimensions={0} | all-to-all | bytes 1048576 | tf_op jit(solution)/shard_map/all_to_all | solution.py:385
  146.7 0.1 convert_reduce_fusion.grads
  146.8 0.6 broadcast_in_dim.6
  147.4 12.7 %all-to-all-start.5 = ((f32[16,8,128]{2,1,0:T(8,128)}), f32[16,8,128]{2,1,0:T(8,128)S(1)}, u32[]{:S(2)}, u32[]{:S(2)}) async-start(f32[16,8,128]{2,1,0:T(8,128)} %broadcast_in_dim.6), calls=%async_computation.5 | async-start | bytes 131072 | tf_op jit(solution)/shard_map/all_to_all | solution.py:390
  160.1 5.2 %collective-permute-start.1 = (f32[64,128]{1,0:T(8,128)S(1)}, f32[64,128]{1,0:T(8,128)S(1)}, u32[]{:S(2)}, u32[]{:S(2)}) collective-permute-start(f32[64,128]{1,0:T(8,128)S(1)} %slice.9), channel_id=1, source_target_pairs={{0,0},{1,1},{2,64},{3,65},{4,128},{5,129},{6,192},{7,193},{8,256},... | collective-permute-start | bytes 98312 | tf_op jit(solution)/shard_map/ppermute | solution.py:388
  165.3 6.4 %all-to-all-done.5 = f32[16,8,128]{2,1,0:T(8,128)S(1)} async-done(((f32[16,8,128]{2,1,0:T(8,128)}), f32[16,8,128]{2,1,0:T(8,128)S(1)}, u32[]{:S(2)}, u32[]{:S(2)}) %all-to-all-start.5) | async-done | bytes 65568 | tf_op jit(solution)/shard_map/all_to_all | solution.py:390
  171.7 0.0 collective-permute-done.1.grad_up
  171.7 16.5 %all_to_all.38.squares = f32[32,8,128]{2,1,0:T(8,128)S(1)} all-to-all(f32[32,8,128]{2,1,0:T(8,128)S(1)} %broadcast_in_dim.7), channel_id=1, replica_groups={{0,16,32,48,64,80,96,112,128,144,160,176,192,208,224,240,256,272,288,30..., dimensions={0} | all-to-all | bytes 262144 | tf_op jit(solution)/shard_map/all_to_all | solution.py:393
  188.2 0.0 copy-done
  188.2 0.0 copy-done.1
  188.2 0.0 copy-done.2
  188.2 0.9 shard_map.107
  (5 shorter events, 0.1 us)
Async XLA Ops:
  3.9 5.0 %copy-start.3 = (bf16[1,2,64,128]{3,2,1,0:T(8,128)(2,1)S(1)}, bf16[1,2,64,128]{3,2,1,0:T(8,128)(2,1)}, u32[]{:S(2)}) copy-start(bf16[1,2,64,128]{3,2,1,0:T(8,128)(2,1)} %param.9) | copy-start | bytes 98308
  3.9 39.7 %all-to-all-start = ((bf16[4,128,2304]{2,1,0:T(8,128)(2,1)}), bf16[4,128,2304]{2,1,0:T(8,128)(2,1)S(1)}, u32[]{:S(2)}, u32[]{:S(2)}) async-start(bf16[4,128,2304]{2,1,0:T(8,128)(2,1)} %shard_map.102), calls=%async_computation | async-start | bytes 4718592 | tf_op jit(solution)/shard_map/all_to_all | solution.py:343
  43.6 16.8 %collective-permute-start = (bf16[4,128,256]{2,1,0:T(8,128)(2,1)S(1)}, bf16[4,128,256]{2,1,0:T(8,128)(2,1)S(1)}, u32[]{:S(2)}, u32[]{:S(2)}) collective-permute-start(bf16[4,128,256]{2,1,0:T(8,128)(2,1)S(1)} %slice.8), channel_id=1, source_target_pairs={{0,0},{1,1},{2,2},{3,3},{4,4},{5,5},{6,6},{7,7},{8,8},{9,9},{10,10... | collective-permute-start | bytes 786440 | tf_op jit(solution)/shard_map/ppermute | solution.py:346
  55.0 15.0 %all-to-all-start.1 = ((bf16[8,2,2,64,128]{4,3,2,1,0:T(8,128)(2,1)}), bf16[8,2,2,64,128]{4,3,2,1,0:T(8,128)(2,1)S(1)}, u32[]{:S(2)}, u32[]{:S(2)}) async-start(bf16[8,2,2,64,128]{4,3,2,1,0:T(8,128)(2,1)} %bitcast.2), calls=%async_computation.1 | async-start | bytes 1048576 | tf_op jit(solution)/shard_map/all_to_all | solution.py:347
  117.4 70.8 %copy-start = (f32[1,2,64,128]{3,2,1,0:T(8,128)S(1)}, f32[1,2,64,128]{3,2,1,0:T(8,128)}, u32[]{:S(2)}) copy-start(f32[1,2,64,128]{3,2,1,0:T(8,128)} %master.1) | copy-start | bytes 196612
  117.4 70.8 %copy-start.1 = (f32[1,2,64,128]{3,2,1,0:T(8,128)S(1)}, f32[1,2,64,128]{3,2,1,0:T(8,128)}, u32[]{:S(2)}) copy-start(f32[1,2,64,128]{3,2,1,0:T(8,128)} %moment1.1) | copy-start | bytes 196612
  117.4 70.8 %copy-start.2 = (f32[1,2,64,128]{3,2,1,0:T(8,128)S(1)}, f32[1,2,64,128]{3,2,1,0:T(8,128)}, u32[]{:S(2)}) copy-start(f32[1,2,64,128]{3,2,1,0:T(8,128)} %moment2.1) | copy-start | bytes 196612
  147.4 24.3 %all-to-all-start.5 = ((f32[16,8,128]{2,1,0:T(8,128)}), f32[16,8,128]{2,1,0:T(8,128)S(1)}, u32[]{:S(2)}, u32[]{:S(2)}) async-start(f32[16,8,128]{2,1,0:T(8,128)} %broadcast_in_dim.6), calls=%async_computation.5 | async-start | bytes 131072 | tf_op jit(solution)/shard_map/all_to_all | solution.py:390
  160.1 11.6 %collective-permute-start.1 = (f32[64,128]{1,0:T(8,128)S(1)}, f32[64,128]{1,0:T(8,128)S(1)}, u32[]{:S(2)}, u32[]{:S(2)}) collective-permute-start(f32[64,128]{1,0:T(8,128)S(1)} %slice.9), channel_id=1, source_target_pairs={{0,0},{1,1},{2,64},{3,65},{4,128},{5,129},{6,192},{7,193},{8,256},... | collective-permute-start | bytes 98312 | tf_op jit(solution)/shard_map/ppermute | solution.py:388

commit v9 on v7

--- a/solution.py
+++ b/solution.py
@@ -20,7 +20,9 @@
 Y_SIZE = 4
 VMEM_LIMIT = 48 * 1024 * 1024
 SORT_LIMIT = 63 * 1024 * 1024
+SMALL_LIMIT = 8 * 1024 * 1024
 PRE_WEIGHT = 12
+JOIN_WEIGHT = 1 << 34
 INTERPRET = False
 BF16 = jnp.bfloat16
 F32 = jnp.float32
@@ -315,13 +317,17 @@
         out_ref[b, 0 : lay.rank, :] = grad_down[:, b * LANES : (b + 1) * LANES]
 
 
-def update_kernel(norm_limit, squares, grads, grad_up, master, moment1, moment2, *outs):
+def join_kernel(grads, grad_up, out_ref):
+    out_ref[0] = grads[0 : grad_up.shape[0], :]
+    out_ref[1] = grad_up[...]
+
+
+def update_kernel(norm_limit, squares, grads, master, moment1, moment2, *outs):
     new_master, new_moment1, new_moment2, new_weights = outs
-    rank = grad_up.shape[0]
     square_sum = jnp.sum(jnp.sum(squares[...], axis=0), keepdims=True)
     clip_factor = jnp.minimum(1.0, norm_limit / jnp.sqrt(square_sum + NORM_EPS))
-    for side, grad in enumerate((grads[0:rank, :], grad_up[...])):
-        scaled = grad * clip_factor
+    for side in range(2):
+        scaled = grads[side] * clip_factor
         first = BETA_ONE * moment1[0, side] + (1.0 - BETA_ONE) * scaled
         second = BETA_TWO * moment2[0, side] + (1.0 - BETA_TWO) * scaled * scaled
         old = master[0, side]
@@ -386,24 +392,32 @@
     grads = jnp.sum(grads.astype(F32), axis=0)
     squares = jnp.sum((grads * grads).reshape(-1, 8, LANES), axis=0)
     grad_up = lax.ppermute(grads[lay.rank :], both, lay.gradient_home())
+    joined = pl.pallas_call(
+        join_kernel,
+        out_shape=jax.ShapeDtypeStruct((2, lay.rank, LANES), F32),
+        in_specs=vmem_specs(2),
+        out_specs=vmem_specs(1)[0],
+        compiler_params=pltpu.CompilerParams(vmem_limit_bytes=SMALL_LIMIT),
+        cost_estimate=pl.CostEstimate(flops=JOIN_WEIGHT, bytes_accessed=0, transcendentals=0),
+        interpret=INTERPRET,
+    )(grads, grad_up)
     squares = jnp.broadcast_to(squares, (lay.group, 8, LANES))
     squares = lax.all_to_all(squares, both, 0, 0, axis_index_groups=lay.plane)
-    squares, grad_up = lax.optimization_barrier((jnp.sum(squares, axis=0), grad_up))
-    squares = jnp.broadcast_to(squares, (lay.z, 8, LANES))
+    squares = jnp.broadcast_to(jnp.sum(squares, axis=0), (lay.z, 8, LANES))
     squares = lax.all_to_all(squares, "dp", 0, 0, axis_index_groups=lay.along_z)
     norm_limit = CLIP_RMS * math.sqrt(2.0 * pipe * lay.rank * lay.width)
     state = jax.ShapeDtypeStruct(master.shape, F32)
     return pl.pallas_call(
         functools.partial(update_kernel, norm_limit),
         out_shape=(state, state, state, jax.ShapeDtypeStruct(master.shape, BF16)),
-        in_specs=vmem_specs(6),
+        in_specs=vmem_specs(5),
         out_specs=tuple(vmem_specs(4)),
-        compiler_params=pltpu.CompilerParams(vmem_limit_bytes=8 * 1024 * 1024),
+        compiler_params=pltpu.CompilerParams(vmem_limit_bytes=SMALL_LIMIT),
         cost_estimate=pl.CostEstimate(
             flops=0, bytes_accessed=30 * math.prod(master.shape), transcendentals=0
         ),
         interpret=INTERPRET,
-    )(squares, grads, grad_up, master, moment1, moment2)
+    )(squares, joined, master, moment1, moment2)
 
 
 def solution(mesh):

time: 195 us -> 189 us (0.969)
  blocking collectives: 133 us -> 108 us
  waiting for transfers between devices: 12.4 us -> 23.9 us
  starting transfers between devices: 35.5 us -> 44.1 us
    all_to_all x1 -> x0, blocking collectives: 25.5 us -> none  [body(): squares = lax.all_to_all(squares, 'dp', 0, 0, axis_index_groups=lay.along_z)]
    all_to_all x0 -> x1, waiting for transfers between devices: none -> 11.5 us  [body(): squares = lax.all_to_all(squares, 'dp', 0, 0, axis_index_groups=lay.along_z)]
    all_to_all x0 -> x1, starting transfers between devices: none -> 8.58 us  [body(): squares = lax.all_to_all(squares, 'dp', 0, 0, axis_index_groups=lay.along_z)]
  transfers between devices with their start and end apart: 5 -> 6, of which waited for: 2 -> 3; matrix products, arithmetic and copies ran while one was open for 0% -> 0% of each run, Pallas kernels for 1% -> 1%
where the time goes in v9:
time: 189 us; the launch traced here: 187 us
  blocking collectives  108 us (57%)
  starting transfers between devices  44.1 us (23%)
  waiting for transfers between devices  23.9 us (13%)
  Pallas kernels  8.88 us (5%)
    all_gather x1, blocking collectives, body(): maps = lax.all_gather(weights, 'dp', axis_index_groups=lay.along_z)  34.6 us
    all_to_all x1, blocking collectives, body(): grads = lax.all_to_all(grads, 'dp', 0, 0, axis_index_groups=lay.along_z)  29.2 us
    all_to_all x1, blocking collectives, body(): sums = lax.all_to_all(sums, both, 0, 0, axis_index_groups=lay.plane)  24.4 us
    all_to_all x1, blocking collectives, body(): parts = lax.all_to_all(parts, both, 0, 0, axis_index_groups=lay.plane)  19.3 us
    all_to_all x1, waiting for transfers between devices, body(): squares = lax.all_to_all(squares, 'dp', 0, 0, axis_index_groups=lay.along_z)  11.5 us
    ppermute x1, starting transfers between devices, body(): cots = lax.ppermute(cots, both, lay.cotangent_turn())  11.3 us
    all_to_all x1, starting transfers between devices, body(): squares = lax.all_to_all(squares, both, 0, 0, axis_index_groups=lay.plane)  10.7 us
    all_to_all x1, starting transfers between devices, body(): squares = lax.all_to_all(squares, 'dp', 0, 0, axis_index_groups=lay.along_z)  8.58 us
  transfers between devices with their start and end apart: 6, of which 3 were waited for; matrix products, arithmetic and copies ran while one was open for 0% of the time, Pallas kernels for 1%

profile of v9, /device:TPU:1, one launch (start us, length us, event | category | flops | bytes accessed | tf_op | source)
XLA Modules:
  0.0 187.3 jit_solution(16013590866947948166)
XLA Ops:
  1.3 2.6 %shard_map.102 = bf16[4,128,2304]{2,1,0:T(8,128)(2,1)} custom-call(s32[1]{0:T(128)S(6)} %copy.11.valid, bf16[128,8192]{1,0:T(8,128)(2,1)} %bitcast.5, bf16[128,1024]{1,0:T(8,128)(2,1)} %c_ref.1), custom_call_target="tpu_custom_call" | custom-call | bytes 4718592 | tf_op jit(solution)/shard_map/pallas_call | solution.py:142
  3.9 0.0 copy-start.3
  3.9 5.0 %all-to-all-start = ((bf16[4,128,2304]{2,1,0:T(8,128)(2,1)}), bf16[4,128,2304]{2,1,0:T(8,128)(2,1)S(1)}, u32[]{:S(2)}, u32[]{:S(2)}) async-start(bf16[4,128,2304]{2,1,0:T(8,128)(2,1)} %shard_map.102), calls=%async_computation | async-start | bytes 4718592 | tf_op jit(solution)/shard_map/all_to_all | solution.py:349
  8.9 0.0 copy-done.3
  8.9 34.6 %all_gather.3.w_ref = bf16[16,2,64,128]{3,2,1,0:T(8,128)(2,1)} all-gather(bf16[1,2,64,128]{3,2,1,0:T(8,128)(2,1)S(1)} %copy-done.3), channel_id=1, replica_groups={{0,1,2,3,4,5,6,7,8,9,10,11,12,13,14,15},{16,17,18,19,20,21,22,23,24,25,..., dimensions={0}, use_global_device_ids=true | all-gather | bytes 557056 | tf_op jit(solution)/shard_map/all_gather | solution.py:350
  43.6 0.0 all-to-all-done.x_ref
  43.6 11.3 %collective-permute-start = (bf16[4,128,256]{2,1,0:T(8,128)(2,1)S(1)}, bf16[4,128,256]{2,1,0:T(8,128)(2,1)S(1)}, u32[]{:S(2)}, u32[]{:S(2)}) collective-permute-start(bf16[4,128,256]{2,1,0:T(8,128)(2,1)S(1)} %slice.8), channel_id=1, source_target_pairs={{0,0},{1,1},{2,2},{3,3},{4,4},{5,5},{6,6},{7,7},{8,8},{9,9},{10,10... | collective-permute-start | bytes 786440 | tf_op jit(solution)/shard_map/ppermute | solution.py:352
  54.9 5.4 %all-to-all-start.1 = ((bf16[8,2,2,64,128]{4,3,2,1,0:T(8,128)(2,1)}), bf16[8,2,2,64,128]{4,3,2,1,0:T(8,128)(2,1)S(1)}, u32[]{:S(2)}, u32[]{:S(2)}) async-start(bf16[8,2,2,64,128]{4,3,2,1,0:T(8,128)(2,1)} %bitcast.2), calls=%async_computation.1 | async-start | bytes 1048576 | tf_op jit(solution)/shard_map/all_to_all | solution.py:353
  60.4 0.0 collective-permute-done.c_ref
  60.4 1.8 shard_map.103.pre_ref
  62.2 7.7 %all-to-all-done.1.w_ref = bf16[8,2,2,64,128]{4,3,2,1,0:T(8,128)(2,1)S(1)} async-done(((bf16[8,2,2,64,128]{4,3,2,1,0:T(8,128)(2,1)}), bf16[8,2,2,64,128]{4,3,2,1,0:T(8,128)(2,1)S(1)}, u32[]{:S(2)}, u32[]{:S(2)}) %all-to-all-start.1) | async-done | bytes 524320 | tf_op jit(solution)/shard_map/all_to_all | solution.py:353
  69.9 0.7 shard_map.104
  70.6 19.3 %all_to_all.35.r_ref = bf16[32,16,896]{2,1,0:T(8,128)(2,1)S(1)} all-to-all(bf16[32,16,896]{2,1,0:T(8,128)(2,1)S(1)} %shard_map.104), channel_id=1, replica_groups={{0,16,32,48,64,80,96,112,128,144,160,176,192,208,224,240,256,272,288,30..., dimensions={0} | all-to-all | bytes 1835008 | tf_op jit(solution)/shard_map/all_to_all | solution.py:368
  89.9 0.2 shard_map.105
  90.0 24.4 %all_to_all.36.q_ref = bf16[32,16,1280]{2,1,0:T(8,128)(2,1)S(1)} all-to-all(bf16[32,16,1280]{2,1,0:T(8,128)(2,1)S(1)} %shard_map.105), channel_id=1, replica_groups={{0,16,32,48,64,80,96,112,128,144,160,176,192,208,224,240,256,272,288,30..., dimensions={0} | all-to-all | bytes 2621440 | tf_op jit(solution)/shard_map/all_to_all | solution.py:375
  114.5 2.8 %shard_map.106 = bf16[16,128,128]{2,1,0:T(8,128)(2,1)S(1)} custom-call(s32[1]{0:T(128)} %bitcast.index, bf16[32,16,1280]{2,1,0:T(8,128)(2,1)S(1)} %all_to_all.36.q_ref, bf16[8,2,2,64,128]{4,3,2,1,0:T(8,128)(2,1)S(1)} %all-to-all-done.1.w_ref, bf16[4,128,256]{2,1,0:T(8,128)(2,1)S(1)} %collective-permute-done.c_ref, bf16[4,128,2304]{2,1,0:T(8,128)(2,1)S(1)} %all-to-all-done.x_ref), custom_call_target="tpu_custom_call" | custom-call | flops 536870912 | bytes 4980740 | tf_op jit(solution)/shard_map/pallas_call | solution.py:45
  117.3 29.2 %all_to_all.37 = bf16[16,128,128]{2,1,0:T(8,128)(2,1)S(1)} all-to-all(bf16[16,128,128]{2,1,0:T(8,128)(2,1)S(1)} %shard_map.106), channel_id=1, replica_groups={{0,1,2,3,4,5,6,7,8,9,10,11,12,13,14,15},{16,17,18,19,20,21,22,23,24,25,..., dimensions={0} | all-to-all | bytes 1048576 | tf_op jit(solution)/shard_map/all_to_all | solution.py:391
  146.5 0.1 convert_reduce_fusion.grads
  146.6 0.7 broadcast_in_dim.6
  147.2 10.7 %all-to-all-start.5 = ((f32[32,8,128]{2,1,0:T(8,128)}), f32[32,8,128]{2,1,0:T(8,128)S(1)}, u32[]{:S(2)}, u32[]{:S(2)}) async-start(f32[32,8,128]{2,1,0:T(8,128)} %broadcast_in_dim.6), calls=%async_computation.5 | async-start | bytes 262144 | tf_op jit(solution)/shard_map/all_to_all | solution.py:405
  158.0 3.0 %collective-permute-start.1 = (f32[64,128]{1,0:T(8,128)S(1)}, f32[64,128]{1,0:T(8,128)S(1)}, u32[]{:S(2)}, u32[]{:S(2)}) collective-permute-start(f32[64,128]{1,0:T(8,128)S(1)} %slice.9), channel_id=1, source_target_pairs={{0,0},{1,1},{2,64},{3,65},{4,128},{5,129},{6,192},{7,193},{8,256},... | collective-permute-start | bytes 98312 | tf_op jit(solution)/shard_map/ppermute | solution.py:394
  161.0 4.7 %all-to-all-done.5 = f32[32,8,128]{2,1,0:T(8,128)S(1)} async-done(((f32[32,8,128]{2,1,0:T(8,128)}), f32[32,8,128]{2,1,0:T(8,128)S(1)}, u32[]{:S(2)}, u32[]{:S(2)}) %all-to-all-start.5) | async-done | bytes 131104 | tf_op jit(solution)/shard_map/all_to_all | solution.py:405
  165.7 0.6 broadcast_in_dim.7
  166.3 8.6 %all-to-all-start.6 = ((f32[16,8,128]{2,1,0:T(8,128)}), f32[16,8,128]{2,1,0:T(8,128)S(1)}, u32[]{:S(2)}, u32[]{:S(2)}) async-start(f32[16,8,128]{2,1,0:T(8,128)} %broadcast_in_dim.7), calls=%async_computation.6 | async-start | bytes 131072 | tf_op jit(solution)/shard_map/all_to_all | solution.py:407
  174.9 0.0 copy-start
  174.9 0.0 copy-start.1
  174.9 0.0 copy-start.2
  174.9 0.0 collective-permute-done.1.grad_up
  175.0 11.5 %all-to-all-done.6.squares = f32[16,8,128]{2,1,0:T(8,128)S(1)} async-done(((f32[16,8,128]{2,1,0:T(8,128)}), f32[16,8,128]{2,1,0:T(8,128)S(1)}, u32[]{:S(2)}, u32[]{:S(2)}) %all-to-all-start.6) | async-done | bytes 65568 | tf_op jit(solution)/shard_map/all_to_all | solution.py:407
  186.5 0.0 copy-done
  186.5 0.0 copy-done.1
  186.5 0.0 copy-done.2
  186.5 0.8 shard_map.108
  (5 shorter events, 0.1 us)
Async XLA Ops:
  3.9 5.0 %copy-start.3 = (bf16[1,2,64,128]{3,2,1,0:T(8,128)(2,1)S(1)}, bf16[1,2,64,128]{3,2,1,0:T(8,128)(2,1)}, u32[]{:S(2)}) copy-start(bf16[1,2,64,128]{3,2,1,0:T(8,128)(2,1)} %param.9) | copy-start | bytes 98308
  3.9 39.7 %all-to-all-start = ((bf16[4,128,2304]{2,1,0:T(8,128)(2,1)}), bf16[4,128,2304]{2,1,0:T(8,128)(2,1)S(1)}, u32[]{:S(2)}, u32[]{:S(2)}) async-start(bf16[4,128,2304]{2,1,0:T(8,128)(2,1)} %shard_map.102), calls=%async_computation | async-start | bytes 4718592 | tf_op jit(solution)/shard_map/all_to_all | solution.py:349
  43.6 16.8 %collective-permute-start = (bf16[4,128,256]{2,1,0:T(8,128)(2,1)S(1)}, bf16[4,128,256]{2,1,0:T(8,128)(2,1)S(1)}, u32[]{:S(2)}, u32[]{:S(2)}) collective-permute-start(bf16[4,128,256]{2,1,0:T(8,128)(2,1)S(1)} %slice.8), channel_id=1, source_target_pairs={{0,0},{1,1},{2,2},{3,3},{4,4},{5,5},{6,6},{7,7},{8,8},{9,9},{10,10... | collective-permute-start | bytes 786440 | tf_op jit(solution)/shard_map/ppermute | solution.py:352
  54.9 15.0 %all-to-all-start.1 = ((bf16[8,2,2,64,128]{4,3,2,1,0:T(8,128)(2,1)}), bf16[8,2,2,64,128]{4,3,2,1,0:T(8,128)(2,1)S(1)}, u32[]{:S(2)}, u32[]{:S(2)}) async-start(bf16[8,2,2,64,128]{4,3,2,1,0:T(8,128)(2,1)} %bitcast.2), calls=%async_computation.1 | async-start | bytes 1048576 | tf_op jit(solution)/shard_map/all_to_all | solution.py:353
  147.2 18.4 %all-to-all-start.5 = ((f32[32,8,128]{2,1,0:T(8,128)}), f32[32,8,128]{2,1,0:T(8,128)S(1)}, u32[]{:S(2)}, u32[]{:S(2)}) async-start(f32[32,8,128]{2,1,0:T(8,128)} %broadcast_in_dim.6), calls=%async_computation.5 | async-start | bytes 262144 | tf_op jit(solution)/shard_map/all_to_all | solution.py:405
  158.0 17.0 %collective-permute-start.1 = (f32[64,128]{1,0:T(8,128)S(1)}, f32[64,128]{1,0:T(8,128)S(1)}, u32[]{:S(2)}, u32[]{:S(2)}) collective-permute-start(f32[64,128]{1,0:T(8,128)S(1)} %slice.9), channel_id=1, source_target_pairs={{0,0},{1,1},{2,64},{3,65},{4,128},{5,129},{6,192},{7,193},{8,256},... | collective-permute-start | bytes 98312 | tf_op jit(solution)/shard_map/ppermute | solution.py:394
  166.3 20.2 %all-to-all-start.6 = ((f32[16,8,128]{2,1,0:T(8,128)}), f32[16,8,128]{2,1,0:T(8,128)S(1)}, u32[]{:S(2)}, u32[]{:S(2)}) async-start(f32[16,8,128]{2,1,0:T(8,128)} %broadcast_in_dim.7), calls=%async_computation.6 | async-start | bytes 131072 | tf_op jit(solution)/shard_map/all_to_all | solution.py:407
  174.9 11.6 %copy-start = (f32[1,2,64,128]{3,2,1,0:T(8,128)S(1)}, f32[1,2,64,128]{3,2,1,0:T(8,128)}, u32[]{:S(2)}) copy-start(f32[1,2,64,128]{3,2,1,0:T(8,128)} %master.1) | copy-start | bytes 196612
  174.9 11.6 %copy-start.1 = (f32[1,2,64,128]{3,2,1,0:T(8,128)S(1)}, f32[1,2,64,128]{3,2,1,0:T(8,128)}, u32[]{:S(2)}) copy-start(f32[1,2,64,128]{3,2,1,0:T(8,128)} %moment1.1) | copy-start | bytes 196612
  174.9 11.6 %copy-start.2 = (f32[1,2,64,128]{3,2,1,0:T(8,128)S(1)}, f32[1,2,64,128]{3,2,1,0:T(8,128)}, u32[]{:S(2)}) copy-start(f32[1,2,64,128]{3,2,1,0:T(8,128)} %moment2.1) | copy-start | bytes 196612

commit v10 on v9

--- a/solution.py
+++ b/solution.py
@@ -390,7 +390,7 @@
     )
     grads = lax.all_to_all(grads, "dp", 0, 0, axis_index_groups=lay.along_z)
     grads = jnp.sum(grads.astype(F32), axis=0)
-    squares = jnp.sum((grads * grads).reshape(-1, 8, LANES), axis=0)
+    squares = jnp.sum(grads * grads, axis=0, keepdims=True)
     grad_up = lax.ppermute(grads[lay.rank :], both, lay.gradient_home())
     joined = pl.pallas_call(
         join_kernel,
@@ -401,9 +401,9 @@
         cost_estimate=pl.CostEstimate(flops=JOIN_WEIGHT, bytes_accessed=0, transcendentals=0),
         interpret=INTERPRET,
     )(grads, grad_up)
-    squares = jnp.broadcast_to(squares, (lay.group, 8, LANES))
+    squares = jnp.broadcast_to(squares, (lay.group, 1, LANES))
     squares = lax.all_to_all(squares, both, 0, 0, axis_index_groups=lay.plane)
-    squares = jnp.broadcast_to(jnp.sum(squares, axis=0), (lay.z, 8, LANES))
+    squares = jnp.broadcast_to(jnp.sum(squares, axis=0), (lay.z, 1, LANES))
     squares = lax.all_to_all(squares, "dp", 0, 0, axis_index_groups=lay.along_z)
     norm_limit = CLIP_RMS * math.sqrt(2.0 * pipe * lay.rank * lay.width)
     state = jax.ShapeDtypeStruct(master.shape, F32)

time: 189 us -> 193 us (1.021)
  blocking collectives: 108 us -> 123 us
  starting transfers between devices: 44.1 us -> 38.4 us
  waiting for transfers between devices: 23.9 us -> 18.9 us
    all_to_all x0 -> x1, blocking collectives: none -> 15.9 us  [body(): squares = lax.all_to_all(squares, both, 0, 0, axis_index_groups=lay.plane)]
    all_to_all x1 -> x0, starting transfers between devices: 10.7 us -> none  [body(): squares = lax.all_to_all(squares, both, 0, 0, axis_index_groups=lay.plane)]
    ppermute x1, starting transfers between devices: 2.99 us -> 9.86 us  [body(): grad_up = lax.ppermute(grads[lay.rank:], both, lay.gradient_home())]
    all_to_all x1 -> x0, waiting for transfers between devices: 4.66 us -> none  [body(): squares = lax.all_to_all(squares, both, 0, 0, axis_index_groups=lay.plane)]
  transfers between devices with their start and end apart: 6 -> 5, of which waited for: 3 -> 2; matrix products, arithmetic and copies ran while one was open for 0% -> 0% of each run, Pallas kernels for 1% -> 1%
where the time goes in v10:
time: 193 us; the launch traced here: 192 us
  blocking collectives  123 us (64%)
  starting transfers between devices  38.4 us (20%)
  waiting for transfers between devices  18.9 us (10%)
  Pallas kernels  8.94 us (5%)
    all_gather x1, blocking collectives, body(): maps = lax.all_gather(weights, 'dp', axis_index_groups=lay.along_z)  34.6 us
    all_to_all x1, blocking collectives, body(): grads = lax.all_to_all(grads, 'dp', 0, 0, axis_index_groups=lay.along_z)  29.2 us
    all_to_all x1, blocking collectives, body(): sums = lax.all_to_all(sums, both, 0, 0, axis_index_groups=lay.plane)  24.4 us
    all_to_all x1, blocking collectives, body(): parts = lax.all_to_all(parts, both, 0, 0, axis_index_groups=lay.plane)  19.3 us
    all_to_all x1, blocking collectives, body(): squares = lax.all_to_all(squares, both, 0, 0, axis_index_groups=lay.plane)  15.9 us
    ppermute x1, starting transfers between devices, body(): cots = lax.ppermute(cots, both, lay.cotangent_turn())  11.3 us
    all_to_all x1, waiting for transfers between devices, body(): squares = lax.all_to_all(squares, 'dp', 0, 0, axis_index_groups=lay.along_z)  11.2 us
    ppermute x1, starting transfers between devices, body(): grad_up = lax.ppermute(grads[lay.rank:], both, lay.gradient_home())  9.86 us
  transfers between devices with their start and end apart: 5, of which 2 were waited for; matrix products, arithmetic and copies ran while one was open for 0% of the time, Pallas kernels for 1%

profile of v10, /device:TPU:1, one launch (start us, length us, event | category | flops | bytes accessed | tf_op | source)
XLA Modules:
  0.0 191.9 jit_solution(5224599135435350755)
XLA Ops:
  1.3 2.6 %shard_map.102 = bf16[4,128,2304]{2,1,0:T(8,128)(2,1)} custom-call(s32[1]{0:T(128)S(6)} %copy.12.valid, bf16[128,8192]{1,0:T(8,128)(2,1)} %bitcast.4, bf16[128,1024]{1,0:T(8,128)(2,1)} %c_ref.1), custom_call_target="tpu_custom_call" | custom-call | bytes 4718592 | tf_op jit(solution)/shard_map/pallas_call | solution.py:142
  3.9 0.0 copy-start.3
  3.9 5.0 %all-to-all-start = ((bf16[4,128,2304]{2,1,0:T(8,128)(2,1)}), bf16[4,128,2304]{2,1,0:T(8,128)(2,1)S(1)}, u32[]{:S(2)}, u32[]{:S(2)}) async-start(bf16[4,128,2304]{2,1,0:T(8,128)(2,1)} %shard_map.102), calls=%async_computation | async-start | bytes 4718592 | tf_op jit(solution)/shard_map/all_to_all | solution.py:349
  9.0 0.0 copy-done.3
  9.0 34.6 %all_gather.3.w_ref = bf16[16,2,64,128]{3,2,1,0:T(8,128)(2,1)} all-gather(bf16[1,2,64,128]{3,2,1,0:T(8,128)(2,1)S(1)} %copy-done.3), channel_id=1, replica_groups={{0,1,2,3,4,5,6,7,8,9,10,11,12,13,14,15},{16,17,18,19,20,21,22,23,24,25,..., dimensions={0}, use_global_device_ids=true | all-gather | bytes 557056 | tf_op jit(solution)/shard_map/all_gather | solution.py:350
  43.6 0.0 all-to-all-done.x_ref
  43.6 11.3 %collective-permute-start = (bf16[4,128,256]{2,1,0:T(8,128)(2,1)S(1)}, bf16[4,128,256]{2,1,0:T(8,128)(2,1)S(1)}, u32[]{:S(2)}, u32[]{:S(2)}) collective-permute-start(bf16[4,128,256]{2,1,0:T(8,128)(2,1)S(1)} %slice.8), channel_id=1, source_target_pairs={{0,0},{1,1},{2,2},{3,3},{4,4},{5,5},{6,6},{7,7},{8,8},{9,9},{10,10... | collective-permute-start | bytes 786440 | tf_op jit(solution)/shard_map/ppermute | solution.py:352
  55.0 5.4 %all-to-all-start.1 = ((bf16[8,2,2,64,128]{4,3,2,1,0:T(8,128)(2,1)}), bf16[8,2,2,64,128]{4,3,2,1,0:T(8,128)(2,1)S(1)}, u32[]{:S(2)}, u32[]{:S(2)}) async-start(bf16[8,2,2,64,128]{4,3,2,1,0:T(8,128)(2,1)} %bitcast.2), calls=%async_computation.1 | async-start | bytes 1048576 | tf_op jit(solution)/shard_map/all_to_all | solution.py:353
  60.4 0.0 collective-permute-done.c_ref
  60.4 1.8 shard_map.103.pre_ref
  62.2 7.7 %all-to-all-done.1.w_ref = bf16[8,2,2,64,128]{4,3,2,1,0:T(8,128)(2,1)S(1)} async-done(((bf16[8,2,2,64,128]{4,3,2,1,0:T(8,128)(2,1)}), bf16[8,2,2,64,128]{4,3,2,1,0:T(8,128)(2,1)S(1)}, u32[]{:S(2)}, u32[]{:S(2)}) %all-to-all-start.1) | async-done | bytes 524320 | tf_op jit(solution)/shard_map/all_to_all | solution.py:353
  69.9 0.7 shard_map.104
  70.6 19.3 %all_to_all.35.r_ref = bf16[32,16,896]{2,1,0:T(8,128)(2,1)S(1)} all-to-all(bf16[32,16,896]{2,1,0:T(8,128)(2,1)S(1)} %shard_map.104), channel_id=1, replica_groups={{0,16,32,48,64,80,96,112,128,144,160,176,192,208,224,240,256,272,288,30..., dimensions={0} | all-to-all | bytes 1835008 | tf_op jit(solution)/shard_map/all_to_all | solution.py:368
  89.9 0.2 shard_map.105
  90.1 24.4 %all_to_all.36.q_ref = bf16[32,16,1280]{2,1,0:T(8,128)(2,1)S(1)} all-to-all(bf16[32,16,1280]{2,1,0:T(8,128)(2,1)S(1)} %shard_map.105), channel_id=1, replica_groups={{0,16,32,48,64,80,96,112,128,144,160,176,192,208,224,240,256,272,288,30..., dimensions={0} | all-to-all | bytes 2621440 | tf_op jit(solution)/shard_map/all_to_all | solution.py:375
  114.5 2.8 %shard_map.106 = bf16[16,128,128]{2,1,0:T(8,128)(2,1)S(1)} custom-call(s32[1]{0:T(128)} %bitcast.index, bf16[32,16,1280]{2,1,0:T(8,128)(2,1)S(1)} %all_to_all.36.q_ref, bf16[8,2,2,64,128]{4,3,2,1,0:T(8,128)(2,1)S(1)} %all-to-all-done.1.w_ref, bf16[4,128,256]{2,1,0:T(8,128)(2,1)S(1)} %collective-permute-done.c_ref, bf16[4,128,2304]{2,1,0:T(8,128)(2,1)S(1)} %all-to-all-done.x_ref), custom_call_target="tpu_custom_call" | custom-call | flops 536870912 | bytes 4980740 | tf_op jit(solution)/shard_map/pallas_call | solution.py:45
  117.4 29.2 %all_to_all.37 = bf16[16,128,128]{2,1,0:T(8,128)(2,1)S(1)} all-to-all(bf16[16,128,128]{2,1,0:T(8,128)(2,1)S(1)} %shard_map.106), channel_id=1, replica_groups={{0,1,2,3,4,5,6,7,8,9,10,11,12,13,14,15},{16,17,18,19,20,21,22,23,24,25,..., dimensions={0} | all-to-all | bytes 1048576 | tf_op jit(solution)/shard_map/all_to_all | solution.py:391
  146.5 0.1 convert_reduce_fusion.grads
  146.6 9.9 %collective-permute-start.1 = (f32[64,128]{1,0:T(8,128)S(1)}, f32[64,128]{1,0:T(8,128)S(1)}, u32[]{:S(2)}, u32[]{:S(2)}) collective-permute-start(f32[64,128]{1,0:T(8,128)S(1)} %slice.9), channel_id=1, source_target_pairs={{0,0},{1,1},{2,64},{3,65},{4,128},{5,129},{6,192},{7,193},{8,256},... | collective-permute-start | bytes 98312 | tf_op jit(solution)/shard_map/ppermute | solution.py:394
  156.5 15.9 %all_to_all.38 = f32[32,1,128]{2,1,0:T(1,128)S(1)} all-to-all(f32[32,1,128]{2,1,0:T(1,128)S(1)} %broadcast_in_dim.7), channel_id=1, replica_groups={{0,16,32,48,64,80,96,112,128,144,160,176,192,208,224,240,256,272,288,30..., dimensions={0} | all-to-all | bytes 32768 | tf_op jit(solution)/shard_map/all_to_all | solution.py:405
  172.4 0.6 broadcast_in_dim.8
  173.0 6.8 %all-to-all-start.6 = ((f32[16,1,128]{2,1,0:T(1,128)}), f32[16,1,128]{2,1,0:T(1,128)S(1)}, u32[]{:S(2)}, u32[]{:S(2)}) async-start(f32[16,1,128]{2,1,0:T(1,128)} %broadcast_in_dim.8), calls=%async_computation.6 | async-start | bytes 16384 | tf_op jit(solution)/shard_map/all_to_all | solution.py:407
  179.8 0.0 copy-start
  179.8 0.0 copy-start.1
  179.8 0.0 copy-start.2
  179.8 0.0 collective-permute-done.1.grad_up
  179.9 11.2 %all-to-all-done.6.squares = f32[16,1,128]{2,1,0:T(1,128)S(1)} async-done(((f32[16,1,128]{2,1,0:T(1,128)}), f32[16,1,128]{2,1,0:T(1,128)S(1)}, u32[]{:S(2)}, u32[]{:S(2)}) %all-to-all-start.6) | async-done | bytes 8224 | tf_op jit(solution)/shard_map/all_to_all | solution.py:407
  191.0 0.0 copy-done
  191.0 0.0 copy-done.1
  191.0 0.0 copy-done.2
  191.0 0.8 shard_map.108
  (6 shorter events, 0.1 us)
Async XLA Ops:
  3.9 5.0 %copy-start.3 = (bf16[1,2,64,128]{3,2,1,0:T(8,128)(2,1)S(1)}, bf16[1,2,64,128]{3,2,1,0:T(8,128)(2,1)}, u32[]{:S(2)}) copy-start(bf16[1,2,64,128]{3,2,1,0:T(8,128)(2,1)} %param.9) | copy-start | bytes 98308
  3.9 39.7 %all-to-all-start = ((bf16[4,128,2304]{2,1,0:T(8,128)(2,1)}), bf16[4,128,2304]{2,1,0:T(8,128)(2,1)S(1)}, u32[]{:S(2)}, u32[]{:S(2)}) async-start(bf16[4,128,2304]{2,1,0:T(8,128)(2,1)} %shard_map.102), calls=%async_computation | async-start | bytes 4718592 | tf_op jit(solution)/shard_map/all_to_all | solution.py:349
  43.6 16.8 %collective-permute-start = (bf16[4,128,256]{2,1,0:T(8,128)(2,1)S(1)}, bf16[4,128,256]{2,1,0:T(8,128)(2,1)S(1)}, u32[]{:S(2)}, u32[]{:S(2)}) collective-permute-start(bf16[4,128,256]{2,1,0:T(8,128)(2,1)S(1)} %slice.8), channel_id=1, source_target_pairs={{0,0},{1,1},{2,2},{3,3},{4,4},{5,5},{6,6},{7,7},{8,8},{9,9},{10,10... | collective-permute-start | bytes 786440 | tf_op jit(solution)/shard_map/ppermute | solution.py:352
  55.0 15.0 %all-to-all-start.1 = ((bf16[8,2,2,64,128]{4,3,2,1,0:T(8,128)(2,1)}), bf16[8,2,2,64,128]{4,3,2,1,0:T(8,128)(2,1)S(1)}, u32[]{:S(2)}, u32[]{:S(2)}) async-start(bf16[8,2,2,64,128]{4,3,2,1,0:T(8,128)(2,1)} %bitcast.2), calls=%async_computation.1 | async-start | bytes 1048576 | tf_op jit(solution)/shard_map/all_to_all | solution.py:353
  146.6 33.2 %collective-permute-start.1 = (f32[64,128]{1,0:T(8,128)S(1)}, f32[64,128]{1,0:T(8,128)S(1)}, u32[]{:S(2)}, u32[]{:S(2)}) collective-permute-start(f32[64,128]{1,0:T(8,128)S(1)} %slice.9), channel_id=1, source_target_pairs={{0,0},{1,1},{2,64},{3,65},{4,128},{5,129},{6,192},{7,193},{8,256},... | collective-permute-start | bytes 98312 | tf_op jit(solution)/shard_map/ppermute | solution.py:394
  173.0 18.0 %all-to-all-start.6 = ((f32[16,1,128]{2,1,0:T(1,128)}), f32[16,1,128]{2,1,0:T(1,128)S(1)}, u32[]{:S(2)}, u32[]{:S(2)}) async-start(f32[16,1,128]{2,1,0:T(1,128)} %broadcast_in_dim.8), calls=%async_computation.6 | async-start | bytes 16384 | tf_op jit(solution)/shard_map/all_to_all | solution.py:407
  179.8 11.2 %copy-start = (f32[1,2,64,128]{3,2,1,0:T(8,128)S(1)}, f32[1,2,64,128]{3,2,1,0:T(8,128)}, u32[]{:S(2)}) copy-start(f32[1,2,64,128]{3,2,1,0:T(8,128)} %master.1) | copy-start | bytes 196612
  179.8 11.2 %copy-start.1 = (f32[1,2,64,128]{3,2,1,0:T(8,128)S(1)}, f32[1,2,64,128]{3,2,1,0:T(8,128)}, u32[]{:S(2)}) copy-start(f32[1,2,64,128]{3,2,1,0:T(8,128)} %moment1.1) | copy-start | bytes 196612
  179.8 11.2 %copy-start.2 = (f32[1,2,64,128]{3,2,1,0:T(8,128)S(1)}, f32[1,2,64,128]{3,2,1,0:T(8,128)}, u32[]{:S(2)}) copy-start(f32[1,2,64,128]{3,2,1,0:T(8,128)} %moment2.1) | copy-start | bytes 196612

commit v11 on v8

--- a/solution.py
+++ b/solution.py
@@ -20,7 +20,9 @@
 Y_SIZE = 4
 VMEM_LIMIT = 48 * 1024 * 1024
 SORT_LIMIT = 63 * 1024 * 1024
+SMALL_LIMIT = 8 * 1024 * 1024
 PRE_WEIGHT = 12
+SPREAD = 2
 INTERPRET = False
 BF16 = jnp.bfloat16
 F32 = jnp.float32
@@ -317,9 +319,9 @@
 
 def update_kernel(norm_limit, squares, grads, grad_up, master, moment1, moment2, *outs):
     new_master, new_moment1, new_moment2, new_weights = outs
+    square_sum = jnp.sum(jnp.sum(squares[:, 0:1, :], axis=0), keepdims=True)
+    clip_factor = jnp.minimum(1.0, norm_limit / jnp.sqrt(square_sum + NORM_EPS))
     rank = grad_up.shape[0]
-    square_sum = jnp.sum(jnp.sum(squares[...], axis=0), keepdims=True)
-    clip_factor = jnp.minimum(1.0, norm_limit / jnp.sqrt(square_sum + NORM_EPS))
     for side, grad in enumerate((grads[0:rank, :], grad_up[...])):
         scaled = grad * clip_factor
         first = BETA_ONE * moment1[0, side] + (1.0 - BETA_ONE) * scaled
@@ -384,13 +386,12 @@
     )
     grads = lax.all_to_all(grads, "dp", 0, 0, axis_index_groups=lay.along_z)
     grads = jnp.sum(grads.astype(F32), axis=0)
-    squares = jnp.sum((grads * grads).reshape(-1, 8, LANES), axis=0)
+    squares = jnp.sum(grads * grads, axis=0, keepdims=True)
+    squares = jnp.broadcast_to(squares, (lay.group, 1, LANES))
+    squares = lax.all_to_all(squares, both, 0, 0, axis_index_groups=lay.plane)
     grad_up = lax.ppermute(grads[lay.rank :], both, lay.gradient_home())
-    squares = jnp.broadcast_to(squares, (lay.z, 8, LANES))
+    squares = jnp.broadcast_to(jnp.sum(squares, axis=0), (lay.z, SPREAD, LANES))
     squares = lax.all_to_all(squares, "dp", 0, 0, axis_index_groups=lay.along_z)
-    squares, grad_up = lax.optimization_barrier((jnp.sum(squares, axis=0), grad_up))
-    squares = jnp.broadcast_to(squares, (lay.group, 8, LANES))
-    squares = lax.all_to_all(squares, both, 0, 0, axis_index_groups=lay.plane)
     norm_limit = CLIP_RMS * math.sqrt(2.0 * pipe * lay.rank * lay.width)
     state = jax.ShapeDtypeStruct(master.shape, F32)
     return pl.pallas_call(
@@ -398,7 +399,7 @@
         out_shape=(state, state, state, jax.ShapeDtypeStruct(master.shape, BF16)),
         in_specs=vmem_specs(6),
         out_specs=tuple(vmem_specs(4)),
-        compiler_params=pltpu.CompilerParams(vmem_limit_bytes=8 * 1024 * 1024),
+        compiler_params=pltpu.CompilerParams(vmem_limit_bytes=SMALL_LIMIT),
         cost_estimate=pl.CostEstimate(
             flops=0, bytes_accessed=30 * math.prod(master.shape), transcendentals=0
         ),

time: 190 us -> 188 us (0.989)
  the two profiles are of different devices: /device:TPU:1 before, /device:TPU:36 now
where the time goes in v11:
time: 188 us; the launch traced here: 187 us
  blocking collectives  131 us (70%)
  starting transfers between devices  34.2 us (18%)
  waiting for transfers between devices  10.2 us (5%)
  Pallas kernels  8.88 us (5%)
    all_gather x1, blocking collectives, body(): maps = lax.all_gather(weights, 'dp', axis_index_groups=lay.along_z)  38.6 us
    all_to_all x1, blocking collectives, body(): grads = lax.all_to_all(grads, 'dp', 0, 0, axis_index_groups=lay.along_z)  37.5 us
    all_to_all x1, blocking collectives, body(): sums = lax.all_to_all(sums, both, 0, 0, axis_index_groups=lay.plane)  23.6 us
    all_to_all x1, blocking collectives, body(): parts = lax.all_to_all(parts, both, 0, 0, axis_index_groups=lay.plane)  20.7 us
    ppermute x1, starting transfers between devices, body(): grad_up = lax.ppermute(grads[lay.rank:], both, lay.gradient_home())  12.9 us
    all_to_all x1, blocking collectives, body(): squares = lax.all_to_all(squares, both, 0, 0, axis_index_groups=lay.plane)  10.4 us
    all_to_all x1, starting transfers between devices, body(): squares = lax.all_to_all(squares, 'dp', 0, 0, axis_index_groups=lay.along_z)  6.67 us
    all_to_all x1, waiting for transfers between devices, body(): lax.all_to_all(maps.reshape(pipe, lay.per, 2, lay.rank, LANES), 'pipe', 0...  5.85 us
  transfers between devices with their start and end apart: 5, of which 2 were waited for; matrix products, arithmetic and copies ran while one was open for 0% of the time, Pallas kernels for 1%

profile of v11, /device:TPU:36, one launch (start us, length us, event | category | flops | bytes accessed | tf_op | source)
XLA Modules:
  0.0 187.0 jit_solution(15795081442534130831)
XLA Ops:
  1.3 2.6 %shard_map.102 = bf16[4,128,2304]{2,1,0:T(8,128)(2,1)} custom-call(s32[1]{0:T(128)S(6)} %copy.12.valid, bf16[128,8192]{1,0:T(8,128)(2,1)} %bitcast.4, bf16[128,1024]{1,0:T(8,128)(2,1)} %c_ref.1), custom_call_target="tpu_custom_call" | custom-call | bytes 4718592 | tf_op jit(solution)/shard_map/pallas_call | solution.py:142
  3.9 0.0 copy-start.3
  3.9 4.5 %all-to-all-start = ((bf16[4,128,2304]{2,1,0:T(8,128)(2,1)}), bf16[4,128,2304]{2,1,0:T(8,128)(2,1)S(1)}, u32[]{:S(2)}, u32[]{:S(2)}) async-start(bf16[4,128,2304]{2,1,0:T(8,128)(2,1)} %shard_map.102), calls=%async_computation | async-start | bytes 4718592 | tf_op jit(solution)/shard_map/all_to_all | solution.py:345
  8.4 0.0 copy-done.3
  8.4 38.6 %all_gather.3.w_ref = bf16[16,2,64,128]{3,2,1,0:T(8,128)(2,1)} all-gather(bf16[1,2,64,128]{3,2,1,0:T(8,128)(2,1)S(1)} %copy-done.3), channel_id=1, replica_groups={{0,1,2,3,4,5,6,7,8,9,10,11,12,13,14,15},{16,17,18,19,20,21,22,23,24,25,..., dimensions={0}, use_global_device_ids=true | all-gather | bytes 557056 | tf_op jit(solution)/shard_map/all_gather | solution.py:346
  47.0 0.0 all-to-all-done.x_ref
  47.0 0.7 slice.8
  47.7 5.3 %collective-permute-start = (bf16[4,128,256]{2,1,0:T(8,128)(2,1)}, bf16[4,128,256]{2,1,0:T(8,128)(2,1)S(1)}, u32[]{:S(2)}, u32[]{:S(2)}) collective-permute-start(bf16[4,128,256]{2,1,0:T(8,128)(2,1)} %slice.8), channel_id=1, source_target_pairs={{0,0},{1,1},{2,2},{3,3},{4,4},{5,5},{6,6},{7,7},{8,8},{9,9},{10,10... | collective-permute-start | bytes 786440 | tf_op jit(solution)/shard_map/ppermute | solution.py:348
  53.1 4.8 %all-to-all-start.1 = ((bf16[8,2,2,64,128]{4,3,2,1,0:T(8,128)(2,1)}), bf16[8,2,2,64,128]{4,3,2,1,0:T(8,128)(2,1)S(1)}, u32[]{:S(2)}, u32[]{:S(2)}) async-start(bf16[8,2,2,64,128]{4,3,2,1,0:T(8,128)(2,1)} %bitcast.2), calls=%async_computation.1 | async-start | bytes 1048576 | tf_op jit(solution)/shard_map/all_to_all | solution.py:349
  57.9 0.0 collective-permute-done.c_ref
  57.9 1.8 shard_map.103.pre_ref
  59.7 5.8 %all-to-all-done.1.w_ref = bf16[8,2,2,64,128]{4,3,2,1,0:T(8,128)(2,1)S(1)} async-done(((bf16[8,2,2,64,128]{4,3,2,1,0:T(8,128)(2,1)}), bf16[8,2,2,64,128]{4,3,2,1,0:T(8,128)(2,1)S(1)}, u32[]{:S(2)}, u32[]{:S(2)}) %all-to-all-start.1) | async-done | bytes 524320 | tf_op jit(solution)/shard_map/all_to_all | solution.py:349
  65.5 0.7 shard_map.104
  66.2 20.7 %all_to_all.35.r_ref = bf16[32,16,896]{2,1,0:T(8,128)(2,1)S(1)} all-to-all(bf16[32,16,896]{2,1,0:T(8,128)(2,1)S(1)} %shard_map.104), channel_id=1, replica_groups={{0,16,32,48,64,80,96,112,128,144,160,176,192,208,224,240,256,272,288,30..., dimensions={0} | all-to-all | bytes 1835008 | tf_op jit(solution)/shard_map/all_to_all | solution.py:364
  86.9 0.2 shard_map.105
  87.1 23.6 %all_to_all.36.q_ref = bf16[32,16,1280]{2,1,0:T(8,128)(2,1)S(1)} all-to-all(bf16[32,16,1280]{2,1,0:T(8,128)(2,1)S(1)} %shard_map.105), channel_id=1, replica_groups={{0,16,32,48,64,80,96,112,128,144,160,176,192,208,224,240,256,272,288,30..., dimensions={0} | all-to-all | bytes 2621440 | tf_op jit(solution)/shard_map/all_to_all | solution.py:371
  110.7 0.0 copy-start
  110.7 0.0 copy-start.1
  110.7 0.0 copy-start.2
  110.7 2.8 %shard_map.106 = bf16[16,128,128]{2,1,0:T(8,128)(2,1)S(1)} custom-call(s32[1]{0:T(128)} %bitcast.index, bf16[32,16,1280]{2,1,0:T(8,128)(2,1)S(1)} %all_to_all.36.q_ref, bf16[8,2,2,64,128]{4,3,2,1,0:T(8,128)(2,1)S(1)} %all-to-all-done.1.w_ref, bf16[4,128,256]{2,1,0:T(8,128)(2,1)S(1)} %collective-permute-done.c_ref, bf16[4,128,2304]{2,1,0:T(8,128)(2,1)S(1)} %all-to-all-done.x_ref), custom_call_target="tpu_custom_call" | custom-call | flops 536870912 | bytes 4980740 | tf_op jit(solution)/shard_map/pallas_call | solution.py:45
  113.5 37.5 %all_to_all.37 = bf16[16,128,128]{2,1,0:T(8,128)(2,1)S(1)} all-to-all(bf16[16,128,128]{2,1,0:T(8,128)(2,1)S(1)} %shard_map.106), channel_id=1, replica_groups={{0,1,2,3,4,5,6,7,8,9,10,11,12,13,14,15},{16,17,18,19,20,21,22,23,24,25,..., dimensions={0} | all-to-all | bytes 1048576 | tf_op jit(solution)/shard_map/all_to_all | solution.py:387
  151.1 0.1 convert_reduce_fusion.grads
  151.2 10.4 %all_to_all.38 = f32[32,1,128]{2,1,0:T(1,128)S(1)} all-to-all(f32[32,1,128]{2,1,0:T(1,128)S(1)} %broadcast_in_dim.4), channel_id=1, replica_groups={{0,16,32,48,64,80,96,112,128,144,160,176,192,208,224,240,256,272,288,30..., dimensions={0} | all-to-all | bytes 32768 | tf_op jit(solution)/shard_map/all_to_all | solution.py:391
  161.6 0.6 broadcast_in_dim.10
  162.2 6.7 %all-to-all-start.6 = ((f32[16,2,128]{2,1,0:T(2,128)}), f32[16,2,128]{2,1,0:T(2,128)S(1)}, u32[]{:S(2)}, u32[]{:S(2)}) async-start(f32[16,2,128]{2,1,0:T(2,128)} %broadcast_in_dim.10), calls=%async_computation.6 | async-start | bytes 32768 | tf_op jit(solution)/shard_map/all_to_all | solution.py:394
  168.9 12.9 %collective-permute-start.1 = (f32[64,128]{1,0:T(8,128)S(1)}, f32[64,128]{1,0:T(8,128)S(1)}, u32[]{:S(2)}, u32[]{:S(2)}) collective-permute-start(f32[64,128]{1,0:T(8,128)S(1)} %slice.9), channel_id=1, source_target_pairs={{0,0},{1,1},{2,64},{3,65},{4,128},{5,129},{6,192},{7,193},{8,256},... | collective-permute-start | bytes 98312 | tf_op jit(solution)/shard_map/ppermute | solution.py:392
  181.8 4.3 %collective-permute-done.1.grad_up = f32[64,128]{1,0:T(8,128)S(1)} collective-permute-done((f32[64,128]{1,0:T(8,128)S(1)}, f32[64,128]{1,0:T(8,128)S(1)}, u32[]{:S(2)}, u32[]{:S(2)}) %collective-permute-start.1) | collective-permute-done | bytes 32800 | tf_op jit(solution)/shard_map/ppermute | solution.py:392
  186.1 0.0 all-to-all-done.6.squares
  186.2 0.0 copy-done
  186.2 0.0 copy-done.1
  186.2 0.0 copy-done.2
  186.2 0.8 shard_map.107
  (4 shorter events, 0.1 us)
Async XLA Ops:
  3.9 4.5 %copy-start.3 = (bf16[1,2,64,128]{3,2,1,0:T(8,128)(2,1)S(1)}, bf16[1,2,64,128]{3,2,1,0:T(8,128)(2,1)}, u32[]{:S(2)}) copy-start(bf16[1,2,64,128]{3,2,1,0:T(8,128)(2,1)} %param.9) | copy-start | bytes 98308
  3.9 43.1 %all-to-all-start = ((bf16[4,128,2304]{2,1,0:T(8,128)(2,1)}), bf16[4,128,2304]{2,1,0:T(8,128)(2,1)S(1)}, u32[]{:S(2)}, u32[]{:S(2)}) async-start(bf16[4,128,2304]{2,1,0:T(8,128)(2,1)} %shard_map.102), calls=%async_computation | async-start | bytes 4718592 | tf_op jit(solution)/shard_map/all_to_all | solution.py:345
  47.7 10.2 %collective-permute-start = (bf16[4,128,256]{2,1,0:T(8,128)(2,1)}, bf16[4,128,256]{2,1,0:T(8,128)(2,1)S(1)}, u32[]{:S(2)}, u32[]{:S(2)}) collective-permute-start(bf16[4,128,256]{2,1,0:T(8,128)(2,1)} %slice.8), channel_id=1, source_target_pairs={{0,0},{1,1},{2,2},{3,3},{4,4},{5,5},{6,6},{7,7},{8,8},{9,9},{10,10... | collective-permute-start | bytes 786440 | tf_op jit(solution)/shard_map/ppermute | solution.py:348
  53.1 12.4 %all-to-all-start.1 = ((bf16[8,2,2,64,128]{4,3,2,1,0:T(8,128)(2,1)}), bf16[8,2,2,64,128]{4,3,2,1,0:T(8,128)(2,1)S(1)}, u32[]{:S(2)}, u32[]{:S(2)}) async-start(bf16[8,2,2,64,128]{4,3,2,1,0:T(8,128)(2,1)} %bitcast.2), calls=%async_computation.1 | async-start | bytes 1048576 | tf_op jit(solution)/shard_map/all_to_all | solution.py:349
  110.7 75.5 %copy-start = (f32[1,2,64,128]{3,2,1,0:T(8,128)S(1)}, f32[1,2,64,128]{3,2,1,0:T(8,128)}, u32[]{:S(2)}) copy-start(f32[1,2,64,128]{3,2,1,0:T(8,128)} %master.1) | copy-start | bytes 196612
  110.7 75.5 %copy-start.1 = (f32[1,2,64,128]{3,2,1,0:T(8,128)S(1)}, f32[1,2,64,128]{3,2,1,0:T(8,128)}, u32[]{:S(2)}) copy-start(f32[1,2,64,128]{3,2,1,0:T(8,128)} %moment1.1) | copy-start | bytes 196612
  110.7 75.5 %copy-start.2 = (f32[1,2,64,128]{3,2,1,0:T(8,128)S(1)}, f32[1,2,64,128]{3,2,1,0:T(8,128)}, u32[]{:S(2)}) copy-start(f32[1,2,64,128]{3,2,1,0:T(8,128)} %moment2.1) | copy-start | bytes 196612
  162.2 24.0 %all-to-all-start.6 = ((f32[16,2,128]{2,1,0:T(2,128)}), f32[16,2,128]{2,1,0:T(2,128)S(1)}, u32[]{:S(2)}, u32[]{:S(2)}) async-start(f32[16,2,128]{2,1,0:T(2,128)} %broadcast_in_dim.10), calls=%async_computation.6 | async-start | bytes 32768 | tf_op jit(solution)/shard_map/all_to_all | solution.py:394
  168.9 17.3 %collective-permute-start.1 = (f32[64,128]{1,0:T(8,128)S(1)}, f32[64,128]{1,0:T(8,128)S(1)}, u32[]{:S(2)}, u32[]{:S(2)}) collective-permute-start(f32[64,128]{1,0:T(8,128)S(1)} %slice.9), channel_id=1, source_target_pairs={{0,0},{1,1},{2,64},{3,65},{4,128},{5,129},{6,192},{7,193},{8,256},... | collective-permute-start | bytes 98312 | tf_op jit(solution)/shard_map/ppermute | solution.py:392

commit v12 on v11

--- a/solution.py
+++ b/solution.py
@@ -22,7 +22,7 @@
 SORT_LIMIT = 63 * 1024 * 1024
 SMALL_LIMIT = 8 * 1024 * 1024
 PRE_WEIGHT = 12
-SPREAD = 2
+SPREAD = 1
 INTERPRET = False
 BF16 = jnp.bfloat16
 F32 = jnp.float32

time: 188 us -> 189 us (level)
  the two profiles are of different devices: /device:TPU:36 before, /device:TPU:1 now
where the time goes in v12:
time: 189 us; the launch traced here: 188 us
  blocking collectives  108 us (57%)
  starting transfers between devices  44.8 us (24%)
  waiting for transfers between devices  22.9 us (12%)
  Pallas kernels  8.87 us (5%)
  local copies, waits for them, and re-layouts  1.96 us (1%)
    all_gather x1, blocking collectives, body(): maps = lax.all_gather(weights, 'dp', axis_index_groups=lay.along_z)  34.6 us
    all_to_all x1, blocking collectives, body(): grads = lax.all_to_all(grads, 'dp', 0, 0, axis_index_groups=lay.along_z)  29.3 us
    all_to_all x1, blocking collectives, body(): sums = lax.all_to_all(sums, both, 0, 0, axis_index_groups=lay.plane)  24.4 us
    all_to_all x1, blocking collectives, body(): parts = lax.all_to_all(parts, both, 0, 0, axis_index_groups=lay.plane)  19.4 us
    ppermute x1, starting transfers between devices, body(): cots = lax.ppermute(cots, both, lay.cotangent_turn())  11.3 us
    all_to_all x1, waiting for transfers between devices, body(): squares = lax.all_to_all(squares, 'dp', 0, 0, axis_index_groups=lay.along_z)  11.2 us
    all_to_all x1, starting transfers between devices, body(): squares = lax.all_to_all(squares, both, 0, 0, axis_index_groups=lay.plane)  10.7 us
    all_to_all x1, starting transfers between devices, body(): squares = lax.all_to_all(squares, 'dp', 0, 0, axis_index_groups=lay.along_z)  9.31 us
  transfers between devices with their start and end apart: 6, of which 3 were waited for; matrix products, arithmetic and copies ran while one was open for 0% of the time, Pallas kernels for 1%

profile of v12, /device:TPU:1, one launch (start us, length us, event | category | flops | bytes accessed | tf_op | source)
XLA Modules:
  0.0 187.8 jit_solution(4768324941441996931)
XLA Ops:
  1.3 2.6 %shard_map.102 = bf16[4,128,2304]{2,1,0:T(8,128)(2,1)} custom-call(s32[1]{0:T(128)S(6)} %copy.12.valid, bf16[128,8192]{1,0:T(8,128)(2,1)} %bitcast.4, bf16[128,1024]{1,0:T(8,128)(2,1)} %c_ref.1), custom_call_target="tpu_custom_call" | custom-call | bytes 4718592 | tf_op jit(solution)/shard_map/pallas_call | solution.py:142
  3.9 0.0 copy-start.3
  3.9 5.0 %all-to-all-start = ((bf16[4,128,2304]{2,1,0:T(8,128)(2,1)}), bf16[4,128,2304]{2,1,0:T(8,128)(2,1)S(1)}, u32[]{:S(2)}, u32[]{:S(2)}) async-start(bf16[4,128,2304]{2,1,0:T(8,128)(2,1)} %shard_map.102), calls=%async_computation | async-start | bytes 4718592 | tf_op jit(solution)/shard_map/all_to_all | solution.py:345
  8.9 0.0 copy-done.3
  8.9 34.6 %all_gather.3.w_ref = bf16[16,2,64,128]{3,2,1,0:T(8,128)(2,1)} all-gather(bf16[1,2,64,128]{3,2,1,0:T(8,128)(2,1)S(1)} %copy-done.3), channel_id=1, replica_groups={{0,1,2,3,4,5,6,7,8,9,10,11,12,13,14,15},{16,17,18,19,20,21,22,23,24,25,..., dimensions={0}, use_global_device_ids=true | all-gather | bytes 557056 | tf_op jit(solution)/shard_map/all_gather | solution.py:346
  43.6 0.0 all-to-all-done.x_ref
  43.6 0.7 slice.8
  44.3 11.3 %collective-permute-start = (bf16[4,128,256]{2,1,0:T(8,128)(2,1)}, bf16[4,128,256]{2,1,0:T(8,128)(2,1)S(1)}, u32[]{:S(2)}, u32[]{:S(2)}) collective-permute-start(bf16[4,128,256]{2,1,0:T(8,128)(2,1)} %slice.8), channel_id=1, source_target_pairs={{0,0},{1,1},{2,2},{3,3},{4,4},{5,5},{6,6},{7,7},{8,8},{9,9},{10,10... | collective-permute-start | bytes 786440 | tf_op jit(solution)/shard_map/ppermute | solution.py:348
  55.6 5.4 %all-to-all-start.1 = ((bf16[8,2,2,64,128]{4,3,2,1,0:T(8,128)(2,1)}), bf16[8,2,2,64,128]{4,3,2,1,0:T(8,128)(2,1)S(1)}, u32[]{:S(2)}, u32[]{:S(2)}) async-start(bf16[8,2,2,64,128]{4,3,2,1,0:T(8,128)(2,1)} %bitcast.2), calls=%async_computation.1 | async-start | bytes 1048576 | tf_op jit(solution)/shard_map/all_to_all | solution.py:349
  61.1 0.0 collective-permute-done.c_ref
  61.1 1.8 shard_map.103.pre_ref
  62.8 7.7 %all-to-all-done.1.w_ref = bf16[8,2,2,64,128]{4,3,2,1,0:T(8,128)(2,1)S(1)} async-done(((bf16[8,2,2,64,128]{4,3,2,1,0:T(8,128)(2,1)}), bf16[8,2,2,64,128]{4,3,2,1,0:T(8,128)(2,1)S(1)}, u32[]{:S(2)}, u32[]{:S(2)}) %all-to-all-start.1) | async-done | bytes 524320 | tf_op jit(solution)/shard_map/all_to_all | solution.py:349
  70.6 0.7 shard_map.104
  71.3 19.4 %all_to_all.35.r_ref = bf16[32,16,896]{2,1,0:T(8,128)(2,1)S(1)} all-to-all(bf16[32,16,896]{2,1,0:T(8,128)(2,1)S(1)} %shard_map.104), channel_id=1, replica_groups={{0,16,32,48,64,80,96,112,128,144,160,176,192,208,224,240,256,272,288,30..., dimensions={0} | all-to-all | bytes 1835008 | tf_op jit(solution)/shard_map/all_to_all | solution.py:364
  90.6 0.2 shard_map.105
  90.8 24.4 %all_to_all.36.q_ref = bf16[32,16,1280]{2,1,0:T(8,128)(2,1)S(1)} all-to-all(bf16[32,16,1280]{2,1,0:T(8,128)(2,1)S(1)} %shard_map.105), channel_id=1, replica_groups={{0,16,32,48,64,80,96,112,128,144,160,176,192,208,224,240,256,272,288,30..., dimensions={0} | all-to-all | bytes 2621440 | tf_op jit(solution)/shard_map/all_to_all | solution.py:371
  115.2 0.0 copy-start
  115.2 0.0 copy-start.1
  115.2 0.0 copy-start.2
  115.2 2.9 %shard_map.106 = bf16[16,128,128]{2,1,0:T(8,128)(2,1)S(1)} custom-call(s32[1]{0:T(128)} %bitcast.index, bf16[32,16,1280]{2,1,0:T(8,128)(2,1)S(1)} %all_to_all.36.q_ref, bf16[8,2,2,64,128]{4,3,2,1,0:T(8,128)(2,1)S(1)} %all-to-all-done.1.w_ref, bf16[4,128,256]{2,1,0:T(8,128)(2,1)S(1)} %collective-permute-done.c_ref, bf16[4,128,2304]{2,1,0:T(8,128)(2,1)S(1)} %all-to-all-done.x_ref), custom_call_target="tpu_custom_call" | custom-call | flops 536870912 | bytes 4980740 | tf_op jit(solution)/shard_map/pallas_call | solution.py:45
  118.1 29.3 %all_to_all.37 = bf16[16,128,128]{2,1,0:T(8,128)(2,1)S(1)} all-to-all(bf16[16,128,128]{2,1,0:T(8,128)(2,1)S(1)} %shard_map.106), channel_id=1, replica_groups={{0,1,2,3,4,5,6,7,8,9,10,11,12,13,14,15},{16,17,18,19,20,21,22,23,24,25,..., dimensions={0} | all-to-all | bytes 1048576 | tf_op jit(solution)/shard_map/all_to_all | solution.py:387
  147.4 0.1 convert_reduce_fusion.grads
  147.5 0.6 broadcast_in_dim.7
  148.1 10.7 %all-to-all-start.5 = ((f32[32,1,128]{2,1,0:T(1,128)}), f32[32,1,128]{2,1,0:T(1,128)S(1)}, u32[]{:S(2)}, u32[]{:S(2)}) async-start(f32[32,1,128]{2,1,0:T(1,128)} %broadcast_in_dim.7), calls=%async_computation.5 | async-start | bytes 32768 | tf_op jit(solution)/shard_map/all_to_all | solution.py:391
  158.8 3.0 %collective-permute-start.1 = (f32[64,128]{1,0:T(8,128)S(1)}, f32[64,128]{1,0:T(8,128)S(1)}, u32[]{:S(2)}, u32[]{:S(2)}) collective-permute-start(f32[64,128]{1,0:T(8,128)S(1)} %slice.9), channel_id=1, source_target_pairs={{0,0},{1,1},{2,64},{3,65},{4,128},{5,129},{6,192},{7,193},{8,256},... | collective-permute-start | bytes 98312 | tf_op jit(solution)/shard_map/ppermute | solution.py:392
  161.8 3.9 %all-to-all-done.5 = f32[32,1,128]{2,1,0:T(1,128)S(1)} async-done(((f32[32,1,128]{2,1,0:T(1,128)}), f32[32,1,128]{2,1,0:T(1,128)S(1)}, u32[]{:S(2)}, u32[]{:S(2)}) %all-to-all-start.5) | async-done | bytes 16416 | tf_op jit(solution)/shard_map/all_to_all | solution.py:391
  165.8 0.6 broadcast_in_dim.8
  166.4 9.3 %all-to-all-start.6 = ((f32[16,1,128]{2,1,0:T(1,128)}), f32[16,1,128]{2,1,0:T(1,128)S(1)}, u32[]{:S(2)}, u32[]{:S(2)}) async-start(f32[16,1,128]{2,1,0:T(1,128)} %broadcast_in_dim.8), calls=%async_computation.6 | async-start | bytes 16384 | tf_op jit(solution)/shard_map/all_to_all | solution.py:394
  175.7 0.0 collective-permute-done.1.grad_up
  175.7 11.2 %all-to-all-done.6.squares = f32[16,1,128]{2,1,0:T(1,128)S(1)} async-done(((f32[16,1,128]{2,1,0:T(1,128)}), f32[16,1,128]{2,1,0:T(1,128)S(1)}, u32[]{:S(2)}, u32[]{:S(2)}) %all-to-all-start.6) | async-done | bytes 8224 | tf_op jit(solution)/shard_map/all_to_all | solution.py:394
  186.9 0.0 copy-done
  186.9 0.0 copy-done.1
  186.9 0.0 copy-done.2
  186.9 0.8 shard_map.107
  (3 shorter events, 0.1 us)
Async XLA Ops:
  3.9 5.0 %copy-start.3 = (bf16[1,2,64,128]{3,2,1,0:T(8,128)(2,1)S(1)}, bf16[1,2,64,128]{3,2,1,0:T(8,128)(2,1)}, u32[]{:S(2)}) copy-start(bf16[1,2,64,128]{3,2,1,0:T(8,128)(2,1)} %param.9) | copy-start | bytes 98308
  3.9 39.7 %all-to-all-start = ((bf16[4,128,2304]{2,1,0:T(8,128)(2,1)}), bf16[4,128,2304]{2,1,0:T(8,128)(2,1)S(1)}, u32[]{:S(2)}, u32[]{:S(2)}) async-start(bf16[4,128,2304]{2,1,0:T(8,128)(2,1)} %shard_map.102), calls=%async_computation | async-start | bytes 4718592 | tf_op jit(solution)/shard_map/all_to_all | solution.py:345
  44.3 16.8 %collective-permute-start = (bf16[4,128,256]{2,1,0:T(8,128)(2,1)}, bf16[4,128,256]{2,1,0:T(8,128)(2,1)S(1)}, u32[]{:S(2)}, u32[]{:S(2)}) collective-permute-start(bf16[4,128,256]{2,1,0:T(8,128)(2,1)} %slice.8), channel_id=1, source_target_pairs={{0,0},{1,1},{2,2},{3,3},{4,4},{5,5},{6,6},{7,7},{8,8},{9,9},{10,10... | collective-permute-start | bytes 786440 | tf_op jit(solution)/shard_map/ppermute | solution.py:348
  55.6 15.0 %all-to-all-start.1 = ((bf16[8,2,2,64,128]{4,3,2,1,0:T(8,128)(2,1)}), bf16[8,2,2,64,128]{4,3,2,1,0:T(8,128)(2,1)S(1)}, u32[]{:S(2)}, u32[]{:S(2)}) async-start(bf16[8,2,2,64,128]{4,3,2,1,0:T(8,128)(2,1)} %bitcast.2), calls=%async_computation.1 | async-start | bytes 1048576 | tf_op jit(solution)/shard_map/all_to_all | solution.py:349
  115.2 71.7 %copy-start = (f32[1,2,64,128]{3,2,1,0:T(8,128)S(1)}, f32[1,2,64,128]{3,2,1,0:T(8,128)}, u32[]{:S(2)}) copy-start(f32[1,2,64,128]{3,2,1,0:T(8,128)} %master.1) | copy-start | bytes 196612
  115.2 71.7 %copy-start.1 = (f32[1,2,64,128]{3,2,1,0:T(8,128)S(1)}, f32[1,2,64,128]{3,2,1,0:T(8,128)}, u32[]{:S(2)}) copy-start(f32[1,2,64,128]{3,2,1,0:T(8,128)} %moment1.1) | copy-start | bytes 196612
  115.2 71.7 %copy-start.2 = (f32[1,2,64,128]{3,2,1,0:T(8,128)S(1)}, f32[1,2,64,128]{3,2,1,0:T(8,128)}, u32[]{:S(2)}) copy-start(f32[1,2,64,128]{3,2,1,0:T(8,128)} %moment2.1) | copy-start | bytes 196612
  148.1 17.7 %all-to-all-start.5 = ((f32[32,1,128]{2,1,0:T(1,128)}), f32[32,1,128]{2,1,0:T(1,128)S(1)}, u32[]{:S(2)}, u32[]{:S(2)}) async-start(f32[32,1,128]{2,1,0:T(1,128)} %broadcast_in_dim.7), calls=%async_computation.5 | async-start | bytes 32768 | tf_op jit(solution)/shard_map/all_to_all | solution.py:391
  158.8 16.9 %collective-permute-start.1 = (f32[64,128]{1,0:T(8,128)S(1)}, f32[64,128]{1,0:T(8,128)S(1)}, u32[]{:S(2)}, u32[]{:S(2)}) collective-permute-start(f32[64,128]{1,0:T(8,128)S(1)} %slice.9), channel_id=1, source_target_pairs={{0,0},{1,1},{2,64},{3,65},{4,128},{5,129},{6,192},{7,193},{8,256},... | collective-permute-start | bytes 98312 | tf_op jit(solution)/shard_map/ppermute | solution.py:392
  166.4 20.5 %all-to-all-start.6 = ((f32[16,1,128]{2,1,0:T(1,128)}), f32[16,1,128]{2,1,0:T(1,128)S(1)}, u32[]{:S(2)}, u32[]{:S(2)}) async-start(f32[16,1,128]{2,1,0:T(1,128)} %broadcast_in_dim.8), calls=%async_computation.6 | async-start | bytes 16384 | tf_op jit(solution)/shard_map/all_to_all | solution.py:394
